TPU v7x, 128 devices: a whole 4x4x4 slice. The times are simulated.
128 devices in a mesh: row: 32 (over z, y, core), col: 4 (over x).
Axes of the slice: x: 4, y: 4, z: 4, core: 2. Of those that a mesh axis runs over, the one named last changes fastest.
Arguments:
- tokens: bfloat16 [16384, 2048], P('row', 'col'), may hold values from -6 to 6
- cotangent: bfloat16 [16384, 2048], P('row', 'col'), may hold values from -6 to 6
- destination: int32 [16384], P('row'), may hold values from 0 to 16383, as said below
- segment_ids: int32 [16384], P('row'), may hold values from 0 to 7, as said below
- attn_gain: float32 [2048], replicated, may hold values from 0.5 to 1.5
- w_query: bfloat16 [2048, 2048], P('row', 'col'), may hold values from -0.125 to 0.125
- w_key: bfloat16 [2048, 256], P('row', 'col'), may hold values from -0.125 to 0.125
- w_value: bfloat16 [2048, 256], P('row', 'col'), may hold values from -0.125 to 0.125
- w_output: bfloat16 [2048, 2048], P('row', 'col'), may hold values from -0.5 to 0.5
- ffn_gain: float32 [2048], replicated, may hold values from 0.5 to 1.5
- w_gate: bfloat16 [2048, 5632], P('row', 'col'), may hold values from -0.125 to 0.125
- w_up: bfloat16 [2048, 5632], P('row', 'col'), may hold values from -0.125 to 0.125
- w_down: bfloat16 [2048, 5632], P('row', 'col'), may hold values from -0.078125 to 0.078125
Outputs:
- output: bfloat16 [16384, 2048], P('row', 'col')
- input_grad: bfloat16 [16384, 2048], P('row', 'col')
- attn_gain_grad: float32 [2048], P('row')
- w_query_grad: float32 [2048, 2048], P('row', 'col')
- w_key_grad: float32 [2048, 256], P('row', 'col')
- w_value_grad: float32 [2048, 256], P('row', 'col')
- w_output_grad: float32 [2048, 2048], P('row', 'col')
- ffn_gain_grad: float32 [2048], P('row')
- w_gate_grad: float32 [2048, 5632], P('row', 'col')
- w_up_grad: float32 [2048, 5632], P('row', 'col')
- w_down_grad: float32 [2048, 5632], P('row', 'col')
Inputs may be any that keep to these rules, and one draw needn't show every extreme that they name: `destination`: A permutation; the tokens of each aligned block of 512 arriving tokens go to exactly 16 places in each aligned block of 512 balanced places. `segment_ids`: within each aligned block of 512 places the ids start at 0 and rise by one where a new sequence begins, so a block holds at most 8 sequences; in every draw some block holds a single sequence of 512 tokens and some block holds 8 sequences.
All inputs are finite; a program needn't handle non-finite values.
Results may differ from a plain program's by a relative error of at most 0.028.
Values may be sent and summed in bfloat16 or wider, within the bound.
No kernel may reach another device: no remote copies, remote signals or barrier semaphores. Data moves between devices by JAX's collectives and lax.ppermute only.
A program may use at most 128 MiB of HBM per device.

v0:
```python
from functools import partial

import jax
import jax.numpy as jnp
from jax import lax
from jax.sharding import PartitionSpec as P

HEADS = 32
KV = 4
HD = 64


EPS = 1e-05
ROPE_BASE = 10000.0


def rope_tables(positions):
    half_width = HD // 2
    freqs = ROPE_BASE ** (-(jnp.arange(half_width, dtype=jnp.float32) * 2.0 / HD))
    angles = positions.astype(jnp.float32)[:, None] * freqs[None, :]
    return (jnp.cos(angles)[:, None, :], jnp.sin(angles)[:, None, :])


def rotate(values, cosine, sine):
    half_width = values.shape[-1] // 2
    first = values[..., :half_width]
    second = values[..., half_width:]
    return jnp.concatenate(
        [first * cosine - second * sine, second * cosine + first * sine], axis=-1
    )


def rotate_back(grads, cosine, sine):
    half_width = grads.shape[-1] // 2
    first = grads[..., :half_width]
    second = grads[..., half_width:]
    return jnp.concatenate(
        [first * cosine + second * sine, second * cosine - first * sine], axis=-1
    )


def positions_of(segment_ids):
    index = jnp.arange(segment_ids.shape[0], dtype=jnp.int32)
    change = jnp.concatenate([jnp.ones((1,), dtype=jnp.bool_), segment_ids[1:] != segment_ids[:-1]])
    starts = jnp.where(change, index, jnp.zeros_like(index))
    return index - lax.cummax(starts, axis=0)


def allowed_pairs(segment_ids):
    index = jnp.arange(segment_ids.shape[0], dtype=jnp.int32)
    return (segment_ids[:, None] == segment_ids[None, :]) & (index[None, :] <= index[:, None])


def rms_scale(values):
    return lax.rsqrt(jnp.mean(values * values, axis=-1, keepdims=True) + EPS)


def norm_back(values, inv_root, gain, grads):
    normed = values * inv_root
    scaled = grads * gain
    result = inv_root * (scaled - normed * jnp.mean(scaled * normed, axis=-1, keepdims=True))
    return (result, jnp.sum(grads * normed, axis=0))


def matmul(left, right):
    return jnp.dot(left, right, preferred_element_type=jnp.float32)


def head_scores(query_head, key_head, allowed, scale_factor):
    scores = matmul(query_head, key_head.T) * scale_factor
    return jnp.where(allowed, scores, -1e30)


def head_forward(inputs, key_heads, value_heads, allowed, scale_factor):
    query_head, kv_slot = inputs
    scores = head_scores(query_head, key_heads[kv_slot], allowed, scale_factor)
    peak = jnp.max(scores, axis=-1, keepdims=True)
    expo = jnp.exp(scores - peak)
    total = jnp.sum(expo, axis=-1, keepdims=True)
    probs = expo / total
    mixed = matmul(probs.astype(jnp.bfloat16), value_heads[kv_slot])
    return (mixed, (peak + jnp.log(total))[:, 0])


def head_backward(inputs, key_heads, value_heads, allowed, scale_factor):
    query_head, kv_slot, grad_head, log_total = inputs
    key_head = key_heads[kv_slot]
    value_head = value_heads[kv_slot]
    scores = head_scores(query_head, key_head, allowed, scale_factor)
    probs = jnp.exp(scores - log_total[:, None])
    prob_grad = matmul(grad_head, value_head.T)
    value_grad = matmul(probs.astype(jnp.bfloat16).T, grad_head)
    inner = jnp.sum(probs * prob_grad, axis=-1, keepdims=True)
    score_grad = (probs * (prob_grad - inner)).astype(jnp.bfloat16)
    query_grad = matmul(score_grad, key_head) * scale_factor
    key_grad = matmul(score_grad.T, query_head) * scale_factor
    return (query_grad, key_grad, value_grad)


def body(
    tokens,
    cotangent,
    destination,
    segment_ids,
    attn_gain,
    w_query,
    w_key,
    w_value,
    w_output,
    ffn_gain,
    w_gate,
    w_up,
    w_down,
):
    row_count = tokens.shape[0]
    quarter = tokens.shape[1]
    col_start = lax.axis_index("col") * quarter
    group_size = HEADS // KV
    send_order = jnp.argsort(destination)
    slot_ids = destination[send_order] % row_count
    arrived_rows, arrived_grads, arrived_slots = (
        lax.all_to_all(tokens[send_order], "row", split_axis=0, concat_axis=0, tiled=True),
        lax.all_to_all(cotangent[send_order], "row", split_axis=0, concat_axis=0, tiled=True),
        lax.all_to_all(slot_ids, "row", split_axis=0, concat_axis=0, tiled=True),
    )
    placing = jnp.argsort(arrived_slots)
    full_rows, full_grads = (
        lax.all_gather(arrived_rows[placing], "col", axis=1, tiled=True),
        lax.all_gather(arrived_grads[placing], "col", axis=1, tiled=True),
    )
    query_w, key_w, value_w, output_w = (
        lax.all_gather(w_query, "row", axis=0, tiled=True),
        lax.all_gather(w_key, "row", axis=0, tiled=True),
        lax.all_gather(w_value, "row", axis=0, tiled=True),
        lax.all_gather(w_output, "row", axis=0, tiled=True),
    )
    cosine, sine = rope_tables(positions_of(segment_ids))
    allowed = allowed_pairs(segment_ids)
    rows_wide = full_rows.astype(jnp.float32)
    inv_one = rms_scale(rows_wide)
    normed_one = (rows_wide * inv_one * attn_gain).astype(jnp.bfloat16)
    query = matmul(normed_one, query_w)
    key_raw = matmul(normed_one, key_w)
    value_raw = matmul(normed_one, value_w)
    query_heads_count = query.shape[1] // HD
    kv_count = key_raw.shape[1] // HD
    query_rot = (
        rotate(query.reshape(row_count, query_heads_count, HD), cosine, sine)
        .astype(jnp.bfloat16)
        .transpose(1, 0, 2)
    )
    key_rot = (
        rotate(key_raw.reshape(row_count, kv_count, HD), cosine, sine)
        .astype(jnp.bfloat16)
        .transpose(1, 0, 2)
    )
    value_heads = value_raw.astype(jnp.bfloat16).reshape(row_count, kv_count, HD).transpose(1, 0, 2)
    kv_slots = jnp.arange(query_heads_count, dtype=jnp.int32) // group_size
    scale_factor = HD ** (-0.5)
    mixed_heads, log_totals = lax.map(
        partial(
            head_forward,
            key_heads=key_rot,
            value_heads=value_heads,
            allowed=allowed,
            scale_factor=scale_factor,
        ),
        (query_rot, kv_slots),
    )
    mixed = (
        mixed_heads.transpose(1, 0, 2)
        .reshape(row_count, query_heads_count * HD)
        .astype(jnp.bfloat16)
    )
    attn_terms = matmul(mixed, output_w.T)
    attn_full = lax.psum(attn_terms, "col")
    resid = rows_wide + attn_full
    inv_two = rms_scale(resid)
    normed_two = (resid * inv_two * ffn_gain).astype(jnp.bfloat16)
    resid_part = lax.dynamic_slice_in_dim(resid, col_start, quarter, 1)
    gate_w, up_w, down_w = (
        lax.all_gather(w_gate, "row", axis=0, tiled=True),
        lax.all_gather(w_up, "row", axis=0, tiled=True),
        lax.all_gather(w_down, "row", axis=0, tiled=True),
    )
    gate = matmul(normed_two, gate_w)
    upper = matmul(normed_two, up_w)
    sigmoid_gate = jax.nn.sigmoid(gate)
    activ = (gate * sigmoid_gate * upper).astype(jnp.bfloat16)
    ffn_share = lax.psum_scatter(
        matmul(activ, down_w.T).astype(jnp.bfloat16), "col", scatter_dimension=1, tiled=True
    ).astype(jnp.float32)
    output_share = (resid_part + ffn_share).astype(jnp.bfloat16)
    gate_w, up_w, down_w = (
        lax.all_gather(w_gate, "row", axis=0, tiled=True),
        lax.all_gather(w_up, "row", axis=0, tiled=True),
        lax.all_gather(w_down, "row", axis=0, tiled=True),
    )
    down_weight_grad = matmul(full_grads.T, activ)
    act_grad = matmul(full_grads, down_w)
    gate_grad = (act_grad * upper * sigmoid_gate * (1.0 + gate * (1.0 - sigmoid_gate))).astype(
        jnp.bfloat16
    )
    up_grad = (act_grad * gate * sigmoid_gate).astype(jnp.bfloat16)
    gate_weight_grad = matmul(normed_two.T, gate_grad)
    up_weight_grad = matmul(normed_two.T, up_grad)
    normed_terms_two = matmul(gate_grad, gate_w.T) + matmul(up_grad, up_w.T)
    normed_grad_two = lax.psum(normed_terms_two, "col")
    resid_norm_grad, ffn_gain_grad = norm_back(resid, inv_two, ffn_gain, normed_grad_two)
    resid_grad = full_grads.astype(jnp.float32) + resid_norm_grad
    attn_grad_low = resid_grad.astype(jnp.bfloat16)
    ffn_results = (
        lax.psum_scatter(
            gate_weight_grad.astype(jnp.bfloat16), "row", scatter_dimension=0, tiled=True
        ).astype(jnp.float32),
        lax.psum_scatter(
            up_weight_grad.astype(jnp.bfloat16), "row", scatter_dimension=0, tiled=True
        ).astype(jnp.float32),
        lax.psum_scatter(
            down_weight_grad.astype(jnp.bfloat16), "row", scatter_dimension=0, tiled=True
        ).astype(jnp.float32),
        lax.psum_scatter(
            ffn_gain_grad.astype(jnp.bfloat16), "row", scatter_dimension=0, tiled=True
        ).astype(jnp.float32),
    )
    query_w, key_w, value_w, output_w = (
        lax.all_gather(w_query, "row", axis=0, tiled=True),
        lax.all_gather(w_key, "row", axis=0, tiled=True),
        lax.all_gather(w_value, "row", axis=0, tiled=True),
        lax.all_gather(w_output, "row", axis=0, tiled=True),
    )
    output_weight_grad = matmul(attn_grad_low.T, mixed)
    mixed_grad = matmul(attn_grad_low, output_w).astype(jnp.bfloat16)
    mixed_grad_heads = mixed_grad.reshape(row_count, query_heads_count, HD).transpose(1, 0, 2)
    query_grads, key_grads, value_grads = lax.map(
        partial(
            head_backward,
            key_heads=key_rot,
            value_heads=value_heads,
            allowed=allowed,
            scale_factor=scale_factor,
        ),
        (query_rot, kv_slots, mixed_grad_heads, log_totals),
    )
    query_grad = (
        rotate_back(query_grads.transpose(1, 0, 2), cosine, sine)
        .reshape(row_count, query_heads_count * HD)
        .astype(jnp.bfloat16)
    )
    key_sum = key_grads.reshape(kv_count, group_size, row_count, HD).sum(axis=1).transpose(1, 0, 2)
    key_grad = (
        rotate_back(key_sum, cosine, sine).reshape(row_count, kv_count * HD).astype(jnp.bfloat16)
    )
    value_sum = (
        value_grads.reshape(kv_count, group_size, row_count, HD).sum(axis=1).transpose(1, 0, 2)
    )
    value_grad = value_sum.reshape(row_count, kv_count * HD).astype(jnp.bfloat16)
    query_weight_grad = matmul(normed_one.T, query_grad)
    key_weight_grad = matmul(normed_one.T, key_grad)
    value_weight_grad = matmul(normed_one.T, value_grad)
    normed_terms_one = (
        matmul(query_grad, query_w.T) + matmul(key_grad, key_w.T) + matmul(value_grad, value_w.T)
    )
    normed_grad_one = lax.psum(normed_terms_one.astype(jnp.bfloat16), "col").astype(jnp.float32)
    rows_norm_grad, attn_gain_grad = norm_back(rows_wide, inv_one, attn_gain, normed_grad_one)
    rows_grad = resid_grad + rows_norm_grad
    input_share = lax.dynamic_slice_in_dim(rows_grad, col_start, quarter, 1).astype(jnp.bfloat16)
    attn_results = (
        lax.psum_scatter(
            query_weight_grad.astype(jnp.bfloat16), "row", scatter_dimension=0, tiled=True
        ).astype(jnp.float32),
        lax.psum_scatter(
            key_weight_grad.astype(jnp.bfloat16), "row", scatter_dimension=0, tiled=True
        ).astype(jnp.float32),
        lax.psum_scatter(
            value_weight_grad.astype(jnp.bfloat16), "row", scatter_dimension=0, tiled=True
        ).astype(jnp.float32),
        lax.psum_scatter(
            output_weight_grad.astype(jnp.bfloat16), "row", scatter_dimension=0, tiled=True
        ).astype(jnp.float32),
        lax.psum_scatter(
            attn_gain_grad.astype(jnp.bfloat16), "row", scatter_dimension=0, tiled=True
        ).astype(jnp.float32),
    )
    back_rows, back_grads = (
        lax.all_to_all(output_share[arrived_slots], "row", split_axis=0, concat_axis=0, tiled=True),
        lax.all_to_all(input_share[arrived_slots], "row", split_axis=0, concat_axis=0, tiled=True),
    )
    restore = jnp.argsort(send_order)
    return (
        back_rows[restore],
        back_grads[restore],
        attn_results[4],
        attn_results[0],
        attn_results[1],
        attn_results[2],
        attn_results[3],
        ffn_results[3],
        ffn_results[0],
        ffn_results[1],
        ffn_results[2],
    )


def solution(mesh):
    placed = (
        P("row", "col"),
        P("row", "col"),
        P("row"),
        P("row"),
        P(),
        P("row", "col"),
        P("row", "col"),
        P("row", "col"),
        P("row", "col"),
        P(),
        P("row", "col"),
        P("row", "col"),
        P("row", "col"),
    )
    return jax.shard_map(
        body,
        mesh=mesh,
        in_specs=placed,
        out_specs=(
            P("row", "col"),
            P("row", "col"),
            P("row"),
            P("row", "col"),
            P("row", "col"),
            P("row", "col"),
            P("row", "col"),
            P("row"),
            P("row", "col"),
            P("row", "col"),
            P("row", "col"),
        ),
        check_vma=False,
    )
```

profile of v0, /device:TPU:0, one launch (start us, length us, event | category | flops | bytes accessed | tf_op | source)
XLA Modules:
  0.0 1312.7 jit_solution(15525933860058886407)
XLA Ops:
  7.2 4.5 sort.45
  12.3 3.6 gather_fusion.1
  16.6 8.4 all-to-all-start.1
  25.0 2.6 gather_fusion
  27.7 4.6 all-to-all-done.1
  32.3 3.9 all-to-all-start
  37.6 3.8 sort.46
  41.4 6.6 all-to-all-done
  48.0 2.6 gather_fusion.2
  53.0 22.4 %all_gather.36 = bf16[2048,64]{1,0:T(8,128)(2,1)S(1)} all-gather(bf16[64,64]{1,0:T(8,128)(2,1)S(1)} %copy-done.22), channel_id=1, replica_groups=mesh['row'=32,'col'=4] {'row'}, dimensions={0}, use_global_device_ids=true | all-gather | bytes 270336 | tf_op jit(solution)/shard_map/all_gather | solution.py:133
  75.5 26.7 %all_gather.37 = bf16[2048,64]{1,0:T(8,128)(2,1)} all-gather(bf16[64,64]{1,0:T(8,128)(2,1)S(1)} %copy-done.23), channel_id=1, replica_groups=mesh['row'=32,'col'=4] {'row'}, dimensions={0}, use_global_device_ids=true | all-gather | bytes 270336 | tf_op jit(solution)/shard_map/all_gather | solution.py:134
  102.5 2.2 fusion.42
  104.8 2.4 convolution_bitcast_fusion.2
  107.7 2.5 fusion.43
  111.2 14.4 %all-gather.10.cloned.1.call-done = bf16[2048,512]{1,0:T(8,128)(2,1)} async-done(((bf16[64,512]{1,0:T(8,128)(2,1)}), bf16[2048,512]{1,0:T(8,128)(2,1)}) %all-gather.10.cloned.1.call-update) | async-done | bytes 2097168 | tf_op jit(solution)/shard_map/all_gather | solution.py:132
  125.6 3.0 fusion.73
  129.4 24.0 %while.32 = (s32[]{:T(128)}, bf16[8,512,64]{1,2,0:T(8,128)(2,1)S(1)}, f32[8,512]{1,0:T(8,128)}, bf16[8,512,64]{2,1,0:T(8,128)(2,1)S(1)}, bf16[1,512,64]{2,1,0:T(...) while((s32[]{:T(128)}, bf16[8,512,64]{1,2,0:T(8,128)(2,1)S(1)}, ...), condition=%wide.region_8.9_spmd.clone.clone, body=%wide.region_5.8_spmd.clone.sunk.clone | while | flops 69991936 | bytes 3695189 | solution.py:160
  153.4 17.8 %all-gather.12.cloned.1.call-done = bf16[2048,512]{1,0:T(8,128)(2,1)} async-done(((bf16[64,512]{1,0:T(8,128)(2,1)}), bf16[2048,512]{1,0:T(8,128)(2,1)}) %all-gather.12.cloned.1.call-update) | async-done | bytes 2097168 | tf_op jit(solution)/shard_map/all_gather | solution.py:135
  171.2 4.9 fusion.75
  177.4 2.6 gather_fusion.5
  180.0 17.1 %all_to_all.60 = bf16[32,16,512]{2,1,0:T(8,128)(2,1)S(1)} all-to-all(bf16[32,16,512]{2,1,0:T(8,128)(2,1)} %bitcast.194), channel_id=1, replica_groups=mesh['row'=32,'col'=4] {'row'}, dimensions={0} | all-to-all | bytes 1048576 | tf_op jit(solution)/shard_map/all_to_all | solution.py:123
  197.1 2.8 gather_fusion.6
  201.1 67.2 %all-reduce.7.cloned.1.call-done = f32[512,2048]{1,0:T(8,128)} async-done(((f32[512,2048]{1,0:T(8,128)}), f32[512,2048]{1,0:T(8,128)}) %all-reduce.7.cloned.1.call-update) | async-done | bytes 4194320 | tf_op jit(solution)/shard_map/psum | solution.py:176
  268.3 2.8 multiply_reduce_fusion.4
  271.1 2.0 copy-done.2
  274.8 44.2 %all-gather.14.cloned.1.call-done = bf16[2048,1408]{1,0:T(8,128)(2,1)} async-done(((bf16[64,1408]{1,0:T(8,128)(2,1)}), bf16[2048,1408]{1,0:T(8,128)(2,1)}) %all-gather.14.cloned.1.call-update) | async-done | bytes 5767184 | tf_op jit(solution)/shard_map/all_gather | solution.py:182
  319.0 8.3 fusion.76
  327.3 41.5 %all-gather.16.cloned.1.call-done = bf16[2048,1408]{1,0:T(8,128)(2,1)} async-done(((bf16[64,1408]{1,0:T(8,128)(2,1)}), bf16[2048,1408]{1,0:T(8,128)(2,1)}) %all-gather.16.cloned.1.call-update) | async-done | bytes 5767184 | tf_op jit(solution)/shard_map/all_gather | solution.py:183
  368.8 8.3 fusion.77
  377.1 23.9 %all-gather.22.cloned.1.call-done = bf16[512,2048]{1,0:T(8,128)(2,1)} async-done(((bf16[512,512]{1,0:T(8,128)(2,1)}), bf16[512,2048]{1,0:T(8,128)(2,1)}) %all-gather.22.cloned.1.call-update) | async-done | bytes 2097168 | tf_op jit(solution)/shard_map/all_gather | solution.py:129
  400.9 51.0 %all-gather.18.cloned.1.call-done = bf16[2048,1408]{1,0:T(8,128)(2,1)} async-done(((bf16[64,1408]{1,0:T(8,128)(2,1)}), bf16[2048,1408]{1,0:T(8,128)(2,1)}) %all-gather.18.cloned.1.call-update) | async-done | bytes 5767184 | tf_op jit(solution)/shard_map/all_gather | solution.py:184
  452.0 10.3 multiply_convert_fusion.3
  462.3 6.6 fusion.78
  468.9 5.1 convolution_add_fusion
  474.2 7.9 convolution_convert_fusion.5
  482.2 83.7 %all-reduce.9.cloned.1.call-done = f32[512,2048]{1,0:T(8,128)} async-done(((f32[512,2048]{1,0:T(8,128)}), f32[512,2048]{1,0:T(8,128)}) %all-reduce.9.cloned.1.call-update) | async-done | bytes 4194320 | tf_op jit(solution)/shard_map/psum | solution.py:208
  565.9 5.2 multiply_reduce_fusion.1
  571.8 2.8 multiply_add_fusion
  574.6 2.0 copy-done.4
  579.3 65.5 %while.33 = (s32[]{:T(128)}, f32[8,512,64]{1,2,0:T(8,128)}, f32[8,512,64]{1,2,0:T(8,128)}, f32[8,512,64]{1,2,0:T(8,128)}, bf16[8,512,64]{2,1,0:T(8,128)(2,1)}, /...) while((s32[]{:T(128)}, f32[8,512,64]{1,2,0:T(8,128)}, ...), condition=%wide.region_17.18_spmd.clone.clone, body=%wide.region_15.17_spmd.clone.sunk.clone | while | flops 170982912 | bytes 8996457 | solution.py:235
  602.0 1.9 fusion.161
  653.1 2.1 add_convert_fusion
  659.3 2.8 convolution_convert_fusion.4
  662.2 5.2 convolution_convert_fusion.3
  667.5 8.0 convolution_convert_fusion.2
  675.5 8.1 convolution_convert_fusion.1
  683.9 7.9 convolution_convert_fusion
  693.6 2.6 gather_fusion.3
  696.3 7.3 all-to-all-start.2
  703.5 10.4 all-reduce.11.cloned.1.call-done
  713.9 2.9 fusion.41
  718.4 2.6 gather_fusion.7
  721.0 7.3 all-to-all-start.4
  728.3 3.8 sort.47
  733.4 61.5 %reduce-scatter.13.cloned.1.call-done = bf16[64,64]{1,0:T(8,128)(2,1)} async-done(((bf16[2048,64]{1,0:T(8,128)(2,1)}), bf16[64,64]{1,0:T(8,128)(2,1)}) %reduce-scatter.13.cloned.1.call-update) | async-done | bytes 8208 | tf_op jit(solution)/shard_map/reduce_scatter | solution.py:272
  796.2 78.6 %reduce-scatter.15.cloned.1.call-done = bf16[64,64]{1,0:T(8,128)(2,1)} async-done(((bf16[2048,64]{1,0:T(8,128)(2,1)}), bf16[64,64]{1,0:T(8,128)(2,1)}) %reduce-scatter.15.cloned.1.call-update) | async-done | bytes 8208 | tf_op jit(solution)/shard_map/reduce_scatter | solution.py:275
  876.1 2.6 gather_fusion.4
  878.7 64.4 %all-reduce.2 = (bf16[2048]{0:T(1024)(128)(2,1)S(1)}, bf16[2048]{0:T(1024)(128)(2,1)S(1)}) all-reduce(bf16[2048]{0:T(1024)(128)(2,1)S(1)} %get-tuple-element.249, bf16[2048]{0:T(1024)(128)(2,1)S(1)} %copy-done.20), channel_id=5, replica_groups=mesh['row'=32,'col'=4] {'row'}, use_global_device_ids=true, to_apply=%region_23.24.clone | all-reduce | flops 4096 | bytes 16384
  943.7 2.6 gather_fusion.8
  946.4 10.0 reduce-scatter.11.cloned.1.call-done
  957.9 80.2 %reduce-scatter.17.cloned.1.call-done = bf16[64,512]{1,0:T(8,128)(2,1)} async-done(((bf16[2048,512]{1,0:T(8,128)(2,1)}), bf16[64,512]{1,0:T(8,128)(2,1)}) %reduce-scatter.17.cloned.1.call-update) | async-done | bytes 65552 | tf_op jit(solution)/shard_map/reduce_scatter | solution.py:278
  1039.6 86.9 %reduce-scatter.19.cloned.1.call-done = bf16[64,1408]{1,0:T(8,128)(2,1)} async-done(((bf16[2048,1408]{1,0:T(8,128)(2,1)}), bf16[64,1408]{1,0:T(8,128)(2,1)}) %reduce-scatter.19.cloned.1.call-update) | async-done | bytes 180240 | tf_op jit(solution)/shard_map/reduce_scatter | solution.py:213
  1128.2 87.2 %reduce-scatter.21.cloned.1.call-done = bf16[64,1408]{1,0:T(8,128)(2,1)} async-done(((bf16[2048,1408]{1,0:T(8,128)(2,1)}), bf16[64,1408]{1,0:T(8,128)(2,1)}) %reduce-scatter.21.cloned.1.call-update) | async-done | bytes 180240 | tf_op jit(solution)/shard_map/reduce_scatter | solution.py:216
  1217.0 86.7 %reduce-scatter.23.cloned.1.call-done = bf16[64,1408]{1,0:T(8,128)(2,1)} async-done(((bf16[2048,1408]{1,0:T(8,128)(2,1)}), bf16[64,1408]{1,0:T(8,128)(2,1)}) %reduce-scatter.23.cloned.1.call-update) | async-done | bytes 180240 | tf_op jit(solution)/shard_map/reduce_scatter | solution.py:219
  (266 shorter events, 130.6 us)
Async XLA Ops:
  7.2 17.9 %copy-start = (bf16[512,512]{1,0:T(8,128)(2,1)S(1)}, bf16[512,512]{1,0:T(8,128)(2,1)}, u32[]{:S(2)}) copy-start(bf16[512,512]{1,0:T(8,128)(2,1)} %param.17) | copy-start | bytes 1572868
  11.7 0.6 copy-start.27
  12.3 24.0 %copy-start.16 = (s32[1024]{0:T(1024)}, s32[1024]{0:T(1024)S(1)}, u32[]{:S(2)}) copy-start(s32[1024]{0:T(1024)S(1)} %pad_clamp_fusion.3) | copy-start | bytes 12292
  16.6 15.7 %all-to-all-start.1 = ((s32[32,16,1]{1,2,0:T(1,128)}), s32[32,16,1]{1,2,0:T(1,128)S(1)}, u32[]{:S(2)}, u32[]{:S(2)}) async-start(s32[32,16,1]{1,2,0:T(1,128)} %bitcast.2), calls=%async_computation.1 | async-start | bytes 32768 | tf_op jit(solution)/shard_map/all_to_all | solution.py:124
  27.7 24.6 %copy-start.26 = (s32[512]{0:T(512)S(1)}, s32[512]{0:T(512)}, u32[]{:S(2)}) copy-start(s32[512]{0:T(512)} %param.20) | copy-start | bytes 6148
  27.7 25.3 %copy-start.22 = (bf16[64,64]{1,0:T(8,128)(2,1)S(1)}, bf16[64,64]{1,0:T(8,128)(2,1)}, u32[]{:S(2)}) copy-start(bf16[64,64]{1,0:T(8,128)(2,1)} %param.23) | copy-start | bytes 24580
  27.7 47.8 %copy-start.23 = (bf16[64,64]{1,0:T(8,128)(2,1)S(1)}, bf16[64,64]{1,0:T(8,128)(2,1)}, u32[]{:S(2)}) copy-start(bf16[64,64]{1,0:T(8,128)(2,1)} %param.24) | copy-start | bytes 24580
  32.3 15.7 %all-to-all-start = ((bf16[32,16,512]{2,1,0:T(8,128)(2,1)}), bf16[32,16,512]{2,1,0:T(8,128)(2,1)S(1)}, u32[]{:S(2)}, u32[]{:S(2)}) async-start(bf16[32,16,512]{2,1,0:T(8,128)(2,1)} %bitcast), calls=%async_computation | async-start | bytes 1048576 | tf_op jit(solution)/shard_map/all_to_all | solution.py:122
  36.2 66.3 %all-gather.20.cloned.1.call-start = ((), (), s32[]{:S(2)}) async-start(), calls=%async_computation.29 | async-start | bytes 2621440 | tf_op jit(solution)/shard_map/all_gather | solution.py:128
  41.3 11.6 copy-start.21
  48.0 56.8 %copy-start.24 = (f32[2048]{0:T(1024)S(1)}, f32[2048]{0:T(1024)}, u32[]{:S(2)}) copy-start(f32[2048]{0:T(1024)} %param.21) | copy-start | bytes 24580
  50.6 75.0 %all-gather.10.cloned.1.call-start = ((), (), s32[]{:S(2)}) async-start(), calls=%async_computation.13 | async-start | bytes 2162688 | tf_op jit(solution)/shard_map/all_gather | solution.py:132
  51.4 119.8 %all-gather.12.cloned.1.call-start = ((), (), s32[]{:S(2)}) async-start(), calls=%async_computation.14 | async-start | bytes 2162688 | tf_op jit(solution)/shard_map/all_gather | solution.py:135
  52.1 216.2 %all-reduce.7.cloned.1.call-start = ((), (), s32[]{:S(2)}) async-start(), calls=%async_computation.15 | async-start | bytes 8388608 | tf_op jit(solution)/shard_map/psum | solution.py:176
  52.2 55.4 %copy-start.29 = (f32[32]{0:T(128)}, f32[32]{0:T(128)S(1)}, u32[]{:S(2)}) copy-start(f32[32]{0:T(128)S(1)} %negate_power_fusion) | copy-start | bytes 388
  53.0 54.5 %copy-start.15 = (f32[512]{0:T(512)}, f32[512]{0:T(512)S(1)}, u32[]{:S(2)}) copy-start(f32[512]{0:T(512)S(1)} %fusion.70) | copy-start | bytes 6148
  75.5 34.8 %copy-start.10 = (bf16[2048,64]{1,0:T(8,128)(2,1)}, bf16[2048,64]{1,0:T(8,128)(2,1)S(1)}, u32[]{:S(2)}) copy-start(bf16[2048,64]{1,0:T(8,128)(2,1)S(1)} %all_gather.36) | copy-start | bytes 786436
  102.5 5.2 copy-start.6
  104.8 2.8 copy-start.18
  153.4 22.7 %copy-start.9 = (bf16[8,512,64]{2,1,0:T(8,128)(2,1)}, bf16[8,512,64]{2,1,0:T(8,128)(2,1)S(1)}, u32[]{:S(2)}) copy-start(bf16[8,512,64]{2,1,0:T(8,128)(2,1)S(1)} %get-tuple-element.556) | copy-start | bytes 1572868
  176.1 1.2 copy-start.5
  176.1 1.3 copy-start.17
  176.1 142.8 %all-gather.14.cloned.1.call-start = ((), (), s32[]{:S(2)}) async-start(), calls=%async_computation.16 | async-start | bytes 5947392 | tf_op jit(solution)/shard_map/all_gather | solution.py:182
  176.7 192.1 %all-gather.16.cloned.1.call-start = ((), (), s32[]{:S(2)}) async-start(), calls=%async_computation.17 | async-start | bytes 5947392 | tf_op jit(solution)/shard_map/all_gather | solution.py:183
  177.3 223.6 %all-gather.22.cloned.1.call-start = ((), (), s32[]{:S(2)}) async-start(), calls=%async_computation.30 | async-start | bytes 2621440 | tf_op jit(solution)/shard_map/all_gather | solution.py:129
  180.0 88.3 %copy-start.7 = (bf16[512,2048]{1,0:T(8,128)(2,1)S(1)}, bf16[512,2048]{1,0:T(8,128)(2,1)}, u32[]{:S(2)}) copy-start(bf16[512,2048]{1,0:T(8,128)(2,1)} %all-gather.20.cloned.1.call-done) | copy-start | bytes 6291460
  199.9 252.1 %all-gather.18.cloned.1.call-start = ((), (), s32[]{:S(2)}) async-start(), calls=%async_computation.18 | async-start | bytes 5947392 | tf_op jit(solution)/shard_map/all_gather | solution.py:184
  200.6 72.4 %copy-start.14 = (f32[2048]{0:T(1024)S(1)}, f32[2048]{0:T(1024)}, u32[]{:S(2)}) copy-start(f32[2048]{0:T(1024)} %param.26) | copy-start | bytes 24580
  200.6 365.2 %all-reduce.9.cloned.1.call-start = ((), (), s32[]{:S(2)}) async-start(), calls=%async_computation.20 | async-start | bytes 8388608 | tf_op jit(solution)/shard_map/psum | solution.py:208
  271.1 2.0 copy-start.2
  462.3 6.6 copy-start.33
  462.3 6.6 copy-start.32
  462.3 6.6 copy-start.30
  474.0 218.0 %reduce-scatter.9.cloned.1.call-start = ((), (), s32[]{:S(2)}) async-start(), calls=%async_computation.19 | async-start | bytes 2621440 | tf_op jit(solution)/shard_map/reduce_scatter | solution.py:190
  482.1 231.8 %all-reduce.11.cloned.1.call-start = ((), (), s32[]{:S(2)}) async-start(), calls=%async_computation.21 | async-start | bytes 4194304 | tf_op jit(solution)/shard_map/psum | solution.py:264
  565.9 5.2 copy-start.3
  565.9 5.9 copy-start.8
  571.8 4.8 copy-start.12
  574.6 2.0 copy-start.4
  647.4 4.4 copy-start.11
  651.8 1.3 copy-start.13
  653.1 2.2 copy-start.19
  653.1 2.2 copy-start.25
  655.2 139.7 %reduce-scatter.13.cloned.1.call-start = ((), (), s32[]{:S(2)}) async-start(), calls=%async_computation.23 | async-start | bytes 540672 | tf_op jit(solution)/shard_map/reduce_scatter | solution.py:272
  657.1 217.6 %reduce-scatter.15.cloned.1.call-start = ((), (), s32[]{:S(2)}) async-start(), calls=%async_computation.24 | async-start | bytes 540672 | tf_op jit(solution)/shard_map/reduce_scatter | solution.py:275
  659.2 297.1 %reduce-scatter.11.cloned.1.call-start = ((), (), s32[]{:S(2)}) async-start(), calls=%async_computation.22 | async-start | bytes 2162688 | tf_op jit(solution)/shard_map/reduce_scatter | solution.py:269
  662.1 375.9 %reduce-scatter.17.cloned.1.call-start = ((), (), s32[]{:S(2)}) async-start(), calls=%async_computation.25 | async-start | bytes 2162688 | tf_op jit(solution)/shard_map/reduce_scatter | solution.py:278
  667.4 459.0 %reduce-scatter.19.cloned.1.call-start = ((), (), s32[]{:S(2)}) async-start(), calls=%async_computation.26 | async-start | bytes 5947392 | tf_op jit(solution)/shard_map/reduce_scatter | solution.py:213
  675.5 539.8 %reduce-scatter.21.cloned.1.call-start = ((), (), s32[]{:S(2)}) async-start(), calls=%async_computation.27 | async-start | bytes 5947392 | tf_op jit(solution)/shard_map/reduce_scatter | solution.py:216
  683.6 620.1 %reduce-scatter.23.cloned.1.call-start = ((), (), s32[]{:S(2)}) async-start(), calls=%async_computation.28 | async-start | bytes 5947392 | tf_op jit(solution)/shard_map/reduce_scatter | solution.py:219
  696.3 24.8 %all-to-all-start.2 = ((bf16[32,16,512]{2,1,0:T(8,128)(2,1)}), bf16[32,16,512]{2,1,0:T(8,128)(2,1)S(1)}, u32[]{:S(2)}, u32[]{:S(2)}) async-start(bf16[32,16,512]{2,1,0:T(8,128)(2,1)} %bitcast.14), calls=%async_computation.3 | async-start | bytes 1048576 | tf_op jit(solution)/shard_map/all_to_all | solution.py:286
  716.8 11.5 copy-start.28
  716.9 15.3 %copy-start.31 = (u32[128]{0:T(128)S(1)}, u32[128]{0:T(128)}, u32[]{:S(2)}) copy-start(u32[128]{0:T(128)} %constant.120) | copy-start | bytes 1540
  718.4 160.3 %copy-start.20 = (bf16[2048]{0:T(1024)(128)(2,1)S(1)}, bf16[2048]{0:T(1024)(128)(2,1)}, u32[]{:S(2)}) copy-start(bf16[2048]{0:T(1024)(128)(2,1)} %get-tuple-element.247) | copy-start | bytes 12292
  721.0 222.7 %all-to-all-start.4 = ((bf16[32,16,512]{2,1,0:T(8,128)(2,1)}), bf16[32,16,512]{2,1,0:T(8,128)(2,1)S(1)}, u32[]{:S(2)}, u32[]{:S(2)}) async-start(bf16[32,16,512]{2,1,0:T(8,128)(2,1)} %bitcast.24), calls=%async_computation.5 | async-start | bytes 1048576 | tf_op jit(solution)/shard_map/all_to_all | solution.py:287
  876.1 429.3 %copy-start.1 = (bf16[512,512]{1,0:T(8,128)(2,1)S(1)}, bf16[512,512]{1,0:T(8,128)(2,1)}, u32[]{:S(2)}) copy-start(bf16[512,512]{1,0:T(8,128)(2,1)} %param.17) | copy-start | bytes 1572868
Sparse Core Ops, SparseCore 0:
  50.7 28.4 all-gather.19
  81.5 44.0 all-gather.9
  127.9 43.2 all-gather.11
  176.2 91.9 all-reduce.6
  270.6 48.3 all-gather.13
  321.3 47.4 all-gather.15
  371.1 29.7 all-gather.21
  403.4 48.4 all-gather.17
  474.1 91.7 all-reduce.8
  568.1 29.5 reduce-scatter.8
  655.3 58.5 all-reduce.10
  717.8 77.0 reduce-scatter.12
  798.3 76.3 reduce-scatter.14
  878.2 78.1 reduce-scatter.10
  959.8 78.2 reduce-scatter.16
  1041.7 84.7 reduce-scatter.18
  1130.5 84.7 reduce-scatter.20
  1218.9 84.7 reduce-scatter.22
where the time goes:
time: 1320 us; the launch traced here: 1310 us
  waiting for transfers between devices  860 us (65%)
  matrix products  170 us (13%)
  blocking collectives  131 us (10%)
  other arithmetic  55.9 us (4%)
  local copies, waits for them, and re-layouts  51.2 us (4%)
  starting transfers between devices  28.6 us (2%)
  between operations  16 us (1%)
    dot_general x77, matrix products, matmul(): return jnp.dot(left, right, preferred_element_type=jnp.float32)  170 us
    reduce_scatter x1, waiting for transfers between devices, body(): lax.psum_scatter(up_weight_grad.astype(jnp.bfloat16), 'row', scatter_dime...  87.2 us
    reduce_scatter x1, waiting for transfers between devices, body(): lax.psum_scatter(gate_weight_grad.astype(jnp.bfloat16), 'row', scatter_di...  86.9 us
    reduce_scatter x1, waiting for transfers between devices, body(): lax.psum_scatter(down_weight_grad.astype(jnp.bfloat16), 'row', scatter_di...  86.7 us
    psum x1, waiting for transfers between devices, body(): normed_grad_two = lax.psum(normed_terms_two, 'col')  83.7 us
    reduce_scatter x1, waiting for transfers between devices, body(): lax.psum_scatter(output_weight_grad.astype(jnp.bfloat16), 'row', scatter_...  80.2 us
    reduce_scatter x1, waiting for transfers between devices, body(): lax.psum_scatter(value_weight_grad.astype(jnp.bfloat16), 'row', scatter_d...  78.6 us
    psum x1, waiting for transfers between devices, body(): attn_full = lax.psum(attn_terms, 'col')  67.2 us
  transfers between devices with their start and end apart: 22, of which 18 were waited for; matrix products, arithmetic and copies ran while one was open for 18% of the time, Pallas kernels for 0%

commit v1 on v0

--- a/solution.py
+++ b/solution.py
@@ -95,6 +95,32 @@
     query_grad = matmul(score_grad, key_head) * scale_factor
     key_grad = matmul(score_grad.T, query_head) * scale_factor
     return (query_grad, key_grad, value_grad)
+
+
+def gather_rows(parts):
+    widths = [part.shape[1] for part in parts]
+    packed = lax.all_gather(jnp.concatenate(parts, axis=1), "row", axis=0, tiled=True)
+    pieces = []
+    offset = 0
+    for width in widths:
+        pieces.append(packed[:, offset : offset + width])
+        offset += width
+    return pieces
+
+
+def scatter_rows(parts):
+    columns = [part.reshape(part.shape[0], -1).astype(jnp.bfloat16) for part in parts]
+    widths = [column.shape[1] for column in columns]
+    packed = lax.psum_scatter(
+        jnp.concatenate(columns, axis=1), "row", scatter_dimension=0, tiled=True
+    ).astype(jnp.float32)
+    pieces = []
+    offset = 0
+    for part, width in zip(parts, widths):
+        piece = packed[:, offset : offset + width]
+        pieces.append(piece.reshape(-1) if part.ndim == 1 else piece)
+        offset += width
+    return pieces
 
 
 def body(
@@ -128,12 +154,7 @@
         lax.all_gather(arrived_rows[placing], "col", axis=1, tiled=True),
         lax.all_gather(arrived_grads[placing], "col", axis=1, tiled=True),
     )
-    query_w, key_w, value_w, output_w = (
-        lax.all_gather(w_query, "row", axis=0, tiled=True),
-        lax.all_gather(w_key, "row", axis=0, tiled=True),
-        lax.all_gather(w_value, "row", axis=0, tiled=True),
-        lax.all_gather(w_output, "row", axis=0, tiled=True),
-    )
+    query_w, key_w, value_w, output_w = gather_rows([w_query, w_key, w_value, w_output])
     cosine, sine = rope_tables(positions_of(segment_ids))
     allowed = allowed_pairs(segment_ids)
     rows_wide = full_rows.astype(jnp.float32)
@@ -178,11 +199,7 @@
     inv_two = rms_scale(resid)
     normed_two = (resid * inv_two * ffn_gain).astype(jnp.bfloat16)
     resid_part = lax.dynamic_slice_in_dim(resid, col_start, quarter, 1)
-    gate_w, up_w, down_w = (
-        lax.all_gather(w_gate, "row", axis=0, tiled=True),
-        lax.all_gather(w_up, "row", axis=0, tiled=True),
-        lax.all_gather(w_down, "row", axis=0, tiled=True),
-    )
+    gate_w, up_w, down_w = gather_rows([w_gate, w_up, w_down])
     gate = matmul(normed_two, gate_w)
     upper = matmul(normed_two, up_w)
     sigmoid_gate = jax.nn.sigmoid(gate)
@@ -191,11 +208,6 @@
         matmul(activ, down_w.T).astype(jnp.bfloat16), "col", scatter_dimension=1, tiled=True
     ).astype(jnp.float32)
     output_share = (resid_part + ffn_share).astype(jnp.bfloat16)
-    gate_w, up_w, down_w = (
-        lax.all_gather(w_gate, "row", axis=0, tiled=True),
-        lax.all_gather(w_up, "row", axis=0, tiled=True),
-        lax.all_gather(w_down, "row", axis=0, tiled=True),
-    )
     down_weight_grad = matmul(full_grads.T, activ)
     act_grad = matmul(full_grads, down_w)
     gate_grad = (act_grad * upper * sigmoid_gate * (1.0 + gate * (1.0 - sigmoid_gate))).astype(
@@ -209,26 +221,6 @@
     resid_norm_grad, ffn_gain_grad = norm_back(resid, inv_two, ffn_gain, normed_grad_two)
     resid_grad = full_grads.astype(jnp.float32) + resid_norm_grad
     attn_grad_low = resid_grad.astype(jnp.bfloat16)
-    ffn_results = (
-        lax.psum_scatter(
-            gate_weight_grad.astype(jnp.bfloat16), "row", scatter_dimension=0, tiled=True
-        ).astype(jnp.float32),
-        lax.psum_scatter(
-            up_weight_grad.astype(jnp.bfloat16), "row", scatter_dimension=0, tiled=True
-        ).astype(jnp.float32),
-        lax.psum_scatter(
-            down_weight_grad.astype(jnp.bfloat16), "row", scatter_dimension=0, tiled=True
-        ).astype(jnp.float32),
-        lax.psum_scatter(
-            ffn_gain_grad.astype(jnp.bfloat16), "row", scatter_dimension=0, tiled=True
-        ).astype(jnp.float32),
-    )
-    query_w, key_w, value_w, output_w = (
-        lax.all_gather(w_query, "row", axis=0, tiled=True),
-        lax.all_gather(w_key, "row", axis=0, tiled=True),
-        lax.all_gather(w_value, "row", axis=0, tiled=True),
-        lax.all_gather(w_output, "row", axis=0, tiled=True),
-    )
     output_weight_grad = matmul(attn_grad_low.T, mixed)
     mixed_grad = matmul(attn_grad_low, output_w).astype(jnp.bfloat16)
     mixed_grad_heads = mixed_grad.reshape(row_count, query_heads_count, HD).transpose(1, 0, 2)
@@ -265,22 +257,28 @@
     rows_norm_grad, attn_gain_grad = norm_back(rows_wide, inv_one, attn_gain, normed_grad_one)
     rows_grad = resid_grad + rows_norm_grad
     input_share = lax.dynamic_slice_in_dim(rows_grad, col_start, quarter, 1).astype(jnp.bfloat16)
-    attn_results = (
-        lax.psum_scatter(
-            query_weight_grad.astype(jnp.bfloat16), "row", scatter_dimension=0, tiled=True
-        ).astype(jnp.float32),
-        lax.psum_scatter(
-            key_weight_grad.astype(jnp.bfloat16), "row", scatter_dimension=0, tiled=True
-        ).astype(jnp.float32),
-        lax.psum_scatter(
-            value_weight_grad.astype(jnp.bfloat16), "row", scatter_dimension=0, tiled=True
-        ).astype(jnp.float32),
-        lax.psum_scatter(
-            output_weight_grad.astype(jnp.bfloat16), "row", scatter_dimension=0, tiled=True
-        ).astype(jnp.float32),
-        lax.psum_scatter(
-            attn_gain_grad.astype(jnp.bfloat16), "row", scatter_dimension=0, tiled=True
-        ).astype(jnp.float32),
+    (
+        query_result,
+        key_result,
+        value_result,
+        output_result,
+        gate_result,
+        up_result,
+        down_result,
+        attn_gain_result,
+        ffn_gain_result,
+    ) = scatter_rows(
+        [
+            query_weight_grad,
+            key_weight_grad,
+            value_weight_grad,
+            output_weight_grad,
+            gate_weight_grad,
+            up_weight_grad,
+            down_weight_grad,
+            attn_gain_grad,
+            ffn_gain_grad,
+        ]
     )
     back_rows, back_grads = (
         lax.all_to_all(output_share[arrived_slots], "row", split_axis=0, concat_axis=0, tiled=True),
@@ -290,17 +288,16 @@
     return (
         back_rows[restore],
         back_grads[restore],
-        attn_results[4],
-        attn_results[0],
-        attn_results[1],
-        attn_results[2],
-        attn_results[3],
-        ffn_results[3],
-        ffn_results[0],
-        ffn_results[1],
-        ffn_results[2],
-    )
-
+        attn_gain_result,
+        query_result,
+        key_result,
+        value_result,
+        output_result,
+        ffn_gain_result,
+        gate_result,
+        up_result,
+        down_result,
+    )
 
 def solution(mesh):
     placed = (

time: 1320 us -> 928 us (0.70)
  waiting for transfers between devices: 860 us -> 466 us
  local copies, waits for them, and re-layouts: 51.2 us -> 191 us
  blocking collectives: 131 us -> 16.8 us
  matrix products: 170 us -> 142 us
    reduce_scatter x7 -> x0, waiting for transfers between devices: 491 us -> none  [the longest x1 87.2 us: body(): lax.psum_scatter(up_weight_grad.astype(jnp.bfloat16), 'row', scatter_dime...]
    concatenate x0 -> x2, local copies, waits for them, and re-layouts: none -> 94 us  [the longest x1 93.2 us: scatter_rows(): jnp.concatenate(columns, axis=1)]
    unnamed x18 -> x10, waiting for transfers between devices: 3.34 us -> 90.2 us
    unnamed x1 -> x0, blocking collectives: 64.4 us -> none
    all_gather x2 -> x0, blocking collectives: 49.1 us -> none  [the longest x1 26.7 us: body(): lax.all_gather(w_value, 'row', axis=0, tiled=True)]
    all_gather x5 -> x2, waiting for transfers between devices: 169 us -> 124 us  [gather_rows(): lax.all_gather(jnp.concatenate(parts, axis=1), 'row', axis=0, tiled=True)]
    unnamed x72 -> x82, local copies, waits for them, and re-layouts: 7.56 us -> 51.5 us
    dot_general x77, matrix products: 170 us -> 142 us  [matmul(): return jnp.dot(left, right, preferred_element_type=jnp.float32)]
  transfers between devices with their start and end apart: 22 -> 13, of which waited for: 18 -> 12; matrix products, arithmetic and copies ran while one was open for 18% -> 22% of each run, Pallas kernels for 0% -> 0%
where the time goes in v1:
time: 928 us; the launch traced here: 914 us
  waiting for transfers between devices  466 us (50%)
  local copies, waits for them, and re-layouts  191 us (21%)
  matrix products  142 us (15%)
  other arithmetic  49.6 us (5%)
  starting transfers between devices  34 us (4%)
  blocking collectives  16.8 us (2%)
  between operations  14.9 us (2%)
    dot_general x77, matrix products, matmul(): return jnp.dot(left, right, preferred_element_type=jnp.float32)  142 us
    all_gather x2, waiting for transfers between devices, gather_rows(): lax.all_gather(jnp.concatenate(parts, axis=1), 'row', axis=0, tiled=True)  124 us
    concatenate x1, local copies, waits for them, and re-layouts, scatter_rows(): jnp.concatenate(columns, axis=1)  93.2 us
    unnamed x10, waiting for transfers between devices  90.2 us
    psum x1, waiting for transfers between devices, body(): normed_grad_two = lax.psum(normed_terms_two, 'col')  82.5 us
    psum x1, waiting for transfers between devices, body(): attn_full = lax.psum(attn_terms, 'col')  67.8 us
    unnamed x82, local copies, waits for them, and re-layouts  51.5 us
    all_gather x1, waiting for transfers between devices, body(): lax.all_gather(arrived_rows[placing], 'col', axis=1, tiled=True)  26.6 us
  transfers between devices with their start and end apart: 13, of which 12 were waited for; matrix products, arithmetic and copies ran while one was open for 22% of the time, Pallas kernels for 0%

profile of v1, /device:TPU:0, one launch (start us, length us, event | category | flops | bytes accessed | tf_op | source)
XLA Modules:
  0.0 914.2 jit_solution(13303859457156370730)
XLA Ops:
  7.2 4.5 sort.45
  12.3 3.6 gather_fusion.1
  16.6 8.4 all-to-all-start.1
  25.0 2.6 gather_fusion
  27.7 4.6 all-to-all-done.1
  32.3 3.9 all-to-all-start
  37.5 3.8 sort.46
  41.3 6.6 all-to-all-done
  48.0 2.6 gather_fusion.2
  52.7 26.6 %all-gather.11.cloned.1.call-done = bf16[512,2048]{1,0:T(8,128)(2,1)} async-done(((bf16[512,512]{1,0:T(8,128)(2,1)}), bf16[512,2048]{1,0:T(8,128)(2,1)}) %all-gather.11.cloned.1.call-update) | async-done | bytes 2097168 | tf_op jit(solution)/shard_map/all_gather | solution.py:154
  79.3 2.1 fusion.54
  81.4 47.8 %all-gather.7.cloned.1.call-done = bf16[2048,1152]{1,0:T(8,128)(2,1)} async-done(((bf16[64,1152]{1,0:T(8,128)(2,1)}), bf16[2048,1152]{1,0:T(8,128)(2,1)}) %all-gather.7.cloned.1.call-update) | async-done | bytes 4718608 | tf_op jit(solution)/shard_map/all_gather | solution.py:102
  129.2 3.6 fusion.67
  134.5 1.9 convolution_bitcast_fusion.2
  136.8 2.0 fusion.72
  139.0 25.1 %while.32 = (s32[]{:T(128)}, bf16[8,512,64]{1,2,0:T(8,128)(2,1)S(1)}, f32[8,512]{1,0:T(8,128)}, bf16[8,512,64]{2,1,0:T(8,128)(2,1)}, bf16[1,512,64]{2,1,0:T(8,12...) while((s32[]{:T(128)}, bf16[8,512,64]{1,2,0:T(8,128)(2,1)S(1)}, ...), condition=%wide.region_8.9_spmd.clone.clone, body=%wide.region_5.8_spmd.clone.sunk.clone | while | flops 69991936 | bytes 3694689 | solution.py:181
  164.9 5.0 fusion.63
  170.9 2.0 gather_fusion.5
  172.8 16.8 %all_to_all.60 = bf16[32,16,512]{2,1,0:T(8,128)(2,1)S(1)} all-to-all(bf16[32,16,512]{2,1,0:T(8,128)(2,1)S(1)} %bitcast.184), channel_id=1, replica_groups=mesh['row'=32,'col'=4] {'row'}, dimensions={0} | all-to-all | bytes 1048576 | tf_op jit(solution)/shard_map/all_to_all | solution.py:149
  189.6 2.6 gather_fusion.6
  194.2 67.8 %all-reduce.4.cloned.1.call-done = f32[512,2048]{1,0:T(8,128)} async-done(((f32[512,2048]{1,0:T(8,128)}), f32[512,2048]{1,0:T(8,128)}) %all-reduce.4.cloned.1.call-update) | async-done | bytes 4194320 | tf_op jit(solution)/shard_map/psum | solution.py:197
  262.0 2.8 multiply_reduce_fusion.4
  264.8 2.0 copy-done.2
  268.6 26.3 %all-gather.13.cloned.1.call-done = bf16[512,2048]{1,0:T(8,128)(2,1)} async-done(((bf16[512,512]{1,0:T(8,128)(2,1)}), bf16[512,2048]{1,0:T(8,128)(2,1)}) %all-gather.13.cloned.1.call-update) | async-done | bytes 2097168 | tf_op jit(solution)/shard_map/all_gather | solution.py:155
  294.9 76.3 %all-gather.9.cloned.1.call-done = bf16[2048,4224]{1,0:T(8,128)(2,1)} async-done(((bf16[64,4224]{1,0:T(8,128)(2,1)}), bf16[2048,4224]{1,0:T(8,128)(2,1)}) %all-gather.9.cloned.1.call-update) | async-done | bytes 17301520 | tf_op jit(solution)/shard_map/all_gather | solution.py:102
  371.2 6.5 fusion.41
  377.8 2.3 copy-done.31
  380.1 5.0 fusion.47
  385.1 7.3 multiply_convert_fusion.4
  392.4 5.4 fusion.45
  397.8 5.0 fusion.55
  402.8 9.7 %all-reduce.8.cloned.1.call-start = ((), (), s32[]{:S(2)}) async-start(), calls=%async_computation.12 | async-start | bytes 4194304 | tf_op jit(solution)/shard_map/psum | solution.py:256
  412.6 82.5 %all-reduce.6.cloned.1.call-done = f32[512,2048]{1,0:T(8,128)} async-done(((f32[512,2048]{1,0:T(8,128)}), f32[512,2048]{1,0:T(8,128)}) %all-reduce.6.cloned.1.call-update) | async-done | bytes 4194320 | tf_op jit(solution)/shard_map/psum | solution.py:220
  495.1 4.6 multiply_reduce_fusion.1
  501.0 2.7 multiply_add_fusion
  503.7 1.9 copy-done.7
  505.6 3.7 fusion.69
  510.9 50.9 %while.33 = (s32[]{:T(128)}, f32[8,512,64]{1,2,0:T(8,128)}, f32[8,512,64]{1,2,0:T(8,128)}, f32[8,512,64]{1,2,0:T(8,128)}, bf16[8,512,64]{2,1,0:T(8,128)(2,1)}, /...) while((s32[]{:T(128)}, f32[8,512,64]{1,2,0:T(8,128)}, ...), condition=%wide.region_17.18_spmd.clone.clone, body=%wide.region_15.17_spmd.clone.sunk.clone | while | flops 170982912 | bytes 9126013 | solution.py:227
  539.9 1.9 fusion.176
  566.8 2.9 fusion.65
  571.5 3.2 add_convert_fusion
  574.7 7.9 fusion.58
  582.7 7.9 convolution_convert_fusion.2
  590.6 5.3 convolution_convert_fusion.1
  595.9 5.0 convolution_convert_fusion
  602.6 2.7 convolution_convert_fusion.4
  605.3 2.6 convolution_convert_fusion.3
  607.9 25.5 %all-reduce.8.cloned.1.call-done = bf16[512,2048]{1,0:T(8,128)(2,1)} async-done(((bf16[512,2048]{1,0:T(8,128)(2,1)}), bf16[512,2048]{1,0:T(8,128)(2,1)}) %all-reduce.8.cloned.1.call-update) | async-done | bytes 2097168 | tf_op jit(solution)/shard_map/psum | solution.py:256
  633.3 6.1 fusion.53
  639.5 93.2 %concatenate.53 = bf16[2048,5378]{0,1:T(8,128)(2,1)} concatenate(bf16[2048,512]{0,1:T(8,128)(2,1)} %convolution_convert_fusion.4, bf16[2048,64]{0,1:T(8,128)(2,1)S(1)} %convolution_convert_fusion.6, bf16[2048,64]{0,1:T(8,128)(2,1)S(1)} %convolution_convert_fusion.5, bf16[2048,512]{0,1:T(8,128)(2,1)} %convolution_convert_fusion.3, bf16[2048,1408]{0,1:T(8,128)(2,1)} %convolution_convert_fusion.2, ...), dimensions={1} | concatenate | bytes 44056576 | tf_op jit(solution)/shard_map/concatenate | solution.py:115
  732.7 28.4 %copy.67 = bf16[2048,5378]{1,0:T(8,128)(2,1)} copy(bf16[2048,5378]{0,1:T(8,128)(2,1)} %concatenate.53) | data formatting | bytes 44056576
  763.5 2.6 gather_fusion.3
  766.1 7.3 all-to-all-start.2
  773.4 2.5 fusion.73
  775.9 2.6 gather_fusion.7
  778.6 6.6 all-to-all-done.2
  785.2 4.1 all-to-all-start.4
  789.3 3.8 sort.47
  793.1 2.6 gather_fusion.4
  795.8 5.3 all-to-all-done.4
  801.1 2.6 gather_fusion.8
  803.7 90.1 %reduce-scatter.7.cloned.1.call-done = bf16[64,5378]{1,0:T(8,128)(2,1)} async-done(((bf16[2048,5378]{1,0:T(8,128)(2,1)}), bf16[64,5378]{1,0:T(8,128)(2,1)}) %reduce-scatter.7.cloned.1.call-update) | async-done | bytes 688400
  893.8 2.0 copy.68
  903.2 2.1 copy.64
  (248 shorter events, 109.3 us)
Async XLA Ops:
  7.2 17.9 %copy-start = (bf16[512,512]{1,0:T(8,128)(2,1)S(1)}, bf16[512,512]{1,0:T(8,128)(2,1)}, u32[]{:S(2)}) copy-start(bf16[512,512]{1,0:T(8,128)(2,1)} %param.17) | copy-start | bytes 1572868
  11.7 0.6 copy-start.28
  16.6 15.7 %all-to-all-start.1 = ((s32[32,16,1]{1,2,0:T(1,128)}), s32[32,16,1]{1,2,0:T(1,128)S(1)}, u32[]{:S(2)}, u32[]{:S(2)}) async-start(s32[32,16,1]{1,2,0:T(1,128)} %bitcast.2), calls=%async_computation.1 | async-start | bytes 32768 | tf_op jit(solution)/shard_map/all_to_all | solution.py:150
  27.7 23.0 %copy-start.19 = (bf16[64,512]{1,0:T(8,128)(2,1)S(1)}, bf16[64,512]{1,0:T(8,128)(2,1)}, u32[]{:S(2)}) copy-start(bf16[64,512]{1,0:T(8,128)(2,1)} %param.22) | copy-start | bytes 196612
  27.7 23.0 %copy-start.20 = (bf16[64,512]{1,0:T(8,128)(2,1)S(1)}, bf16[64,512]{1,0:T(8,128)(2,1)}, u32[]{:S(2)}) copy-start(bf16[64,512]{1,0:T(8,128)(2,1)} %param.25) | copy-start | bytes 196612
  27.7 23.0 %copy-start.21 = (bf16[64,64]{1,0:T(8,128)(2,1)S(1)}, bf16[64,64]{1,0:T(8,128)(2,1)}, u32[]{:S(2)}) copy-start(bf16[64,64]{1,0:T(8,128)(2,1)} %param.23) | copy-start | bytes 24580
  27.7 23.0 %copy-start.22 = (bf16[64,64]{1,0:T(8,128)(2,1)S(1)}, bf16[64,64]{1,0:T(8,128)(2,1)}, u32[]{:S(2)}) copy-start(bf16[64,64]{1,0:T(8,128)(2,1)} %param.24) | copy-start | bytes 24580
  27.7 23.9 %copy-start.25 = (s32[512]{0:T(512)S(1)}, s32[512]{0:T(512)}, u32[]{:S(2)}) copy-start(s32[512]{0:T(512)} %param.20) | copy-start | bytes 6148
  32.3 49.0 %copy-start.16 = (s32[32,16,1]{1,2,0:T(1,128)}, s32[32,16,1]{1,2,0:T(1,128)S(1)}, u32[]{:S(2)}) copy-start(s32[32,16,1]{1,2,0:T(1,128)S(1)} %all-to-all-done.1) | copy-start | bytes 6148
  32.3 15.7 %all-to-all-start = ((bf16[32,16,512]{2,1,0:T(8,128)(2,1)}), bf16[32,16,512]{2,1,0:T(8,128)(2,1)S(1)}, u32[]{:S(2)}, u32[]{:S(2)}) async-start(bf16[32,16,512]{2,1,0:T(8,128)(2,1)} %bitcast), calls=%async_computation | async-start | bytes 1048576 | tf_op jit(solution)/shard_map/all_to_all | solution.py:148
  36.2 43.1 %all-gather.11.cloned.1.call-start = ((), (), s32[]{:S(2)}) async-start(), calls=%async_computation.13 | async-start | bytes 2621440 | tf_op jit(solution)/shard_map/all_gather | solution.py:154
  48.0 81.2 %copy-start.23 = (f32[2048]{0:T(1024)S(1)}, f32[2048]{0:T(1024)}, u32[]{:S(2)}) copy-start(f32[2048]{0:T(1024)} %param.21) | copy-start | bytes 24580
  50.6 78.6 %all-gather.7.cloned.1.call-start = ((), (), s32[]{:S(2)}) async-start(), calls=%async_computation.7 | async-start | bytes 4866048 | tf_op jit(solution)/shard_map/all_gather | solution.py:102
  51.5 210.5 %all-reduce.4.cloned.1.call-start = ((), (), s32[]{:S(2)}) async-start(), calls=%async_computation.8 | async-start | bytes 8388608 | tf_op jit(solution)/shard_map/psum | solution.py:197
  52.1 84.2 %copy-start.30 = (f32[32]{0:T(128)}, f32[32]{0:T(128)S(1)}, u32[]{:S(2)}) copy-start(f32[32]{0:T(128)S(1)} %negate_power_fusion) | copy-start | bytes 388
  132.8 1.7 copy-start.5
  134.5 4.5 copy-start.26
  164.1 0.8 copy-start.9
  169.8 1.0 copy-start.4
  169.9 125.1 %all-gather.13.cloned.1.call-start = ((), (), s32[]{:S(2)}) async-start(), calls=%async_computation.14 | async-start | bytes 2621440 | tf_op jit(solution)/shard_map/all_gather | solution.py:155
  189.6 2.7 copy-start.14
  189.6 2.7 copy-start.15
  192.3 178.9 %all-gather.9.cloned.1.call-start = ((), (), s32[]{:S(2)}) async-start(), calls=%async_computation.9 | async-start | bytes 17842176 | tf_op jit(solution)/shard_map/all_gather | solution.py:102
  194.2 72.7 %copy-start.18 = (f32[2048]{0:T(1024)S(1)}, f32[2048]{0:T(1024)}, u32[]{:S(2)}) copy-start(f32[2048]{0:T(1024)} %param.26) | copy-start | bytes 24580
  194.2 300.9 %all-reduce.6.cloned.1.call-start = ((), (), s32[]{:S(2)}) async-start(), calls=%async_computation.11 | async-start | bytes 8388608 | tf_op jit(solution)/shard_map/psum | solution.py:220
  264.8 2.1 copy-start.2
  371.2 6.6 copy-start.11
  371.2 8.9 copy-start.31
  392.4 5.4 copy-start.32
  402.8 230.5 %all-reduce.8.cloned.1.call-start = ((), (), s32[]{:S(2)}) async-start(), calls=%async_computation.12 | async-start | bytes 4194304 | tf_op jit(solution)/shard_map/psum | solution.py:256
  495.1 4.6 copy-start.3
  495.1 5.9 copy-start.6
  503.7 1.9 copy-start.7
  505.6 5.2 copy-start.27
  574.7 187.2 %reduce-scatter.5.cloned.1.call-start = ((), (), s32[]{:S(2)}) async-start(), calls=%async_computation.10 | async-start | bytes 2621440 | tf_op jit(solution)/shard_map/reduce_scatter | solution.py:207
  582.6 311.1 %reduce-scatter.7.cloned.1.call-start = ((), (), s32[]{:S(2)}) async-start(), calls=%async_computation.15 | async-start | bytes 23248896
  582.7 7.9 copy-start.12
  582.7 7.9 copy-start.34
  590.6 5.3 copy-start.13
  590.6 5.3 copy-start.33
  595.9 5.0 copy-start.24
  602.5 2.8 copy-start.8
  602.5 2.7 copy-start.10
  761.1 0.7 copy-start.17
  766.1 19.0 %all-to-all-start.2 = ((bf16[32,16,512]{2,1,0:T(8,128)(2,1)}), bf16[32,16,512]{2,1,0:T(8,128)(2,1)S(1)}, u32[]{:S(2)}, u32[]{:S(2)}) async-start(bf16[32,16,512]{2,1,0:T(8,128)(2,1)} %bitcast.14), calls=%async_computation.3 | async-start | bytes 1048576 | tf_op jit(solution)/shard_map/all_to_all | solution.py:284
  773.4 15.9 %copy-start.29 = (s32[512]{0:T(512)S(1)}, s32[512]{0:T(512)}, u32[]{:S(2)}) copy-start(s32[512]{0:T(512)} %copy-done.28) | copy-start | bytes 6148
  785.2 15.9 %all-to-all-start.4 = ((bf16[32,16,512]{2,1,0:T(8,128)(2,1)}), bf16[32,16,512]{2,1,0:T(8,128)(2,1)S(1)}, u32[]{:S(2)}, u32[]{:S(2)}) async-start(bf16[32,16,512]{2,1,0:T(8,128)(2,1)} %bitcast.24), calls=%async_computation.5 | async-start | bytes 1048576 | tf_op jit(solution)/shard_map/all_to_all | solution.py:285
  896.8 10.4 %copy-start.1 = (bf16[512,512]{1,0:T(8,128)(2,1)S(1)}, bf16[512,512]{1,0:T(8,128)(2,1)}, u32[]{:S(2)}) copy-start(bf16[512,512]{1,0:T(8,128)(2,1)} %param.17) | copy-start | bytes 1572868
Sparse Core Ops, SparseCore 0:
  50.7 28.4 all-gather.10
  82.1 47.0 all-gather.6
  170.0 91.9 all-reduce.3
  264.2 30.6 all-gather.12
  297.3 73.9 all-gather.8
  402.9 92.1 all-reduce.5
  574.8 58.4 all-reduce.7
  635.9 29.4 reduce-scatter.4
  761.3 132.4 reduce-scatter.6

commit v2 on v1

--- a/solution.py
+++ b/solution.py
@@ -3,6 +3,8 @@
 import jax
 import jax.numpy as jnp
 from jax import lax
+from jax.experimental import pallas as pl
+from jax.experimental.pallas import tpu as pltpu
 from jax.sharding import PartitionSpec as P
 
 HEADS = 32
@@ -97,9 +99,10 @@
     return (query_grad, key_grad, value_grad)
 
 
-def gather_rows(parts):
-    widths = [part.shape[1] for part in parts]
-    packed = lax.all_gather(jnp.concatenate(parts, axis=1), "row", axis=0, tiled=True)
+GRAD_BLOCK = 128
+
+
+def split_columns(packed, widths):
     pieces = []
     offset = 0
     for width in widths:
@@ -108,19 +111,54 @@
     return pieces
 
 
-def scatter_rows(parts):
-    columns = [part.reshape(part.shape[0], -1).astype(jnp.bfloat16) for part in parts]
-    widths = [column.shape[1] for column in columns]
-    packed = lax.psum_scatter(
-        jnp.concatenate(columns, axis=1), "row", scatter_dimension=0, tiled=True
-    ).astype(jnp.float32)
-    pieces = []
-    offset = 0
-    for part, width in zip(parts, widths):
-        piece = packed[:, offset : offset + width]
-        pieces.append(piece.reshape(-1) if part.ndim == 1 else piece)
-        offset += width
-    return pieces
+def gather_rows(parts):
+    return lax.all_gather(jnp.concatenate(parts, axis=1), "row", axis=0, tiled=True)
+
+
+def grad_block_kernel(select_ref, left_ref, right_ref, tail_ref, out_ref):
+    step = pl.program_id(0)
+    last = pl.num_programs(0) - 1
+
+    @pl.when(step < last)
+    def _():
+        out_ref[...] = jnp.dot(
+            left_ref[0], right_ref[...], preferred_element_type=jnp.float32
+        ).astype(out_ref.dtype)
+
+    @pl.when(step == last)
+    def _():
+        out_ref[...] = tail_ref[...]
+
+
+def packed_weight_grads(lefts, segments, tail):
+    left_stack = jnp.stack([left.T for left in lefts])
+    right = jnp.concatenate([seg for _, seg in segments], axis=1)
+    column_owner = []
+    for index, seg in segments:
+        column_owner += [index] * seg.shape[1]
+    assert len(column_owner) % GRAD_BLOCK == 0
+    select = column_owner[::GRAD_BLOCK]
+    assert column_owner == [owner for owner in select for _ in range(GRAD_BLOCK)]
+    right_blocks = len(select)
+    select.append(select[-1])
+    features, tokens = left_stack.shape[1], left_stack.shape[2]
+    total = right.shape[1] + GRAD_BLOCK
+    return pl.pallas_call(
+        grad_block_kernel,
+        out_shape=jax.ShapeDtypeStruct((features, total), jnp.bfloat16),
+        grid_spec=pltpu.PrefetchScalarGridSpec(
+            num_scalar_prefetch=1,
+            grid=(len(select),),
+            in_specs=[
+                pl.BlockSpec((1, features, tokens), lambda j, sel: (sel[j], 0, 0)),
+                pl.BlockSpec(
+                    (tokens, GRAD_BLOCK), lambda j, sel: (0, jnp.minimum(j, right_blocks - 1))
+                ),
+                pl.BlockSpec((features, GRAD_BLOCK), lambda j, sel: (0, 0)),
+            ],
+            out_specs=pl.BlockSpec((features, GRAD_BLOCK), lambda j, sel: (0, j)),
+        ),
+    )(jnp.asarray(select, dtype=jnp.int32), left_stack, right, tail)
 
 
 def body(
@@ -144,17 +182,20 @@
     group_size = HEADS // KV
     send_order = jnp.argsort(destination)
     slot_ids = destination[send_order] % row_count
-    arrived_rows, arrived_grads, arrived_slots = (
-        lax.all_to_all(tokens[send_order], "row", split_axis=0, concat_axis=0, tiled=True),
-        lax.all_to_all(cotangent[send_order], "row", split_axis=0, concat_axis=0, tiled=True),
+    arrived_pair, arrived_slots = (
+        lax.all_to_all(
+            jnp.stack([tokens, cotangent])[:, send_order], "row", split_axis=1, concat_axis=1, tiled=True
+        ),
         lax.all_to_all(slot_ids, "row", split_axis=0, concat_axis=0, tiled=True),
     )
     placing = jnp.argsort(arrived_slots)
-    full_rows, full_grads = (
-        lax.all_gather(arrived_rows[placing], "col", axis=1, tiled=True),
-        lax.all_gather(arrived_grads[placing], "col", axis=1, tiled=True),
-    )
-    query_w, key_w, value_w, output_w = gather_rows([w_query, w_key, w_value, w_output])
+    full_pair = lax.all_gather(arrived_pair[:, placing], "col", axis=2, tiled=True)
+    full_rows, full_grads = full_pair[0], full_pair[1]
+    attn_widths = [w_query.shape[1], w_key.shape[1], w_value.shape[1], w_output.shape[1]]
+    ffn_widths = [w_gate.shape[1], w_up.shape[1], w_down.shape[1]]
+    attn_packed = gather_rows([w_query, w_key, w_value, w_output])
+    ffn_packed = gather_rows([w_gate, w_up, w_down])
+    query_w, key_w, value_w, output_w = split_columns(attn_packed, attn_widths)
     cosine, sine = rope_tables(positions_of(segment_ids))
     allowed = allowed_pairs(segment_ids)
     rows_wide = full_rows.astype(jnp.float32)
@@ -194,12 +235,13 @@
         .astype(jnp.bfloat16)
     )
     attn_terms = matmul(mixed, output_w.T)
+    attn_terms, ffn_packed = lax.optimization_barrier((attn_terms, ffn_packed))
     attn_full = lax.psum(attn_terms, "col")
     resid = rows_wide + attn_full
     inv_two = rms_scale(resid)
     normed_two = (resid * inv_two * ffn_gain).astype(jnp.bfloat16)
     resid_part = lax.dynamic_slice_in_dim(resid, col_start, quarter, 1)
-    gate_w, up_w, down_w = gather_rows([w_gate, w_up, w_down])
+    gate_w, up_w, down_w = split_columns(ffn_packed, ffn_widths)
     gate = matmul(normed_two, gate_w)
     upper = matmul(normed_two, up_w)
     sigmoid_gate = jax.nn.sigmoid(gate)
@@ -208,20 +250,16 @@
         matmul(activ, down_w.T).astype(jnp.bfloat16), "col", scatter_dimension=1, tiled=True
     ).astype(jnp.float32)
     output_share = (resid_part + ffn_share).astype(jnp.bfloat16)
-    down_weight_grad = matmul(full_grads.T, activ)
     act_grad = matmul(full_grads, down_w)
     gate_grad = (act_grad * upper * sigmoid_gate * (1.0 + gate * (1.0 - sigmoid_gate))).astype(
         jnp.bfloat16
     )
     up_grad = (act_grad * gate * sigmoid_gate).astype(jnp.bfloat16)
-    gate_weight_grad = matmul(normed_two.T, gate_grad)
-    up_weight_grad = matmul(normed_two.T, up_grad)
     normed_terms_two = matmul(gate_grad, gate_w.T) + matmul(up_grad, up_w.T)
     normed_grad_two = lax.psum(normed_terms_two, "col")
     resid_norm_grad, ffn_gain_grad = norm_back(resid, inv_two, ffn_gain, normed_grad_two)
     resid_grad = full_grads.astype(jnp.float32) + resid_norm_grad
     attn_grad_low = resid_grad.astype(jnp.bfloat16)
-    output_weight_grad = matmul(attn_grad_low.T, mixed)
     mixed_grad = matmul(attn_grad_low, output_w).astype(jnp.bfloat16)
     mixed_grad_heads = mixed_grad.reshape(row_count, query_heads_count, HD).transpose(1, 0, 2)
     query_grads, key_grads, value_grads = lax.map(
@@ -247,9 +285,6 @@
         value_grads.reshape(kv_count, group_size, row_count, HD).sum(axis=1).transpose(1, 0, 2)
     )
     value_grad = value_sum.reshape(row_count, kv_count * HD).astype(jnp.bfloat16)
-    query_weight_grad = matmul(normed_one.T, query_grad)
-    key_weight_grad = matmul(normed_one.T, key_grad)
-    value_weight_grad = matmul(normed_one.T, value_grad)
     normed_terms_one = (
         matmul(query_grad, query_w.T) + matmul(key_grad, key_w.T) + matmul(value_grad, value_w.T)
     )
@@ -257,6 +292,30 @@
     rows_norm_grad, attn_gain_grad = norm_back(rows_wide, inv_one, attn_gain, normed_grad_one)
     rows_grad = resid_grad + rows_norm_grad
     input_share = lax.dynamic_slice_in_dim(rows_grad, col_start, quarter, 1).astype(jnp.bfloat16)
+    gain_tail = jnp.concatenate(
+        [
+            attn_gain_grad[:, None],
+            ffn_gain_grad[:, None],
+            jnp.zeros((attn_gain_grad.shape[0], GRAD_BLOCK - 2), jnp.float32),
+        ],
+        axis=1,
+    ).astype(jnp.bfloat16)
+    grads_packed = packed_weight_grads(
+        [normed_one, attn_grad_low, normed_two, full_grads],
+        [
+            (0, query_grad),
+            (0, key_grad),
+            (0, value_grad),
+            (1, mixed),
+            (2, gate_grad),
+            (2, up_grad),
+            (3, activ),
+        ],
+        gain_tail,
+    )
+    grads_local = lax.psum_scatter(grads_packed, "row", scatter_dimension=0, tiled=True).astype(
+        jnp.float32
+    )
     (
         query_result,
         key_result,
@@ -267,23 +326,17 @@
         down_result,
         attn_gain_result,
         ffn_gain_result,
-    ) = scatter_rows(
-        [
-            query_weight_grad,
-            key_weight_grad,
-            value_weight_grad,
-            output_weight_grad,
-            gate_weight_grad,
-            up_weight_grad,
-            down_weight_grad,
-            attn_gain_grad,
-            ffn_gain_grad,
-        ]
-    )
-    back_rows, back_grads = (
-        lax.all_to_all(output_share[arrived_slots], "row", split_axis=0, concat_axis=0, tiled=True),
-        lax.all_to_all(input_share[arrived_slots], "row", split_axis=0, concat_axis=0, tiled=True),
-    )
+    ) = split_columns(grads_local, attn_widths + ffn_widths + [1, 1])
+    attn_gain_result = attn_gain_result.reshape(-1)
+    ffn_gain_result = ffn_gain_result.reshape(-1)
+    back_pair = lax.all_to_all(
+        jnp.stack([output_share, input_share])[:, arrived_slots],
+        "row",
+        split_axis=1,
+        concat_axis=1,
+        tiled=True,
+    )
+    back_rows, back_grads = back_pair[0], back_pair[1]
     restore = jnp.argsort(send_order)
     return (
         back_rows[restore],

time: 928 us -> 831 us (0.90)
  local copies, waits for them, and re-layouts: 191 us -> 83.9 us
  Pallas kernels: 0 us -> 43.9 us
  blocking collectives: 16.8 us -> 0 us
  other arithmetic: 49.6 us -> 63.6 us
  waiting for transfers between devices: 466 us -> 453 us
  starting transfers between devices: 34 us -> 24.7 us
    reduce_scatter x0 -> x1, waiting for transfers between devices: none -> 92.1 us  [body(): lax.psum_scatter(grads_packed, 'row', scatter_dimension=0, tiled=True)]
    unnamed x10 -> x8, waiting for transfers between devices: 90.2 us -> 0.13 us
    concatenate x1 -> x2, local copies, waits for them, and re-layouts: 93.2 us -> 8.95 us  [the longest x1 8.88 us: packed_weight_grads(): right = jnp.concatenate([seg for _, seg in segments], axis=1)]
    unnamed x82 -> x71, local copies, waits for them, and re-layouts: 51.5 us -> 4.56 us
    pallas_call x0 -> x1, Pallas kernels: none -> 43.9 us  [packed_weight_grads(): pl.pallas_call(grad_block_kernel, out_shape=jax.ShapeDtypeStruct((feature...]
    all_gather x2, waiting for transfers between devices: 124 us -> 84.6 us  [gather_rows(): lax.all_gather(jnp.concatenate(parts, axis=1), 'row', axis=0, tiled=True)]
    another operation x8 -> x15, other arithmetic: 2.85 us -> 21.1 us  [the longest x3 10.8 us: packed_weight_grads(): left_stack = jnp.stack([left.T for left in lefts])]
    all_to_all x1 -> x0, blocking collectives: 16.8 us -> none  [body(): lax.all_to_all(cotangent[send_order], 'row', split_axis=0, concat_axis=0,...]
  transfers between devices with their start and end apart: 13 -> 11, of which waited for: 12 -> 9; matrix products, arithmetic and copies ran while one was open for 22% -> 15% of each run, Pallas kernels for 0% -> 5%
where the time goes in v2:
time: 831 us; the launch traced here: 820 us
  waiting for transfers between devices  453 us (55%)
  matrix products  135 us (16%)
  local copies, waits for them, and re-layouts  83.9 us (10%)
  other arithmetic  63.6 us (8%)
  Pallas kernels  43.9 us (5%)
  starting transfers between devices  24.7 us (3%)
  between operations  15.3 us (2%)
    dot_general x70, matrix products, matmul(): return jnp.dot(left, right, preferred_element_type=jnp.float32)  135 us
    psum x1, waiting for transfers between devices, body(): normed_grad_two = lax.psum(normed_terms_two, 'col')  92.5 us
    reduce_scatter x1, waiting for transfers between devices, body(): lax.psum_scatter(grads_packed, 'row', scatter_dimension=0, tiled=True)  92.1 us
    all_gather x2, waiting for transfers between devices, gather_rows(): lax.all_gather(jnp.concatenate(parts, axis=1), 'row', axis=0, tiled=True)  84.6 us
    psum x1, waiting for transfers between devices, body(): attn_full = lax.psum(attn_terms, 'col')  83.7 us
    pallas_call x1, Pallas kernels, packed_weight_grads(): pl.pallas_call(grad_block_kernel, out_shape=jax.ShapeDtypeStruct((feature...  43.9 us
    all_gather x1, waiting for transfers between devices, body(): lax.all_gather(arrived_pair[:, placing], 'col', axis=2, tiled=True)  42.6 us
    psum x1, waiting for transfers between devices, body(): lax.psum(normed_terms_one.astype(jnp.bfloat16), 'col').astype(jnp.float32)  31.8 us
  transfers between devices with their start and end apart: 11, of which 9 were waited for; matrix products, arithmetic and copies ran while one was open for 15% of the time, Pallas kernels for 5%

profile of v2, /device:TPU:0, one launch (start us, length us, event | category | flops | bytes accessed | tf_op | source)
XLA Modules:
  0.0 819.8 jit_solution(6570279956710814497)
XLA Ops:
  7.2 4.4 sort.45
  12.2 3.6 gather_fusion.1
  16.5 8.4 %all-to-all-start.1 = ((s32[32,16,1]{1,2,0:T(1,128)}), s32[32,16,1]{1,2,0:T(1,128)S(1)}, u32[]{:S(2)}, u32[]{:S(2)}) async-start(s32[32,16,1]{1,2,0:T(1,128)} %bitcast.3), calls=%async_computation.1 | async-start | bytes 32768 | tf_op jit(solution)/shard_map/all_to_all | solution.py:189
  25.0 1.9 copy.114
  26.8 1.9 copy.115
  28.7 2.4 pad_maximum_fusion.1
  31.1 4.1 gather_fusion
  35.3 7.5 all-to-all-start
  44.2 3.8 sort.46
  48.0 12.2 %all-to-all-done = bf16[2,512,512]{2,0,1:T(2,128)(2,1)S(1)} async-done(((bf16[2,512,512]{2,0,1:T(2,128)(2,1)}), bf16[2,512,512]{2,0,1:T(2,128)(2,1)S(1)}, u32[]{:S(2)}, u32[]{:S(2)}) %all-to-all-start) | async-done | bytes 1048608 | tf_op jit(solution)/shard_map/all_to_all | solution.py:186
  60.2 3.6 gather_fusion.2
  63.7 2.5 copy.117
  69.7 42.6 %all-gather.9.cloned.1.call-done = bf16[2,512,2048]{1,2,0:T(8,128)(2,1)} async-done(((bf16[2,512,512]{1,2,0:T(8,128)(2,1)}), bf16[2,512,2048]{1,2,0:T(8,128)(2,1)}) %all-gather.9.cloned.1.call-update) | async-done | bytes 4194320 | tf_op jit(solution)/shard_map/all_gather | solution.py:192
  112.3 2.1 fusion.57
  114.4 48.1 %all-gather.5.cloned.1.call-done = bf16[2048,1152]{1,0:T(8,128)(2,1)} async-done(((bf16[64,1152]{1,0:T(8,128)(2,1)}), bf16[2048,1152]{1,0:T(8,128)(2,1)}) %all-gather.5.cloned.1.call-update) | async-done | bytes 4718608 | tf_op jit(solution)/shard_map/all_gather | solution.py:115
  162.5 2.7 fusion.81
  167.1 2.5 copy.118
  169.5 3.6 fusion.67
  173.8 2.9 convolution_bitcast_fusion.2
  178.1 17.9 %while.32 = (s32[]{:T(128)}, bf16[8,512,64]{1,2,0:T(8,128)(2,1)S(1)}, f32[8,512]{1,0:T(8,128)}, bf16[8,512,64]{2,1,0:T(8,128)(2,1)S(1)}, bf16[1,512,64]{2,1,0:T(...) while((s32[]{:T(128)}, bf16[8,512,64]{1,2,0:T(8,128)(2,1)S(1)}, ...), condition=%wide.region_8.9_spmd.clone.clone, body=%wide.region_5.8_spmd.clone.sunk.clone | while | flops 69991936 | bytes 3694689 | solution.py:222
  196.0 5.4 fusion.74
  201.4 36.5 %all-gather.7.cloned.1.call-done = bf16[2048,4224]{1,0:T(8,128)(2,1)} async-done(((bf16[64,4224]{1,0:T(8,128)(2,1)}), bf16[2048,4224]{1,0:T(8,128)(2,1)}) %all-gather.7.cloned.1.call-update) | async-done | bytes 17301520 | tf_op jit(solution)/shard_map/all_gather | solution.py:115
  237.9 5.4 copy.124
  243.6 8.3 %fusion.44 = f32[512,1408]{1,0:T(8,128)} fusion(bf16[2048,4224]{1,0:T(8,128)(2,1)} %all-gather.7.cloned.1.call-done, bf16[2,512,2048]{1,2,0:T(8,128)(2,1)} %all-gather.9.cloned.1.call-done), kind=kOutput, calls=%fused_computation.67 | convolution fusion | flops 2952790016 | bytes 10747904 | tf_op jit(solution)/shard_map/dot_general | solution.py:68
  251.9 83.7 %all-reduce.4.cloned.1.call-done = f32[512,2048]{0,1:T(8,128)} async-done(((f32[512,2048]{0,1:T(8,128)}), f32[512,2048]{0,1:T(8,128)}) %all-reduce.4.cloned.1.call-update) | async-done | bytes 4194320 | tf_op jit(solution)/shard_map/psum | solution.py:239
  335.7 3.6 multiply_reduce_fusion.4
  339.3 7.5 fusion.54
  346.9 8.9 %multiply_convert_fusion.5 = (bf16[512,1408]{1,0:T(8,128)(2,1)}, bf16[512,1408]{1,0:T(8,128)(2,1)S(1)}, bf16[512,1408]{1,0:T(8,128)(2,1)S(1)}) fusion(f32[512,1408]{1,0:T(8,128)S(1)} %fusion.54, f32[512,1408]{1,0:T(8,128)S(1)} %copy-done.33, bf16[2048,4224]{1,0:T(8,128)(2,1)} %all-gather.7.cloned.1.call-done, f32[512,2048]{0,1:T(8,128)S(1)} %get-tuple-element.328, ...), kind=kOutput, calls=%fused_computation.95 | convolution fusion | flops 2967470080 | bytes 20064256 | tf_op jit(solution)/shard_map/dot_general | solution.py:68
  355.8 6.5 fusion.48
  362.3 7.9 fusion.60
  370.6 92.5 %all-reduce.6.cloned.1.call-done = f32[512,2048]{0,1:T(8,128)} async-done(((f32[512,2048]{0,1:T(8,128)}), f32[512,2048]{0,1:T(8,128)}) %all-reduce.6.cloned.1.call-update) | async-done | bytes 4194320 | tf_op jit(solution)/shard_map/psum | solution.py:259
  463.1 4.9 multiply_reduce_fusion.1
  469.0 2.8 convert_bitcast_fusion.1
  471.8 2.0 copy-done.5
  473.8 2.9 fusion.78
  478.0 65.3 %while.33 = (s32[]{:T(128)}, f32[8,512,64]{1,2,0:T(8,128)}, f32[8,512,64]{1,2,0:T(8,128)}, f32[8,512,64]{1,2,0:T(8,128)}, bf16[8,512,64]{2,1,0:T(8,128)(2,1)}, /...) while((s32[]{:T(128)}, f32[8,512,64]{1,2,0:T(8,128)}, ...), condition=%wide.region_16.17_spmd.clone.clone, body=%wide.region_14.16_spmd.clone.sunk.clone | while | flops 170982912 | bytes 8994941 | solution.py:265
  481.6 1.9 fusion.181
  483.4 1.8 fusion.180
  489.8 1.8 fusion.181
  506.1 1.9 fusion.181
  514.3 1.9 fusion.181
  522.4 1.8 fusion.181
  530.6 1.8 fusion.181
  532.4 1.8 fusion.180
  538.8 1.8 fusion.181
  546.0 2.2 add_convert_fusion.2
  554.4 4.3 add_convert_fusion
  558.8 7.9 fusion.63
  567.1 3.1 slice_bitcast_fusion.1
  571.2 4.1 fusion.133
  576.7 8.9 %concatenate.57.right_ref = bf16[512,5376]{1,0:T(8,128)(2,1)} concatenate(bf16[512,512]{1,0:T(8,128)(2,1)} %copy.137, bf16[512,64]{1,0:T(8,128)(2,1)S(1)} %maximum_bitcast_fusion.1, bf16[512,64]{1,0:T(8,128)(2,1)S(1)} %copy.134, bf16[512,512]{1,0:T(8,128)(2,1)S(1)} %copy-done.7, bf16[512,1408]{1,0:T(8,128)(2,1)} %copy-done.8, bf16[512,1408]{1,0:T(8,128)(2,1)} %copy-done.9, ...), dimensions={1} | concatenate | bytes 11010048 | tf_op jit(solution)/shard_map/concatenate | solution.py:135
  585.6 31.8 %all-reduce.8.cloned.1.call-done = bf16[512,2048]{0,1:T(8,128)(2,1)} async-done(((bf16[512,2048]{0,1:T(8,128)(2,1)}), bf16[512,2048]{0,1:T(8,128)(2,1)}) %all-reduce.8.cloned.1.call-update) | async-done | bytes 2097168 | tf_op jit(solution)/shard_map/psum | solution.py:291
  617.4 5.9 fusion.56
  624.8 3.9 pad_maximum_fusion.left_ref
  628.7 43.9 %shard_map.221 = bf16[2048,5504]{1,0:T(8,128)(2,1)} custom-call(s32[43]{0:T(128)} %constant.123.clone.select_ref, bf16[4,2048,512]{2,1,0:T(8,128)(2,1)} %pad_maximum_fusion.left_ref, bf16[512,5376]{1,0:T(8,128)(2,1)} %concatenate.57.right_ref, bf16[2048,128]{1,0:T(8,128)(2,1)} %maximum_maximum_fusion.tail_ref), custom_call_target="tpu_custom_call" | custom-call | tf_op jit(solution)/shard_map/pallas_call | solution.py:146
  674.3 2.3 fusion.87
  677.6 4.1 gather_fusion.3
  681.8 7.3 all-to-all-start.2
  689.1 3.8 sort.47
  692.9 13.5 %all-to-all-done.2 = bf16[2,512,512]{2,0,1:T(2,128)(2,1)S(1)} async-done(((bf16[2,512,512]{2,0,1:T(2,128)(2,1)}), bf16[2,512,512]{2,0,1:T(2,128)(2,1)S(1)}, u32[]{:S(2)}, u32[]{:S(2)}) %all-to-all-start.2) | async-done | bytes 1048608 | tf_op jit(solution)/shard_map/all_to_all | solution.py:332
  708.2 2.6 gather_fusion.5
  710.8 2.6 gather_fusion.4
  713.4 92.1 %reduce-scatter.5.cloned.1.call-done = bf16[64,5504]{1,0:T(8,128)(2,1)} async-done(((bf16[2048,5504]{1,0:T(8,128)(2,1)}), bf16[64,5504]{1,0:T(8,128)(2,1)}) %reduce-scatter.5.cloned.1.call-update) | async-done | bytes 704528 | tf_op jit(solution)/shard_map/reduce_scatter | solution.py:316
  810.5 2.1 fusion.118
  (242 shorter events, 101.8 us)
Async XLA Ops:
  11.6 0.6 copy-start.29
  16.5 18.8 %all-to-all-start.1 = ((s32[32,16,1]{1,2,0:T(1,128)}), s32[32,16,1]{1,2,0:T(1,128)S(1)}, u32[]{:S(2)}, u32[]{:S(2)}) async-start(s32[32,16,1]{1,2,0:T(1,128)} %bitcast.3), calls=%async_computation.1 | async-start | bytes 32768 | tf_op jit(solution)/shard_map/all_to_all | solution.py:189
  35.2 31.1 %copy-start.15 = (bf16[64,512]{1,0:T(8,128)(2,1)S(1)}, bf16[64,512]{1,0:T(8,128)(2,1)}, u32[]{:S(2)}) copy-start(bf16[64,512]{1,0:T(8,128)(2,1)} %param.23) | copy-start | bytes 196612
  35.2 31.1 %copy-start.16 = (bf16[64,512]{1,0:T(8,128)(2,1)S(1)}, bf16[64,512]{1,0:T(8,128)(2,1)}, u32[]{:S(2)}) copy-start(bf16[64,512]{1,0:T(8,128)(2,1)} %param.26) | copy-start | bytes 196612
  35.2 31.1 %copy-start.24 = (bf16[64,64]{1,0:T(8,128)(2,1)S(1)}, bf16[64,64]{1,0:T(8,128)(2,1)}, u32[]{:S(2)}) copy-start(bf16[64,64]{1,0:T(8,128)(2,1)} %param.24) | copy-start | bytes 24580
  35.2 31.1 %copy-start.25 = (bf16[64,64]{1,0:T(8,128)(2,1)S(1)}, bf16[64,64]{1,0:T(8,128)(2,1)}, u32[]{:S(2)}) copy-start(bf16[64,64]{1,0:T(8,128)(2,1)} %param.25) | copy-start | bytes 24580
  35.2 31.9 %copy-start.10 = (bf16[64,1408]{1,0:T(8,128)(2,1)S(1)}, bf16[64,1408]{1,0:T(8,128)(2,1)}, u32[]{:S(2)}) copy-start(bf16[64,1408]{1,0:T(8,128)(2,1)} %param.30) | copy-start | bytes 540676
  35.3 31.9 %copy-start.11 = (bf16[64,1408]{1,0:T(8,128)(2,1)S(1)}, bf16[64,1408]{1,0:T(8,128)(2,1)}, u32[]{:S(2)}) copy-start(bf16[64,1408]{1,0:T(8,128)(2,1)} %param.29) | copy-start | bytes 540676
  35.3 31.9 %copy-start.12 = (bf16[64,1408]{1,0:T(8,128)(2,1)S(1)}, bf16[64,1408]{1,0:T(8,128)(2,1)}, u32[]{:S(2)}) copy-start(bf16[64,1408]{1,0:T(8,128)(2,1)} %param.28) | copy-start | bytes 540676
  35.3 24.9 %all-to-all-start = ((bf16[2,512,512]{2,0,1:T(2,128)(2,1)}), bf16[2,512,512]{2,0,1:T(2,128)(2,1)S(1)}, u32[]{:S(2)}, u32[]{:S(2)}) async-start(bf16[2,512,512]{2,0,1:T(2,128)(2,1)} %bitcast.2), calls=%async_computation | async-start | bytes 2097152 | tf_op jit(solution)/shard_map/all_to_all | solution.py:186
  42.8 25.8 %copy-start.28 = (s32[512]{0:T(512)S(1)}, s32[512]{0:T(512)}, u32[]{:S(2)}) copy-start(s32[512]{0:T(512)} %param.21) | copy-start | bytes 6148
  42.8 69.5 %all-gather.9.cloned.1.call-start = ((), (), s32[]{:S(2)}) async-start(), calls=%async_computation.12 | async-start | bytes 5242880 | tf_op jit(solution)/shard_map/all_gather | solution.py:192
  63.7 98.8 %copy-start.26 = (f32[2048]{0:T(1024)S(1)}, f32[2048]{0:T(1024)}, u32[]{:S(2)}) copy-start(f32[2048]{0:T(1024)} %param.22) | copy-start | bytes 24580
  66.3 96.3 %all-gather.5.cloned.1.call-start = ((), (), s32[]{:S(2)}) async-start(), calls=%async_computation.5 | async-start | bytes 4866048 | tf_op jit(solution)/shard_map/all_gather | solution.py:115
  67.1 170.8 %all-gather.7.cloned.1.call-start = ((), (), s32[]{:S(2)}) async-start(), calls=%async_computation.6 | async-start | bytes 17842176 | tf_op jit(solution)/shard_map/all_gather | solution.py:115
  68.1 267.6 %all-reduce.4.cloned.1.call-start = ((), (), s32[]{:S(2)}) async-start(), calls=%async_computation.7 | async-start | bytes 8388608 | tf_op jit(solution)/shard_map/psum | solution.py:239
  69.2 107.5 %copy-start.31 = (f32[32]{0:T(128)}, f32[32]{0:T(128)S(1)}, u32[]{:S(2)}) copy-start(f32[32]{0:T(128)S(1)} %negate_power_fusion) | copy-start | bytes 388
  69.4 107.3 %copy-start.17 = (f32[512]{0:T(512)}, f32[512]{0:T(512)S(1)}, u32[]{:S(2)}) copy-start(f32[512]{0:T(512)S(1)} %fusion.113) | copy-start | bytes 6148
  114.4 59.4 %copy-start.21 = (f32[512]{0:T(512)}, f32[512]{0:T(512)S(1)}, u32[]{:S(2)}) copy-start(f32[512]{0:T(512)S(1)} %add_rsqrt_fusion.1) | copy-start | bytes 6148
  196.0 5.4 copy-start.6
  243.4 219.7 %all-reduce.6.cloned.1.call-start = ((), (), s32[]{:S(2)}) async-start(), calls=%async_computation.9 | async-start | bytes 8388608 | tf_op jit(solution)/shard_map/psum | solution.py:259
  251.9 87.3 %copy-start.13 = (f32[2048]{0:T(1024)S(1)}, f32[2048]{0:T(1024)}, u32[]{:S(2)}) copy-start(f32[2048]{0:T(1024)} %param.27) | copy-start | bytes 24580
  339.2 7.6 copy-start
  339.3 128.7 %copy-start.19 = (f32[512]{0:T(512)}, f32[512]{0:T(512)S(1)}, u32[]{:S(2)}) copy-start(f32[512]{0:T(512)S(1)} %add_rsqrt_fusion) | copy-start | bytes 6148
  339.3 7.6 copy-start.33
  355.8 6.5 copy-start.9
  355.8 6.5 copy-start.8
  370.3 247.1 %all-reduce.8.cloned.1.call-start = ((), (), s32[]{:S(2)}) async-start(), calls=%async_computation.10 | async-start | bytes 4194304 | tf_op jit(solution)/shard_map/psum | solution.py:291
  463.1 4.9 copy-start.1
  463.1 5.9 copy-start.2
  471.8 2.0 copy-start.5
  543.3 5.1 copy-start.18
  543.3 5.1 copy-start.32
  558.8 113.9 %reduce-scatter.3.cloned.1.call-start = ((), (), s32[]{:S(2)}) async-start(), calls=%async_computation.8 | async-start | bytes 2621440 | tf_op jit(solution)/shard_map/reduce_scatter | solution.py:249
  566.7 4.5 copy-start.14
  566.7 4.5 copy-start.20
  566.7 238.7 %reduce-scatter.5.cloned.1.call-start = ((), (), s32[]{:S(2)}) async-start(), calls=%async_computation.11 | async-start | bytes 23248896 | tf_op jit(solution)/shard_map/reduce_scatter | solution.py:316
  570.2 6.2 copy-start.23
  571.2 5.5 copy-start.7
  576.7 40.7 %copy-start.22 = (f32[512]{0:T(512)S(1)}, f32[512]{0:T(512)}, u32[]{:S(2)}) copy-start(f32[512]{0:T(512)} %copy-done.21) | copy-start | bytes 6148
  576.7 40.7 %copy-start.27 = (f32[2048]{0:T(1024)S(1)}, f32[2048]{0:T(1024)}, u32[]{:S(2)}) copy-start(f32[2048]{0:T(1024)} %param.22) | copy-start | bytes 24580
  617.4 7.4 copy-start.3
  617.4 7.4 copy-start.4
  676.5 12.5 %copy-start.30 = (s32[512]{0:T(512)S(1)}, s32[512]{0:T(512)}, u32[]{:S(2)}) copy-start(s32[512]{0:T(512)} %copy-done.29) | copy-start | bytes 6148
  681.8 24.6 %all-to-all-start.2 = ((bf16[2,512,512]{2,0,1:T(2,128)(2,1)}), bf16[2,512,512]{2,0,1:T(2,128)(2,1)S(1)}, u32[]{:S(2)}, u32[]{:S(2)}) async-start(bf16[2,512,512]{2,0,1:T(2,128)(2,1)} %bitcast.29), calls=%async_computation.3 | async-start | bytes 2097152 | tf_op jit(solution)/shard_map/all_to_all | solution.py:332
Sparse Core Ops, SparseCore 0:
  66.4 45.8 all-gather.8
  115.1 47.3 all-gather.4
  164.8 73.1 all-gather.6
  243.5 92.1 all-reduce.3
  370.4 92.6 all-reduce.5
  558.9 58.4 all-reduce.7
  619.9 29.4 reduce-scatter.2
  672.7 132.7 reduce-scatter.4

commit v3 on v2

--- a/solution.py
+++ b/solution.py
@@ -128,6 +128,12 @@
     @pl.when(step == last)
     def _():
         out_ref[...] = tail_ref[...]
+
+
+def gain_tail_of(gain_grad):
+    return jnp.concatenate(
+        [gain_grad[:, None], jnp.zeros((gain_grad.shape[0], GRAD_BLOCK - 1), jnp.float32)], axis=1
+    ).astype(jnp.bfloat16)
 
 
 def packed_weight_grads(lefts, segments, tail):
@@ -189,12 +195,16 @@
         lax.all_to_all(slot_ids, "row", split_axis=0, concat_axis=0, tiled=True),
     )
     placing = jnp.argsort(arrived_slots)
-    full_pair = lax.all_gather(arrived_pair[:, placing], "col", axis=2, tiled=True)
-    full_rows, full_grads = full_pair[0], full_pair[1]
     attn_widths = [w_query.shape[1], w_key.shape[1], w_value.shape[1], w_output.shape[1]]
     ffn_widths = [w_gate.shape[1], w_up.shape[1], w_down.shape[1]]
     attn_packed = gather_rows([w_query, w_key, w_value, w_output])
-    ffn_packed = gather_rows([w_gate, w_up, w_down])
+    placed_pair, attn_packed = lax.optimization_barrier((arrived_pair[:, placing], attn_packed))
+    full_pair = lax.all_gather(placed_pair, "col", axis=2, tiled=True)
+    ffn_local, full_pair = lax.optimization_barrier(
+        (jnp.concatenate([w_gate, w_up, w_down], axis=1), full_pair)
+    )
+    ffn_packed = lax.all_gather(ffn_local, "row", axis=0, tiled=True)
+    full_rows, full_grads = full_pair[0], full_pair[1]
     query_w, key_w, value_w, output_w = split_columns(attn_packed, attn_widths)
     cosine, sine = rope_tables(positions_of(segment_ids))
     allowed = allowed_pairs(segment_ids)
@@ -236,7 +246,7 @@
     )
     attn_terms = matmul(mixed, output_w.T)
     attn_terms, ffn_packed = lax.optimization_barrier((attn_terms, ffn_packed))
-    attn_full = lax.psum(attn_terms, "col")
+    attn_full = lax.psum(attn_terms.astype(jnp.bfloat16), "col").astype(jnp.float32)
     resid = rows_wide + attn_full
     inv_two = rms_scale(resid)
     normed_two = (resid * inv_two * ffn_gain).astype(jnp.bfloat16)
@@ -256,8 +266,18 @@
     )
     up_grad = (act_grad * gate * sigmoid_gate).astype(jnp.bfloat16)
     normed_terms_two = matmul(gate_grad, gate_w.T) + matmul(up_grad, up_w.T)
-    normed_grad_two = lax.psum(normed_terms_two, "col")
+    normed_grad_two = lax.psum(normed_terms_two.astype(jnp.bfloat16), "col").astype(jnp.float32)
     resid_norm_grad, ffn_gain_grad = norm_back(resid, inv_two, ffn_gain, normed_grad_two)
+    ffn_grads_local = lax.psum_scatter(
+        packed_weight_grads(
+            [normed_two, full_grads],
+            [(0, gate_grad), (0, up_grad), (1, activ)],
+            gain_tail_of(ffn_gain_grad),
+        ),
+        "row",
+        scatter_dimension=0,
+        tiled=True,
+    )
     resid_grad = full_grads.astype(jnp.float32) + resid_norm_grad
     attn_grad_low = resid_grad.astype(jnp.bfloat16)
     mixed_grad = matmul(attn_grad_low, output_w).astype(jnp.bfloat16)
@@ -288,45 +308,29 @@
     normed_terms_one = (
         matmul(query_grad, query_w.T) + matmul(key_grad, key_w.T) + matmul(value_grad, value_w.T)
     )
-    normed_grad_one = lax.psum(normed_terms_one.astype(jnp.bfloat16), "col").astype(jnp.float32)
+    normed_low_one, ffn_grads_local = lax.optimization_barrier(
+        (normed_terms_one.astype(jnp.bfloat16), ffn_grads_local)
+    )
+    normed_grad_one = lax.psum(normed_low_one, "col").astype(jnp.float32)
     rows_norm_grad, attn_gain_grad = norm_back(rows_wide, inv_one, attn_gain, normed_grad_one)
     rows_grad = resid_grad + rows_norm_grad
     input_share = lax.dynamic_slice_in_dim(rows_grad, col_start, quarter, 1).astype(jnp.bfloat16)
-    gain_tail = jnp.concatenate(
-        [
-            attn_gain_grad[:, None],
-            ffn_gain_grad[:, None],
-            jnp.zeros((attn_gain_grad.shape[0], GRAD_BLOCK - 2), jnp.float32),
-        ],
-        axis=1,
-    ).astype(jnp.bfloat16)
-    grads_packed = packed_weight_grads(
-        [normed_one, attn_grad_low, normed_two, full_grads],
-        [
-            (0, query_grad),
-            (0, key_grad),
-            (0, value_grad),
-            (1, mixed),
-            (2, gate_grad),
-            (2, up_grad),
-            (3, activ),
-        ],
-        gain_tail,
-    )
-    grads_local = lax.psum_scatter(grads_packed, "row", scatter_dimension=0, tiled=True).astype(
-        jnp.float32
-    )
-    (
-        query_result,
-        key_result,
-        value_result,
-        output_result,
-        gate_result,
-        up_result,
-        down_result,
-        attn_gain_result,
-        ffn_gain_result,
-    ) = split_columns(grads_local, attn_widths + ffn_widths + [1, 1])
+    attn_grads_local = lax.psum_scatter(
+        packed_weight_grads(
+            [normed_one, attn_grad_low],
+            [(0, query_grad), (0, key_grad), (0, value_grad), (1, mixed)],
+            gain_tail_of(attn_gain_grad),
+        ),
+        "row",
+        scatter_dimension=0,
+        tiled=True,
+    )
+    query_result, key_result, value_result, output_result, attn_gain_result = split_columns(
+        attn_grads_local.astype(jnp.float32), attn_widths + [1]
+    )
+    gate_result, up_result, down_result, ffn_gain_result = split_columns(
+        ffn_grads_local.astype(jnp.float32), ffn_widths + [1]
+    )
     attn_gain_result = attn_gain_result.reshape(-1)
     ffn_gain_result = ffn_gain_result.reshape(-1)
     back_pair = lax.all_to_all(

time: 831 us -> 708 us (0.85)
  waiting for transfers between devices: 453 us -> 377 us
  matrix products: 135 us -> 95.4 us
    all_gather x2 -> x1, waiting for transfers between devices: 84.6 us -> 0.01 us  [gather_rows(): lax.all_gather(jnp.concatenate(parts, axis=1), 'row', axis=0, tiled=True)]
    psum x3, waiting for transfers between devices: 208 us -> 150 us  [the longest x1 50.5 us: body(): lax.psum(normed_terms_two.astype(jnp.bfloat16), 'col').astype(jnp.float32)]
    dot_general x70, matrix products: 135 us -> 95.4 us  [matmul(): return jnp.dot(left, right, preferred_element_type=jnp.float32)]
    all_gather x1 -> x2, waiting for transfers between devices: 42.6 us -> 80.7 us  [the longest x1 45.8 us: body(): full_pair = lax.all_gather(placed_pair, 'col', axis=2, tiled=True)]
    reduce_scatter x1 -> x2, waiting for transfers between devices: 92.1 us -> 104 us  [the longest x1 56.3 us: body(): lax.psum_scatter(packed_weight_grads([normed_two, full_grads], [(0, gate_...]
    reduce_scatter x1, waiting for transfers between devices: 0.02 us -> 10.2 us  [body(): lax.psum_scatter(matmul(activ, down_w.T).astype(jnp.bfloat16), 'col', sca...]
    pallas_call x1 -> x2, Pallas kernels: 43.9 us -> 46.4 us  [packed_weight_grads(): pl.pallas_call(grad_block_kernel, out_shape=jax.ShapeDtypeStruct((feature...]
  transfers between devices with their start and end apart: 11 -> 12, of which waited for: 9 -> 10; matrix products, arithmetic and copies ran while one was open for 15% -> 27% of each run, Pallas kernels for 5% -> 2%
where the time goes in v3:
time: 708 us; the launch traced here: 699 us
  waiting for transfers between devices  377 us (53%)
  matrix products  95.4 us (13%)
  local copies, waits for them, and re-layouts  75.9 us (11%)
  other arithmetic  63.8 us (9%)
  Pallas kernels  46.4 us (7%)
  starting transfers between devices  24.7 us (3%)
  between operations  15 us (2%)
    dot_general x70, matrix products, matmul(): return jnp.dot(left, right, preferred_element_type=jnp.float32)  95.4 us
    reduce_scatter x1, waiting for transfers between devices, body(): lax.psum_scatter(packed_weight_grads([normed_two, full_grads], [(0, gate_...  56.3 us
    psum x1, waiting for transfers between devices, body(): lax.psum(normed_terms_two.astype(jnp.bfloat16), 'col').astype(jnp.float32)  50.5 us
    psum x1, waiting for transfers between devices, body(): normed_grad_one = lax.psum(normed_low_one, 'col').astype(jnp.float32)  50.3 us
    psum x1, waiting for transfers between devices, body(): lax.psum(attn_terms.astype(jnp.bfloat16), 'col').astype(jnp.float32)  49.6 us
    reduce_scatter x1, waiting for transfers between devices, body(): lax.psum_scatter(packed_weight_grads([normed_one, attn_grad_low], [(0, qu...  48 us
    pallas_call x2, Pallas kernels, packed_weight_grads(): pl.pallas_call(grad_block_kernel, out_shape=jax.ShapeDtypeStruct((feature...  46.4 us
    all_gather x1, waiting for transfers between devices, body(): full_pair = lax.all_gather(placed_pair, 'col', axis=2, tiled=True)  45.8 us
  transfers between devices with their start and end apart: 12, of which 10 were waited for; matrix products, arithmetic and copies ran while one was open for 27% of the time, Pallas kernels for 2%

profile of v3, /device:TPU:0, one launch (start us, length us, event | category | flops | bytes accessed | tf_op | source)
XLA Modules:
  0.0 698.5 jit_solution(3492019348958517383)
XLA Ops:
  7.2 1.7 concatenate.53
  9.0 4.4 sort.45
  14.0 3.6 gather_fusion.1
  18.3 8.4 %all-to-all-start.1 = ((s32[32,16,1]{1,2,0:T(1,128)}), s32[32,16,1]{1,2,0:T(1,128)S(1)}, u32[]{:S(2)}, u32[]{:S(2)}) async-start(s32[32,16,1]{1,2,0:T(1,128)} %bitcast.3), calls=%async_computation.1 | async-start | bytes 32768 | tf_op jit(solution)/shard_map/all_to_all | solution.py:195
  26.7 1.9 copy.115
  29.4 2.4 pad_maximum_fusion.3
  31.9 4.1 gather_fusion
  36.0 7.5 %all-to-all-start = ((bf16[2,512,512]{2,0,1:T(2,128)(2,1)}), bf16[2,512,512]{2,0,1:T(2,128)(2,1)S(1)}, u32[]{:S(2)}, u32[]{:S(2)}) async-start(bf16[2,512,512]{2,0,1:T(2,128)(2,1)} %bitcast.2), calls=%async_computation | async-start | bytes 2097152 | tf_op jit(solution)/shard_map/all_to_all | solution.py:192
  44.9 3.8 sort.46
  48.7 19.7 %all-to-all-done = bf16[2,512,512]{2,0,1:T(2,128)(2,1)S(1)} async-done(((bf16[2,512,512]{2,0,1:T(2,128)(2,1)}), bf16[2,512,512]{2,0,1:T(2,128)(2,1)S(1)}, u32[]{:S(2)}, u32[]{:S(2)}) %all-to-all-start) | async-done | bytes 1048608 | tf_op jit(solution)/shard_map/all_to_all | solution.py:192
  68.4 3.6 gather_fusion.2
  71.9 2.5 copy.118
  75.4 45.8 %all-gather.6.cloned.1.call-done = bf16[2,512,2048]{1,2,0:T(8,128)(2,1)} async-done(((bf16[2,512,512]{1,2,0:T(8,128)(2,1)}), bf16[2,512,2048]{1,2,0:T(8,128)(2,1)}) %all-gather.6.cloned.1.call-update) | async-done | bytes 4194320 | tf_op jit(solution)/shard_map/all_gather | solution.py:202
  123.7 1.7 slice_bitcast_fusion
  125.5 2.5 copy.119
  128.0 2.1 fusion.63
  130.1 2.8 fusion.86
  133.1 3.1 fusion.72
  136.9 2.9 convolution_bitcast_fusion.2
  141.2 17.9 %while.32 = (s32[]{:T(128)}, bf16[8,512,64]{1,2,0:T(8,128)(2,1)S(1)}, f32[8,512]{1,0:T(8,128)}, bf16[8,512,64]{2,1,0:T(8,128)(2,1)S(1)}, bf16[1,512,64]{2,1,0:T(...) while((s32[]{:T(128)}, bf16[8,512,64]{1,2,0:T(8,128)(2,1)S(1)}, ...), condition=%wide.region_8.9_spmd.clone.clone, body=%wide.region_5.8_spmd.clone.sunk.clone | while | flops 69991936 | bytes 3694689 | solution.py:232
  159.9 3.1 fusion.79
  163.0 34.8 %all-gather.8.cloned.1.call-done = bf16[2048,4224]{1,0:T(8,128)(2,1)} async-done(((bf16[64,4224]{1,0:T(8,128)(2,1)}), bf16[2048,4224]{1,0:T(8,128)(2,1)}) %all-gather.8.cloned.1.call-update) | async-done | bytes 17301520 | tf_op jit(solution)/shard_map/all_gather | solution.py:206
  197.8 2.5 copy.125
  200.6 8.3 %fusion.44 = f32[512,1408]{1,0:T(8,128)} fusion(bf16[2048,4224]{1,0:T(8,128)(2,1)} %all-gather.8.cloned.1.call-done, bf16[2,512,2048]{1,2,0:T(8,128)(2,1)} %all-gather.6.cloned.1.call-done), kind=kOutput, calls=%fused_computation.68 | convolution fusion | flops 2952790016 | bytes 10747904 | tf_op jit(solution)/shard_map/dot_general | solution.py:68
  209.0 49.6 %all-reduce.6.cloned.1.call-done = bf16[512,2048]{0,1:T(8,128)(2,1)} async-done(((bf16[512,2048]{0,1:T(8,128)(2,1)}), bf16[512,2048]{0,1:T(8,128)(2,1)}) %all-reduce.6.cloned.1.call-update) | async-done | bytes 2097168 | tf_op jit(solution)/shard_map/psum | solution.py:249
  258.6 3.1 multiply_reduce_fusion.2
  262.0 3.6 fusion.41
  265.6 5.8 fusion.54
  271.4 2.0 copy-done.32
  273.4 7.1 %multiply_convert_fusion.5 = (bf16[512,1408]{1,0:T(8,128)(2,1)}, bf16[512,1408]{1,0:T(8,128)(2,1)S(1)}, bf16[512,1408]{1,0:T(8,128)(2,1)S(1)}) fusion(f32[512,1408]{1,0:T(8,128)S(1)} %fusion.54, f32[512,1408]{1,0:T(8,128)} %fusion.44, bf16[512,2048]{0,1:T(8,128)(2,1)S(1)} %get-tuple-element.342, bf16[2048,4224]{1,0:T(8,128)(2,1)S(1)} %copy-done.32), kind=kOutput, calls=%fused_computation.102 | convolution fusion | flops 2964324352 | bytes 17956864 | tf_op jit(solution)/shard_map/dot_general | solution.py:68
  280.6 3.5 fusion.48
  284.1 4.6 add_convert_fusion.1
  289.0 1.7 slice_bitcast_fusion.1
  290.8 2.5 pad_maximum_fusion.1.left_ref
  294.5 2.4 pad_maximum_fusion.right_ref
  296.9 50.5 %all-reduce.8.cloned.1.call-done = bf16[512,2048]{0,1:T(8,128)(2,1)} async-done(((bf16[512,2048]{0,1:T(8,128)(2,1)}), bf16[512,2048]{0,1:T(8,128)(2,1)}) %all-reduce.8.cloned.1.call-update) | async-done | bytes 2097168 | tf_op jit(solution)/shard_map/psum | solution.py:269
  347.4 4.3 fusion.61
  352.9 34.2 %shard_map.230 = bf16[2048,4352]{1,0:T(8,128)(2,1)} custom-call(s32[34]{0:T(128)} %constant.125.clone.select_ref, bf16[2,2048,512]{2,1,0:T(8,128)(2,1)} %pad_maximum_fusion.1.left_ref, bf16[512,4224]{1,0:T(8,128)(2,1)} %pad_maximum_fusion.right_ref, bf16[2048,128]{1,0:T(8,128)(2,1)} %concatenate.63.tail_ref), custom_call_target="tpu_custom_call" | custom-call | tf_op jit(solution)/shard_map/pallas_call | solution.py:152
  387.9 4.7 convert_bitcast_fusion.1
  392.6 2.0 copy-done.3
  394.6 4.0 fusion.83
  398.6 1.6 copy.129
  400.1 37.3 %while.33 = (s32[]{:T(128)}, f32[8,512,64]{1,2,0:T(8,128)}, f32[8,512,64]{1,2,0:T(8,128)}, f32[8,512,64]{1,2,0:T(8,128)S(1)}, bf16[8,512,64]{2,1,0:T(8,128)(2,1)...) while((s32[]{:T(128)}, f32[8,512,64]{1,2,0:T(8,128)}, ...), condition=%wide.region_16.17_spmd.clone.clone, body=%wide.region_14.16_spmd.clone.sunk.clone | while | flops 170982912 | bytes 9126013 | solution.py:285
  439.2 1.9 fusion.112
  441.4 2.0 fusion.93
  443.4 1.8 fusion.96
  445.2 4.4 add_convert_fusion
  449.6 56.3 %reduce-scatter.6.cloned.1.call-done = bf16[64,4352]{1,0:T(8,128)(2,1)} async-done(((bf16[2048,4352]{1,0:T(8,128)(2,1)}), bf16[64,4352]{1,0:T(8,128)(2,1)}) %reduce-scatter.6.cloned.1.call-update) | async-done | bytes 557072 | tf_op jit(solution)/shard_map/reduce_scatter | solution.py:271
  505.9 7.4 %fusion.68 = bf16[512,2048]{0,1:T(8,128)(2,1)} fusion(bf16[512,1408]{1,0:T(8,128)(2,1)S(1)} %copy-done.10, bf16[2048,4224]{1,0:T(8,128)(2,1)} %all-gather.8.cloned.1.call-done), kind=kOutput, calls=%fused_computation.99 | convolution fusion | flops 2953838592 | bytes 9306112 | tf_op jit(solution)/shard_map/dot_general | solution.py:68
  514.1 1.9 concatenate.64.right_ref
  516.1 50.3 %all-reduce.10.cloned.1.call-done = bf16[512,2048]{0,1:T(8,128)(2,1)} async-done(((bf16[512,2048]{0,1:T(8,128)(2,1)}), bf16[512,2048]{0,1:T(8,128)(2,1)}) %all-reduce.10.cloned.1.call-update) | async-done | bytes 2097168 | tf_op jit(solution)/shard_map/psum | solution.py:314
  566.3 5.7 fusion.62
  573.3 2.5 pad_maximum_fusion.2.left_ref
  575.7 12.2 %shard_map.231 = bf16[2048,1280]{1,0:T(8,128)(2,1)} custom-call(s32[10]{0:T(128)} %constant.126.clone.select_ref, bf16[2,2048,512]{2,1,0:T(8,128)(2,1)} %pad_maximum_fusion.2.left_ref, bf16[512,1152]{1,0:T(8,128)(2,1)} %concatenate.64.right_ref, bf16[2048,128]{1,0:T(8,128)(2,1)} %concatenate.65.tail_ref), custom_call_target="tpu_custom_call" | custom-call | tf_op jit(solution)/shard_map/pallas_call | solution.py:152
  588.0 10.2 %reduce-scatter.4.cloned.1.call-done = bf16[512,512]{0,1:T(8,128)(2,1)} async-done(((bf16[512,2048]{0,1:T(8,128)(2,1)}), bf16[512,512]{0,1:T(8,128)(2,1)}) %reduce-scatter.4.cloned.1.call-update) | async-done | bytes 524304 | tf_op jit(solution)/shard_map/reduce_scatter | solution.py:259
  599.8 2.3 fusion.92
  603.2 4.1 gather_fusion.3
  607.3 7.3 %all-to-all-start.2 = ((bf16[2,512,512]{2,0,1:T(2,128)(2,1)}), bf16[2,512,512]{2,0,1:T(2,128)(2,1)S(1)}, u32[]{:S(2)}, u32[]{:S(2)}) async-start(bf16[2,512,512]{2,0,1:T(2,128)(2,1)} %bitcast.33), calls=%async_computation.4 | async-start | bytes 2097152 | tf_op jit(solution)/shard_map/all_to_all | solution.py:336
  614.6 3.8 sort.47
  620.1 11.8 %all-to-all-done.2 = bf16[2,512,512]{2,0,1:T(2,128)(2,1)S(1)} async-done(((bf16[2,512,512]{2,0,1:T(2,128)(2,1)}), bf16[2,512,512]{2,0,1:T(2,128)(2,1)S(1)}, u32[]{:S(2)}, u32[]{:S(2)}) %all-to-all-start.2) | async-done | bytes 1048608 | tf_op jit(solution)/shard_map/all_to_all | solution.py:336
  633.7 2.6 gather_fusion.5
  636.3 2.6 gather_fusion.4
  638.9 48.0 %reduce-scatter.8.cloned.1.call-done = bf16[64,1280]{1,0:T(8,128)(2,1)} async-done(((bf16[2048,1280]{1,0:T(8,128)(2,1)}), bf16[64,1280]{1,0:T(8,128)(2,1)}) %reduce-scatter.8.cloned.1.call-update) | async-done | bytes 163856 | tf_op jit(solution)/shard_map/reduce_scatter | solution.py:318
  690.0 1.6 fusion.124
  (247 shorter events, 82.2 us)
Async XLA Ops:
  7.2 21.4 %copy-start.17 = (bf16[512,512]{1,0:T(8,128)(2,1)S(1)}, bf16[512,512]{1,0:T(8,128)(2,1)}, u32[]{:S(2)}) copy-start(bf16[512,512]{1,0:T(8,128)(2,1)} %param.20) | copy-start | bytes 1572868
  7.2 67.3 %all-gather.4.cloned.1.call-start = ((), (), s32[]{:S(2)}) async-start(), calls=%async_computation.6 | async-start | bytes 4866048 | tf_op jit(solution)/shard_map/all_gather | solution.py:115
  13.4 0.6 copy-start.29
  18.3 17.7 %all-to-all-start.1 = ((s32[32,16,1]{1,2,0:T(1,128)}), s32[32,16,1]{1,2,0:T(1,128)S(1)}, u32[]{:S(2)}, u32[]{:S(2)}) async-start(s32[32,16,1]{1,2,0:T(1,128)} %bitcast.3), calls=%async_computation.1 | async-start | bytes 32768 | tf_op jit(solution)/shard_map/all_to_all | solution.py:195
  36.0 38.5 %copy-start.18 = (bf16[64,1408]{1,0:T(8,128)(2,1)S(1)}, bf16[64,1408]{1,0:T(8,128)(2,1)}, u32[]{:S(2)}) copy-start(bf16[64,1408]{1,0:T(8,128)(2,1)} %param.31) | copy-start | bytes 540676
  36.0 38.6 %copy-start.19 = (bf16[64,1408]{1,0:T(8,128)(2,1)S(1)}, bf16[64,1408]{1,0:T(8,128)(2,1)}, u32[]{:S(2)}) copy-start(bf16[64,1408]{1,0:T(8,128)(2,1)} %param.30) | copy-start | bytes 540676
  36.0 38.6 %copy-start.20 = (bf16[64,1408]{1,0:T(8,128)(2,1)S(1)}, bf16[64,1408]{1,0:T(8,128)(2,1)}, u32[]{:S(2)}) copy-start(bf16[64,1408]{1,0:T(8,128)(2,1)} %param.29) | copy-start | bytes 540676
  36.0 85.8 %copy-start.27 = (s32[512]{0:T(512)S(1)}, s32[512]{0:T(512)}, u32[]{:S(2)}) copy-start(s32[512]{0:T(512)} %param.22) | copy-start | bytes 6148
  36.0 32.4 %all-to-all-start = ((bf16[2,512,512]{2,0,1:T(2,128)(2,1)}), bf16[2,512,512]{2,0,1:T(2,128)(2,1)S(1)}, u32[]{:S(2)}, u32[]{:S(2)}) async-start(bf16[2,512,512]{2,0,1:T(2,128)(2,1)} %bitcast.2), calls=%async_computation | async-start | bytes 2097152 | tf_op jit(solution)/shard_map/all_to_all | solution.py:192
  43.6 77.7 %all-gather.6.cloned.1.call-start = ((), (), s32[]{:S(2)}) async-start(), calls=%async_computation.7 | async-start | bytes 5242880 | tf_op jit(solution)/shard_map/all_gather | solution.py:202
  74.5 123.4 %all-gather.8.cloned.1.call-start = ((), (), s32[]{:S(2)}) async-start(), calls=%async_computation.8 | async-start | bytes 17842176 | tf_op jit(solution)/shard_map/all_gather | solution.py:206
  121.3 137.3 %all-reduce.6.cloned.1.call-start = ((), (), s32[]{:S(2)}) async-start(), calls=%async_computation.9 | async-start | bytes 4194304 | tf_op jit(solution)/shard_map/psum | solution.py:249
  122.4 17.4 %copy-start.31 = (f32[32]{0:T(128)}, f32[32]{0:T(128)S(1)}, u32[]{:S(2)}) copy-start(f32[32]{0:T(128)S(1)} %negate_power_fusion) | copy-start | bytes 388
  123.4 16.4 %copy-start.21 = (f32[512]{0:T(512)}, f32[512]{0:T(512)S(1)}, u32[]{:S(2)}) copy-start(f32[512]{0:T(512)S(1)} %fusion.118) | copy-start | bytes 6148
  125.5 4.6 copy-start.25
  130.1 6.8 copy-start.23
  130.1 3.0 copy-start.5
  136.9 4.3 copy-start.6
  136.9 4.2 copy-start.28
  159.1 0.8 copy-start.7
  200.4 147.0 %all-reduce.8.cloned.1.call-start = ((), (), s32[]{:S(2)}) async-start(), calls=%async_computation.11 | async-start | bytes 4194304 | tf_op jit(solution)/shard_map/psum | solution.py:269
  258.6 3.4 copy-start
  262.0 3.6 copy-start.22
  265.6 7.8 %copy-start.32 = (bf16[2048,4224]{1,0:T(8,128)(2,1)S(1)}, bf16[2048,4224]{1,0:T(8,128)(2,1)}, u32[]{:S(2)}) copy-start(bf16[2048,4224]{1,0:T(8,128)(2,1)} %all-gather.8.cloned.1.call-done) | copy-start | bytes 51904516
  280.6 3.5 copy-start.13
  280.6 3.5 copy-start.11
  288.7 217.1 %reduce-scatter.6.cloned.1.call-start = ((), (), s32[]{:S(2)}) async-start(), calls=%async_computation.12 | async-start | bytes 18382848 | tf_op jit(solution)/shard_map/reduce_scatter | solution.py:271
  290.7 2.5 copy-start.9
  290.7 2.9 copy-start.12
  290.8 3.7 copy-start.14
  294.5 52.9 %copy-start.1 = (bf16[512,2048]{0,1:T(8,128)(2,1)S(1)}, bf16[512,2048]{0,1:T(8,128)(2,1)}, u32[]{:S(2)}) copy-start(bf16[512,2048]{0,1:T(8,128)(2,1)} %all-reduce.6.cloned.1.call-done) | copy-start | bytes 6291460
  387.2 179.2 %all-reduce.10.cloned.1.call-start = ((), (), s32[]{:S(2)}) async-start(), calls=%async_computation.13 | async-start | bytes 4194304 | tf_op jit(solution)/shard_map/psum | solution.py:314
  392.6 2.0 copy-start.3
  394.6 5.5 copy-start.15
  437.5 3.8 copy-start.16
  445.2 60.8 %copy-start.10 = (bf16[512,1408]{1,0:T(8,128)(2,1)S(1)}, bf16[512,1408]{1,0:T(8,128)(2,1)}, u32[]{:S(2)}) copy-start(bf16[512,1408]{1,0:T(8,128)(2,1)} %get-tuple-element.343) | copy-start | bytes 4325380
  505.9 7.8 %copy-start.8 = (bf16[8,512,64]{1,2,0:T(8,128)(2,1)S(1)}, bf16[8,512,64]{1,2,0:T(8,128)(2,1)}, u32[]{:S(2)}) copy-start(bf16[8,512,64]{1,2,0:T(8,128)(2,1)} %copy-done.7) | copy-start | bytes 1572868
  505.9 92.3 %reduce-scatter.4.cloned.1.call-start = ((), (), s32[]{:S(2)}) async-start(), calls=%async_computation.10 | async-start | bytes 2621440 | tf_op jit(solution)/shard_map/reduce_scatter | solution.py:259
  513.3 53.0 %copy-start.24 = (f32[512]{0:T(512)S(1)}, f32[512]{0:T(512)}, u32[]{:S(2)}) copy-start(f32[512]{0:T(512)} %copy-done.23) | copy-start | bytes 6148
  513.3 53.0 %copy-start.26 = (f32[2048]{0:T(1024)S(1)}, f32[2048]{0:T(1024)}, u32[]{:S(2)}) copy-start(f32[2048]{0:T(1024)} %param.23) | copy-start | bytes 24580
  513.4 173.6 %reduce-scatter.8.cloned.1.call-start = ((), (), s32[]{:S(2)}) async-start(), calls=%async_computation.14 | async-start | bytes 5406720 | tf_op jit(solution)/shard_map/reduce_scatter | solution.py:318
  516.1 57.2 %copy-start.2 = (bf16[1,2048,512]{2,1,0:T(8,128)(2,1)S(1)}, bf16[1,2048,512]{2,1,0:T(8,128)(2,1)}, u32[]{:S(2)}) copy-start(bf16[1,2048,512]{2,1,0:T(8,128)(2,1)} %get-tuple-element.335) | copy-start | bytes 6291460
  602.0 12.5 %copy-start.30 = (s32[512]{0:T(512)S(1)}, s32[512]{0:T(512)}, u32[]{:S(2)}) copy-start(s32[512]{0:T(512)} %copy-done.29) | copy-start | bytes 6148
  602.1 16.3 %copy-start.4 = (bf16[64,4352]{1,0:T(8,128)(2,1)S(1)}, bf16[64,4352]{1,0:T(8,128)(2,1)}, u32[]{:S(2)}) copy-start(bf16[64,4352]{1,0:T(8,128)(2,1)} %reduce-scatter.6.cloned.1.call-done) | copy-start | bytes 1671172
  607.3 24.6 %all-to-all-start.2 = ((bf16[2,512,512]{2,0,1:T(2,128)(2,1)}), bf16[2,512,512]{2,0,1:T(2,128)(2,1)S(1)}, u32[]{:S(2)}, u32[]{:S(2)}) async-start(bf16[2,512,512]{2,0,1:T(2,128)(2,1)} %bitcast.33), calls=%async_computation.4 | async-start | bytes 2097152 | tf_op jit(solution)/shard_map/all_to_all | solution.py:336
Sparse Core Ops, SparseCore 0:
  10.8 59.7 all-gather.3
  74.6 46.5 all-gather.5
  123.5 74.2 all-gather.7
  200.5 58.0 all-reduce.5
  288.9 58.4 all-reduce.7
  387.3 118.5 reduce-scatter.5
  508.3 57.9 all-reduce.9
  568.7 29.4 reduce-scatter.3
  602.4 84.4 reduce-scatter.7

commit v4 on v3

--- a/solution.py
+++ b/solution.py
@@ -130,13 +130,19 @@
         out_ref[...] = tail_ref[...]
 
 
-def gain_tail_of(gain_grad):
-    return jnp.concatenate(
-        [gain_grad[:, None], jnp.zeros((gain_grad.shape[0], GRAD_BLOCK - 1), jnp.float32)], axis=1
-    ).astype(jnp.bfloat16)
-
-
-def packed_weight_grads(lefts, segments, tail):
+def grad_plain_kernel(select_ref, left_ref, right_ref, out_ref):
+    out_ref[...] = jnp.dot(
+        left_ref[0], right_ref[...], preferred_element_type=jnp.float32
+    ).astype(out_ref.dtype)
+
+
+def gain_tail_of(gain_grads):
+    columns = [grad[:, None] for grad in gain_grads]
+    padding = jnp.zeros((gain_grads[0].shape[0], GRAD_BLOCK - len(columns)), jnp.float32)
+    return jnp.concatenate(columns + [padding], axis=1).astype(jnp.bfloat16)
+
+
+def packed_weight_grads(lefts, segments, tail=None):
     left_stack = jnp.stack([left.T for left in lefts])
     right = jnp.concatenate([seg for _, seg in segments], axis=1)
     column_owner = []
@@ -146,25 +152,28 @@
     select = column_owner[::GRAD_BLOCK]
     assert column_owner == [owner for owner in select for _ in range(GRAD_BLOCK)]
     right_blocks = len(select)
-    select.append(select[-1])
     features, tokens = left_stack.shape[1], left_stack.shape[2]
-    total = right.shape[1] + GRAD_BLOCK
+    in_specs = [
+        pl.BlockSpec((1, features, tokens), lambda j, sel: (sel[j], 0, 0)),
+        pl.BlockSpec((tokens, GRAD_BLOCK), lambda j, sel: (0, jnp.minimum(j, right_blocks - 1))),
+    ]
+    operands = [left_stack, right]
+    kernel = grad_plain_kernel
+    if tail is not None:
+        select.append(select[-1])
+        in_specs.append(pl.BlockSpec((features, GRAD_BLOCK), lambda j, sel: (0, 0)))
+        operands.append(tail)
+        kernel = grad_block_kernel
     return pl.pallas_call(
-        grad_block_kernel,
-        out_shape=jax.ShapeDtypeStruct((features, total), jnp.bfloat16),
+        kernel,
+        out_shape=jax.ShapeDtypeStruct((features, len(select) * GRAD_BLOCK), jnp.bfloat16),
         grid_spec=pltpu.PrefetchScalarGridSpec(
             num_scalar_prefetch=1,
             grid=(len(select),),
-            in_specs=[
-                pl.BlockSpec((1, features, tokens), lambda j, sel: (sel[j], 0, 0)),
-                pl.BlockSpec(
-                    (tokens, GRAD_BLOCK), lambda j, sel: (0, jnp.minimum(j, right_blocks - 1))
-                ),
-                pl.BlockSpec((features, GRAD_BLOCK), lambda j, sel: (0, 0)),
-            ],
+            in_specs=in_specs,
             out_specs=pl.BlockSpec((features, GRAD_BLOCK), lambda j, sel: (0, j)),
         ),
-    )(jnp.asarray(select, dtype=jnp.int32), left_stack, right, tail)
+    )(jnp.asarray(select, dtype=jnp.int32), *operands)
 
 
 def body(
@@ -256,28 +265,28 @@
     upper = matmul(normed_two, up_w)
     sigmoid_gate = jax.nn.sigmoid(gate)
     activ = (gate * sigmoid_gate * upper).astype(jnp.bfloat16)
-    ffn_share = lax.psum_scatter(
+    ffn_share_low = lax.psum_scatter(
         matmul(activ, down_w.T).astype(jnp.bfloat16), "col", scatter_dimension=1, tiled=True
-    ).astype(jnp.float32)
-    output_share = (resid_part + ffn_share).astype(jnp.bfloat16)
+    )
     act_grad = matmul(full_grads, down_w)
     gate_grad = (act_grad * upper * sigmoid_gate * (1.0 + gate * (1.0 - sigmoid_gate))).astype(
         jnp.bfloat16
     )
     up_grad = (act_grad * gate * sigmoid_gate).astype(jnp.bfloat16)
     normed_terms_two = matmul(gate_grad, gate_w.T) + matmul(up_grad, up_w.T)
-    normed_grad_two = lax.psum(normed_terms_two.astype(jnp.bfloat16), "col").astype(jnp.float32)
+    normed_low_two, ffn_share_low = lax.optimization_barrier(
+        (normed_terms_two.astype(jnp.bfloat16), ffn_share_low)
+    )
+    output_share = (resid_part + ffn_share_low.astype(jnp.float32)).astype(jnp.bfloat16)
+    normed_grad_two = lax.psum(normed_low_two, "col").astype(jnp.float32)
+    ffn_grads_packed = packed_weight_grads(
+        [normed_two, full_grads], [(0, gate_grad), (0, up_grad), (1, activ)]
+    )
+    ffn_grads_packed, normed_grad_two = lax.optimization_barrier(
+        (ffn_grads_packed, normed_grad_two)
+    )
     resid_norm_grad, ffn_gain_grad = norm_back(resid, inv_two, ffn_gain, normed_grad_two)
-    ffn_grads_local = lax.psum_scatter(
-        packed_weight_grads(
-            [normed_two, full_grads],
-            [(0, gate_grad), (0, up_grad), (1, activ)],
-            gain_tail_of(ffn_gain_grad),
-        ),
-        "row",
-        scatter_dimension=0,
-        tiled=True,
-    )
+    ffn_grads_local = lax.psum_scatter(ffn_grads_packed, "row", scatter_dimension=0, tiled=True)
     resid_grad = full_grads.astype(jnp.float32) + resid_norm_grad
     attn_grad_low = resid_grad.astype(jnp.bfloat16)
     mixed_grad = matmul(attn_grad_low, output_w).astype(jnp.bfloat16)
@@ -319,17 +328,22 @@
         packed_weight_grads(
             [normed_one, attn_grad_low],
             [(0, query_grad), (0, key_grad), (0, value_grad), (1, mixed)],
-            gain_tail_of(attn_gain_grad),
+            gain_tail_of([attn_gain_grad, ffn_gain_grad]),
         ),
         "row",
         scatter_dimension=0,
         tiled=True,
     )
-    query_result, key_result, value_result, output_result, attn_gain_result = split_columns(
-        attn_grads_local.astype(jnp.float32), attn_widths + [1]
-    )
-    gate_result, up_result, down_result, ffn_gain_result = split_columns(
-        ffn_grads_local.astype(jnp.float32), ffn_widths + [1]
+    (
+        query_result,
+        key_result,
+        value_result,
+        output_result,
+        attn_gain_result,
+        ffn_gain_result,
+    ) = split_columns(attn_grads_local.astype(jnp.float32), attn_widths + [1, 1])
+    gate_result, up_result, down_result = split_columns(
+        ffn_grads_local.astype(jnp.float32), ffn_widths
     )
     attn_gain_result = attn_gain_result.reshape(-1)
     ffn_gain_result = ffn_gain_result.reshape(-1)

time: 708 us -> 687 us (0.970)
  waiting for transfers between devices: 377 us -> 342 us
  matrix products: 95.4 us -> 104 us
    psum x1, waiting for transfers between devices: 50.5 us -> 18.6 us  [body(): normed_grad_two = lax.psum(normed_low_two, 'col').astype(jnp.float32)]
    dot_general x70, matrix products: 95.4 us -> 104 us  [matmul(): return jnp.dot(left, right, preferred_element_type=jnp.float32)]
    psum x1, waiting for transfers between devices: 50.3 us -> 57.4 us  [body(): normed_grad_one = lax.psum(normed_low_one, 'col').astype(jnp.float32)]
  transfers between devices with their start and end apart: 12 -> 12, of which waited for: 10 -> 10; matrix products, arithmetic and copies ran while one was open for 27% -> 28% of each run, Pallas kernels for 2% -> 5%
where the time goes in v4:
time: 687 us; the launch traced here: 676 us
  waiting for transfers between devices  342 us (50%)
  matrix products  104 us (15%)
  local copies, waits for them, and re-layouts  78.9 us (11%)
  other arithmetic  66.3 us (10%)
  Pallas kernels  45.8 us (7%)
  starting transfers between devices  24.7 us (4%)
  between operations  15 us (2%)
    dot_general x70, matrix products, matmul(): return jnp.dot(left, right, preferred_element_type=jnp.float32)  104 us
    psum x1, waiting for transfers between devices, body(): normed_grad_one = lax.psum(normed_low_one, 'col').astype(jnp.float32)  57.4 us
    reduce_scatter x1, waiting for transfers between devices, body(): lax.psum_scatter(ffn_grads_packed, 'row', scatter_dimension=0, tiled=True)  50.6 us
    psum x1, waiting for transfers between devices, body(): lax.psum(attn_terms.astype(jnp.bfloat16), 'col').astype(jnp.float32)  49.6 us
    all_gather x1, waiting for transfers between devices, body(): full_pair = lax.all_gather(placed_pair, 'col', axis=2, tiled=True)  45.8 us
    pallas_call x2, Pallas kernels, packed_weight_grads(): pl.pallas_call(kernel, out_shape=jax.ShapeDtypeStruct((features, len(sele...  45.8 us
    reduce_scatter x1, waiting for transfers between devices, body(): lax.psum_scatter(packed_weight_grads([normed_one, attn_grad_low], [(0, qu...  43.2 us
    all_gather x1, waiting for transfers between devices, body(): ffn_packed = lax.all_gather(ffn_local, 'row', axis=0, tiled=True)  28.3 us
  transfers between devices with their start and end apart: 12, of which 10 were waited for; matrix products, arithmetic and copies ran while one was open for 28% of the time, Pallas kernels for 5%

profile of v4, /device:TPU:0, one launch (start us, length us, event | category | flops | bytes accessed | tf_op | source)
XLA Modules:
  0.0 676.5 jit_solution(17800166988128742721)
XLA Ops:
  7.2 1.7 concatenate.51
  9.0 4.4 sort.45
  14.0 3.6 gather_fusion.1
  18.3 8.4 %all-to-all-start.1 = ((s32[32,16,1]{1,2,0:T(1,128)}), s32[32,16,1]{1,2,0:T(1,128)S(1)}, u32[]{:S(2)}, u32[]{:S(2)}) async-start(s32[32,16,1]{1,2,0:T(1,128)} %bitcast.3), calls=%async_computation.1 | async-start | bytes 32768 | tf_op jit(solution)/shard_map/all_to_all | solution.py:204
  26.7 1.9 copy.115
  29.4 2.4 pad_maximum_fusion.3
  31.9 4.1 gather_fusion
  36.0 7.5 %all-to-all-start = ((bf16[2,512,512]{2,0,1:T(2,128)(2,1)}), bf16[2,512,512]{2,0,1:T(2,128)(2,1)S(1)}, u32[]{:S(2)}, u32[]{:S(2)}) async-start(bf16[2,512,512]{2,0,1:T(2,128)(2,1)} %bitcast.2), calls=%async_computation | async-start | bytes 2097152 | tf_op jit(solution)/shard_map/all_to_all | solution.py:201
  44.9 3.8 sort.46
  48.7 19.7 %all-to-all-done = bf16[2,512,512]{2,0,1:T(2,128)(2,1)S(1)} async-done(((bf16[2,512,512]{2,0,1:T(2,128)(2,1)}), bf16[2,512,512]{2,0,1:T(2,128)(2,1)S(1)}, u32[]{:S(2)}, u32[]{:S(2)}) %all-to-all-start) | async-done | bytes 1048608 | tf_op jit(solution)/shard_map/all_to_all | solution.py:201
  68.4 3.6 gather_fusion.2
  71.9 2.5 copy.118
  75.4 45.8 %all-gather.6.cloned.1.call-done = bf16[2,512,2048]{1,2,0:T(8,128)(2,1)} async-done(((bf16[2,512,512]{1,2,0:T(8,128)(2,1)}), bf16[2,512,2048]{1,2,0:T(8,128)(2,1)}) %all-gather.6.cloned.1.call-update) | async-done | bytes 4194320 | tf_op jit(solution)/shard_map/all_gather | solution.py:211
  123.7 1.7 slice_bitcast_fusion
  125.4 2.5 copy.119
  127.9 2.1 fusion.57
  130.0 3.6 fusion.66
  134.3 2.9 fusion.80
  137.3 2.9 convolution_bitcast_fusion.2
  141.6 24.0 %while.32 = (s32[]{:T(128)}, bf16[8,512,64]{1,2,0:T(8,128)(2,1)S(1)}, f32[8,512]{1,0:T(8,128)}, bf16[8,512,64]{2,1,0:T(8,128)(2,1)S(1)}, bf16[1,512,64]{2,1,0:T(...) while((s32[]{:T(128)}, bf16[8,512,64]{1,2,0:T(8,128)(2,1)S(1)}, ...), condition=%wide.region_8.9_spmd.clone.clone, body=%wide.region_5.8_spmd.clone.sunk.clone | while | flops 69991936 | bytes 3695189 | solution.py:241
  166.4 3.1 fusion.73
  169.5 28.3 %all-gather.8.cloned.1.call-done = bf16[2048,4224]{1,0:T(8,128)(2,1)} async-done(((bf16[64,4224]{1,0:T(8,128)(2,1)}), bf16[2048,4224]{1,0:T(8,128)(2,1)}) %all-gather.8.cloned.1.call-update) | async-done | bytes 17301520 | tf_op jit(solution)/shard_map/all_gather | solution.py:215
  197.8 2.5 copy.125
  200.6 8.4 %fusion.54 = f32[512,1408]{1,0:T(8,128)} fusion(bf16[2048,4224]{1,0:T(8,128)(2,1)} %all-gather.8.cloned.1.call-done, bf16[2,512,2048]{1,2,0:T(8,128)(2,1)} %all-gather.6.cloned.1.call-done), kind=kOutput, calls=%fused_computation.76 | convolution fusion | flops 2952790016 | bytes 10747904 | tf_op jit(solution)/shard_map/dot_general | solution.py:68
  208.9 49.6 %all-reduce.4.cloned.1.call-done = bf16[512,2048]{0,1:T(8,128)(2,1)} async-done(((bf16[512,2048]{0,1:T(8,128)(2,1)}), bf16[512,2048]{0,1:T(8,128)(2,1)}) %all-reduce.4.cloned.1.call-update) | async-done | bytes 2097168 | tf_op jit(solution)/shard_map/psum | solution.py:258
  258.6 3.1 multiply_reduce_fusion.4
  262.0 3.5 fusion.41
  265.6 5.8 fusion.50
  271.4 2.0 copy-done.35
  274.2 6.1 multiply_convert_fusion.5
  281.5 4.6 fusion.62
  286.2 6.0 fusion.44
  292.3 7.5 %add_convert_fusion.1 = bf16[512,2048]{0,1:T(8,128)(2,1)} fusion(f32[512,2048]{0,1:T(8,128)S(1)} %fusion.44, bf16[512,1408]{1,0:T(8,128)(2,1)S(1)} %copy-done.11, bf16[2048,4224]{1,0:T(8,128)(2,1)} %all-gather.8.cloned.1.call-done), kind=kOutput, calls=%fused_computation.90 | convolution fusion | flops 2954887168 | bytes 13500416 | tf_op jit(solution)/shard_map/dot_general | solution.py:68
  299.8 16.0 %reduce-scatter.4.cloned.1.call-done = bf16[512,512]{0,1:T(8,128)(2,1)} async-done(((bf16[512,2048]{0,1:T(8,128)(2,1)}), bf16[512,512]{0,1:T(8,128)(2,1)}) %reduce-scatter.4.cloned.1.call-update) | async-done | bytes 524304 | tf_op jit(solution)/shard_map/reduce_scatter | solution.py:268
  316.1 1.7 slice_bitcast_fusion.1
  317.8 2.5 pad_maximum_fusion.1.left_ref
  321.5 2.2 pad_maximum_fusion.right_ref
  323.7 34.0 %shard_map.230 = bf16[2048,4224]{1,0:T(8,128)(2,1)} custom-call(s32[33]{0:T(128)} %constant.125.clone.select_ref, bf16[2,2048,512]{2,1,0:T(8,128)(2,1)} %pad_maximum_fusion.1.left_ref, bf16[512,4224]{1,0:T(8,128)(2,1)} %pad_maximum_fusion.right_ref), custom_call_target="tpu_custom_call" | custom-call | tf_op jit(solution)/shard_map/pallas_call | solution.py:167
  357.8 18.6 %all-reduce.6.cloned.1.call-done = bf16[512,2048]{0,1:T(8,128)(2,1)} async-done(((bf16[512,2048]{0,1:T(8,128)(2,1)}), bf16[512,2048]{0,1:T(8,128)(2,1)}) %all-reduce.6.cloned.1.call-update) | async-done | bytes 2097168 | tf_op jit(solution)/shard_map/psum | solution.py:281
  376.4 4.2 convert_element_type.150
  382.2 4.4 multiply_reduce_fusion.1
  387.6 2.5 convert_bitcast_fusion.1
  390.0 2.0 copy-done.5
  392.1 4.0 fusion.77
  397.6 37.3 %while.33 = (s32[]{:T(128)}, f32[8,512,64]{1,2,0:T(8,128)}, f32[8,512,64]{1,2,0:T(8,128)S(1)}, f32[8,512,64]{1,2,0:T(8,128)}, bf16[8,512,64]{2,1,0:T(8,128)(2,1)...) while((s32[]{:T(128)}, f32[8,512,64]{1,2,0:T(8,128)}, ...), condition=%wide.region_16.17_spmd.clone.clone, body=%wide.region_14.16_spmd.clone.sunk.clone | while | flops 170982912 | bytes 9127021 | solution.py:294
  435.1 1.9 reduce_sum.96
  437.1 1.9 fusion.106
  439.4 1.7 fusion.90
  441.1 1.8 fusion.87
  442.9 4.5 add_convert_fusion
  447.4 50.6 %reduce-scatter.6.cloned.1.call-done = bf16[64,4224]{1,0:T(8,128)(2,1)} async-done(((bf16[2048,4224]{1,0:T(8,128)(2,1)}), bf16[64,4224]{1,0:T(8,128)(2,1)}) %reduce-scatter.6.cloned.1.call-update) | async-done | bytes 540688 | tf_op jit(solution)/shard_map/reduce_scatter | solution.py:289
  499.2 1.9 concatenate.61.right_ref
  501.2 57.4 %all-reduce.8.cloned.1.call-done = bf16[512,2048]{0,1:T(8,128)(2,1)} async-done(((bf16[512,2048]{0,1:T(8,128)(2,1)}), bf16[512,2048]{0,1:T(8,128)(2,1)}) %all-reduce.8.cloned.1.call-update) | async-done | bytes 2097168 | tf_op jit(solution)/shard_map/psum | solution.py:323
  558.5 5.7 fusion.56
  564.6 2.4 pad_maximum_fusion.2.left_ref
  568.2 11.8 %shard_map.231 = bf16[2048,1280]{1,0:T(8,128)(2,1)} custom-call(s32[10]{0:T(128)} %constant.126.clone.select_ref, bf16[2,2048,512]{2,1,0:T(8,128)(2,1)} %pad_maximum_fusion.2.left_ref, bf16[512,1152]{1,0:T(8,128)(2,1)} %concatenate.61.right_ref, bf16[2048,128]{1,0:T(8,128)(2,1)} %maximum_maximum_fusion.tail_ref), custom_call_target="tpu_custom_call" | custom-call | tf_op jit(solution)/shard_map/pallas_call | solution.py:167
  582.4 2.3 fusion.86
  585.8 4.1 gather_fusion.3
  589.9 7.3 %all-to-all-start.2 = ((bf16[2,512,512]{2,0,1:T(2,128)(2,1)}), bf16[2,512,512]{2,0,1:T(2,128)(2,1)S(1)}, u32[]{:S(2)}, u32[]{:S(2)}) async-start(bf16[2,512,512]{2,0,1:T(2,128)(2,1)} %bitcast.33), calls=%async_computation.4 | async-start | bytes 2097152 | tf_op jit(solution)/shard_map/all_to_all | solution.py:350
  597.2 3.8 sort.47
  602.0 12.5 %all-to-all-done.2 = bf16[2,512,512]{2,0,1:T(2,128)(2,1)S(1)} async-done(((bf16[2,512,512]{2,0,1:T(2,128)(2,1)}), bf16[2,512,512]{2,0,1:T(2,128)(2,1)S(1)}, u32[]{:S(2)}, u32[]{:S(2)}) %all-to-all-start.2) | async-done | bytes 1048608 | tf_op jit(solution)/shard_map/all_to_all | solution.py:350
  616.3 2.6 gather_fusion.5
  618.9 2.6 gather_fusion.4
  621.5 43.2 %reduce-scatter.8.cloned.1.call-done = bf16[64,1280]{1,0:T(8,128)(2,1)} async-done(((bf16[2048,1280]{1,0:T(8,128)(2,1)}), bf16[64,1280]{1,0:T(8,128)(2,1)}) %reduce-scatter.8.cloned.1.call-update) | async-done | bytes 163856 | tf_op jit(solution)/shard_map/reduce_scatter | solution.py:327
  (255 shorter events, 93.3 us)
Async XLA Ops:
  7.2 21.4 %copy-start.17 = (bf16[512,512]{1,0:T(8,128)(2,1)S(1)}, bf16[512,512]{1,0:T(8,128)(2,1)}, u32[]{:S(2)}) copy-start(bf16[512,512]{1,0:T(8,128)(2,1)} %param.20) | copy-start | bytes 1572868
  7.2 67.2 %all-gather.4.cloned.1.call-start = ((), (), s32[]{:S(2)}) async-start(), calls=%async_computation.6 | async-start | bytes 4866048 | tf_op jit(solution)/shard_map/all_gather | solution.py:115
  13.4 0.6 copy-start.32
  18.3 17.7 %all-to-all-start.1 = ((s32[32,16,1]{1,2,0:T(1,128)}), s32[32,16,1]{1,2,0:T(1,128)S(1)}, u32[]{:S(2)}, u32[]{:S(2)}) async-start(s32[32,16,1]{1,2,0:T(1,128)} %bitcast.3), calls=%async_computation.1 | async-start | bytes 32768 | tf_op jit(solution)/shard_map/all_to_all | solution.py:204
  36.0 38.5 %copy-start.19 = (bf16[64,1408]{1,0:T(8,128)(2,1)S(1)}, bf16[64,1408]{1,0:T(8,128)(2,1)}, u32[]{:S(2)}) copy-start(bf16[64,1408]{1,0:T(8,128)(2,1)} %param.31) | copy-start | bytes 540676
  36.0 38.5 %copy-start.20 = (bf16[64,1408]{1,0:T(8,128)(2,1)S(1)}, bf16[64,1408]{1,0:T(8,128)(2,1)}, u32[]{:S(2)}) copy-start(bf16[64,1408]{1,0:T(8,128)(2,1)} %param.30) | copy-start | bytes 540676
  36.0 38.5 %copy-start.21 = (bf16[64,1408]{1,0:T(8,128)(2,1)S(1)}, bf16[64,1408]{1,0:T(8,128)(2,1)}, u32[]{:S(2)}) copy-start(bf16[64,1408]{1,0:T(8,128)(2,1)} %param.29) | copy-start | bytes 540676
  36.0 85.8 %copy-start.31 = (s32[512]{0:T(512)S(1)}, s32[512]{0:T(512)}, u32[]{:S(2)}) copy-start(s32[512]{0:T(512)} %param.22) | copy-start | bytes 6148
  36.0 32.4 %all-to-all-start = ((bf16[2,512,512]{2,0,1:T(2,128)(2,1)}), bf16[2,512,512]{2,0,1:T(2,128)(2,1)S(1)}, u32[]{:S(2)}, u32[]{:S(2)}) async-start(bf16[2,512,512]{2,0,1:T(2,128)(2,1)} %bitcast.2), calls=%async_computation | async-start | bytes 2097152 | tf_op jit(solution)/shard_map/all_to_all | solution.py:201
  43.6 77.7 %all-gather.6.cloned.1.call-start = ((), (), s32[]{:S(2)}) async-start(), calls=%async_computation.7 | async-start | bytes 5242880 | tf_op jit(solution)/shard_map/all_gather | solution.py:211
  74.5 123.4 %all-gather.8.cloned.1.call-start = ((), (), s32[]{:S(2)}) async-start(), calls=%async_computation.8 | async-start | bytes 17842176 | tf_op jit(solution)/shard_map/all_gather | solution.py:215
  121.2 137.4 %all-reduce.4.cloned.1.call-start = ((), (), s32[]{:S(2)}) async-start(), calls=%async_computation.9 | async-start | bytes 4194304 | tf_op jit(solution)/shard_map/psum | solution.py:258
  122.4 17.8 %copy-start.34 = (f32[32]{0:T(128)}, f32[32]{0:T(128)S(1)}, u32[]{:S(2)}) copy-start(f32[32]{0:T(128)S(1)} %negate_power_fusion) | copy-start | bytes 388
  123.4 16.8 %copy-start.23 = (f32[512]{0:T(512)}, f32[512]{0:T(512)S(1)}, u32[]{:S(2)}) copy-start(f32[512]{0:T(512)S(1)} %fusion.112) | copy-start | bytes 6148
  125.4 4.6 copy-start.29
  130.0 7.3 %copy-start.26 = (f32[512]{0:T(512)}, f32[512]{0:T(512)S(1)}, u32[]{:S(2)}) copy-start(f32[512]{0:T(512)S(1)} %add_rsqrt_fusion.1) | copy-start | bytes 6148
  137.3 4.2 copy-start.7
  165.6 0.8 copy-start.8
  200.3 115.4 %reduce-scatter.4.cloned.1.call-start = ((), (), s32[]{:S(2)}) async-start(), calls=%async_computation.10 | async-start | bytes 2621440 | tf_op jit(solution)/shard_map/reduce_scatter | solution.py:268
  258.6 3.4 copy-start
  262.0 3.6 copy-start.24
  265.6 7.8 %copy-start.35 = (bf16[2048,4224]{1,0:T(8,128)(2,1)S(1)}, bf16[2048,4224]{1,0:T(8,128)(2,1)}, u32[]{:S(2)}) copy-start(bf16[2048,4224]{1,0:T(8,128)(2,1)} %all-gather.8.cloned.1.call-done) | copy-start | bytes 51904516
  265.6 8.6 %copy-start.36 = (f32[512,1408]{1,0:T(8,128)S(1)}, f32[512,1408]{1,0:T(8,128)}, u32[]{:S(2)}) copy-start(f32[512,1408]{1,0:T(8,128)} %fusion.54) | copy-start | bytes 8650756
  280.4 1.2 copy-start.13
  286.2 90.2 %all-reduce.6.cloned.1.call-start = ((), (), s32[]{:S(2)}) async-start(), calls=%async_computation.11 | async-start | bytes 4194304 | tf_op jit(solution)/shard_map/psum | solution.py:281
  286.2 6.0 copy-start.11
  315.8 182.2 %reduce-scatter.6.cloned.1.call-start = ((), (), s32[]{:S(2)}) async-start(), calls=%async_computation.12 | async-start | bytes 17842176 | tf_op jit(solution)/shard_map/reduce_scatter | solution.py:289
  317.8 2.5 copy-start.10
  317.8 2.9 copy-start.12
  317.8 3.7 copy-start.14
  380.6 1.6 copy-start.3
  380.6 177.9 %all-reduce.8.cloned.1.call-start = ((), (), s32[]{:S(2)}) async-start(), calls=%async_computation.13 | async-start | bytes 4194304 | tf_op jit(solution)/shard_map/psum | solution.py:323
  382.2 4.4 copy-start.1
  382.2 5.4 copy-start.2
  382.2 5.4 copy-start.22
  382.2 5.4 copy-start.25
  390.0 2.0 copy-start.5
  392.1 5.5 copy-start.15
  434.9 4.2 copy-start.16
  442.9 55.5 %copy-start.9 = (bf16[8,512,64]{1,2,0:T(8,128)(2,1)S(1)}, bf16[8,512,64]{1,2,0:T(8,128)(2,1)}, u32[]{:S(2)}) copy-start(bf16[8,512,64]{1,2,0:T(8,128)(2,1)} %copy-done.8) | copy-start | bytes 1572868
  447.4 51.5 %copy-start.28 = (bf16[2048]{0:T(1024)(128)(2,1)S(1)}, bf16[2048]{0:T(1024)(128)(2,1)}, u32[]{:S(2)}) copy-start(bf16[2048]{0:T(1024)(128)(2,1)} %get-tuple-element.305) | copy-start | bytes 12292
  447.4 111.1 %copy-start.27 = (f32[512]{0:T(512)S(1)}, f32[512]{0:T(512)}, u32[]{:S(2)}) copy-start(f32[512]{0:T(512)} %copy-done.26) | copy-start | bytes 6148
  447.4 111.1 %copy-start.30 = (f32[2048]{0:T(1024)S(1)}, f32[2048]{0:T(1024)}, u32[]{:S(2)}) copy-start(f32[2048]{0:T(1024)} %param.23) | copy-start | bytes 24580
  498.1 166.7 %reduce-scatter.8.cloned.1.call-start = ((), (), s32[]{:S(2)}) async-start(), calls=%async_computation.14 | async-start | bytes 5406720 | tf_op jit(solution)/shard_map/reduce_scatter | solution.py:327
  501.2 63.4 %copy-start.4 = (bf16[1,2048,512]{2,1,0:T(8,128)(2,1)S(1)}, bf16[1,2048,512]{2,1,0:T(8,128)(2,1)}, u32[]{:S(2)}) copy-start(bf16[1,2048,512]{2,1,0:T(8,128)(2,1)} %get-tuple-element.345) | copy-start | bytes 6291460
  580.0 1.0 copy-start.18
  584.7 12.5 %copy-start.33 = (s32[512]{0:T(512)S(1)}, s32[512]{0:T(512)}, u32[]{:S(2)}) copy-start(s32[512]{0:T(512)} %copy-done.32) | copy-start | bytes 6148
  584.7 16.3 %copy-start.6 = (bf16[64,4224]{1,0:T(8,128)(2,1)S(1)}, bf16[64,4224]{1,0:T(8,128)(2,1)}, u32[]{:S(2)}) copy-start(bf16[64,4224]{1,0:T(8,128)(2,1)} %reduce-scatter.6.cloned.1.call-done) | copy-start | bytes 1622020
  589.9 24.6 %all-to-all-start.2 = ((bf16[2,512,512]{2,0,1:T(2,128)(2,1)}), bf16[2,512,512]{2,0,1:T(2,128)(2,1)S(1)}, u32[]{:S(2)}, u32[]{:S(2)}) async-start(bf16[2,512,512]{2,0,1:T(2,128)(2,1)} %bitcast.33), calls=%async_computation.4 | async-start | bytes 2097152 | tf_op jit(solution)/shard_map/all_to_all | solution.py:350
Sparse Core Ops, SparseCore 0:
  10.8 59.7 all-gather.3
  74.6 46.5 all-gather.5
  123.5 74.2 all-gather.7
  200.5 58.0 all-reduce.3
  286.3 29.4 reduce-scatter.3
  318.0 58.3 all-reduce.5
  380.9 117.1 reduce-scatter.5
  500.5 57.9 all-reduce.7
  580.1 84.6 reduce-scatter.7

commit v5 on v4

--- a/solution.py
+++ b/solution.py
@@ -109,6 +109,25 @@
         pieces.append(packed[:, offset : offset + width])
         offset += width
     return pieces
+
+
+def col_scatter(values):
+    count = lax.axis_size("col")
+    lead = values.shape[:-1]
+    blocks = jnp.moveaxis(values.reshape(*lead, count, values.shape[-1] // count), -2, 0)
+    received = lax.all_to_all(blocks, "col", split_axis=0, concat_axis=0, tiled=True)
+    return jnp.sum(received.astype(jnp.float32), axis=0)
+
+
+def col_gather(block):
+    count = lax.axis_size("col")
+    copies = jnp.broadcast_to(block[None], (count,) + block.shape)
+    received = lax.all_to_all(copies, "col", split_axis=0, concat_axis=0, tiled=True)
+    return jnp.moveaxis(received, 0, -2).reshape(*block.shape[:-1], count * block.shape[-1])
+
+
+def col_sum(values):
+    return col_gather(col_scatter(values).astype(jnp.bfloat16)).astype(jnp.float32)
 
 
 def gather_rows(parts):
@@ -207,12 +226,8 @@
     attn_widths = [w_query.shape[1], w_key.shape[1], w_value.shape[1], w_output.shape[1]]
     ffn_widths = [w_gate.shape[1], w_up.shape[1], w_down.shape[1]]
     attn_packed = gather_rows([w_query, w_key, w_value, w_output])
-    placed_pair, attn_packed = lax.optimization_barrier((arrived_pair[:, placing], attn_packed))
-    full_pair = lax.all_gather(placed_pair, "col", axis=2, tiled=True)
-    ffn_local, full_pair = lax.optimization_barrier(
-        (jnp.concatenate([w_gate, w_up, w_down], axis=1), full_pair)
-    )
-    ffn_packed = lax.all_gather(ffn_local, "row", axis=0, tiled=True)
+    ffn_packed = gather_rows([w_gate, w_up, w_down])
+    full_pair = col_gather(arrived_pair[:, placing])
     full_rows, full_grads = full_pair[0], full_pair[1]
     query_w, key_w, value_w, output_w = split_columns(attn_packed, attn_widths)
     cosine, sine = rope_tables(positions_of(segment_ids))
@@ -254,8 +269,7 @@
         .astype(jnp.bfloat16)
     )
     attn_terms = matmul(mixed, output_w.T)
-    attn_terms, ffn_packed = lax.optimization_barrier((attn_terms, ffn_packed))
-    attn_full = lax.psum(attn_terms.astype(jnp.bfloat16), "col").astype(jnp.float32)
+    attn_full = col_sum(attn_terms.astype(jnp.bfloat16))
     resid = rows_wide + attn_full
     inv_two = rms_scale(resid)
     normed_two = (resid * inv_two * ffn_gain).astype(jnp.bfloat16)
@@ -265,25 +279,19 @@
     upper = matmul(normed_two, up_w)
     sigmoid_gate = jax.nn.sigmoid(gate)
     activ = (gate * sigmoid_gate * upper).astype(jnp.bfloat16)
-    ffn_share_low = lax.psum_scatter(
-        matmul(activ, down_w.T).astype(jnp.bfloat16), "col", scatter_dimension=1, tiled=True
-    )
+    ffn_share = col_scatter(matmul(activ, down_w.T).astype(jnp.bfloat16))
     act_grad = matmul(full_grads, down_w)
     gate_grad = (act_grad * upper * sigmoid_gate * (1.0 + gate * (1.0 - sigmoid_gate))).astype(
         jnp.bfloat16
     )
     up_grad = (act_grad * gate * sigmoid_gate).astype(jnp.bfloat16)
     normed_terms_two = matmul(gate_grad, gate_w.T) + matmul(up_grad, up_w.T)
-    normed_low_two, ffn_share_low = lax.optimization_barrier(
-        (normed_terms_two.astype(jnp.bfloat16), ffn_share_low)
-    )
-    output_share = (resid_part + ffn_share_low.astype(jnp.float32)).astype(jnp.bfloat16)
-    normed_grad_two = lax.psum(normed_low_two, "col").astype(jnp.float32)
+    output_share = (resid_part + ffn_share.astype(jnp.bfloat16).astype(jnp.float32)).astype(
+        jnp.bfloat16
+    )
+    normed_grad_two = col_sum(normed_terms_two.astype(jnp.bfloat16))
     ffn_grads_packed = packed_weight_grads(
         [normed_two, full_grads], [(0, gate_grad), (0, up_grad), (1, activ)]
-    )
-    ffn_grads_packed, normed_grad_two = lax.optimization_barrier(
-        (ffn_grads_packed, normed_grad_two)
     )
     resid_norm_grad, ffn_gain_grad = norm_back(resid, inv_two, ffn_gain, normed_grad_two)
     ffn_grads_local = lax.psum_scatter(ffn_grads_packed, "row", scatter_dimension=0, tiled=True)
@@ -317,10 +325,7 @@
     normed_terms_one = (
         matmul(query_grad, query_w.T) + matmul(key_grad, key_w.T) + matmul(value_grad, value_w.T)
     )
-    normed_low_one, ffn_grads_local = lax.optimization_barrier(
-        (normed_terms_one.astype(jnp.bfloat16), ffn_grads_local)
-    )
-    normed_grad_one = lax.psum(normed_low_one, "col").astype(jnp.float32)
+    normed_grad_one = col_sum(normed_terms_one.astype(jnp.bfloat16))
     rows_norm_grad, attn_gain_grad = norm_back(rows_wide, inv_one, attn_gain, normed_grad_one)
     rows_grad = resid_grad + rows_norm_grad
     input_share = lax.dynamic_slice_in_dim(rows_grad, col_start, quarter, 1).astype(jnp.bfloat16)

time: 687 us -> 717 us (1.044)
  waiting for transfers between devices: 342 us -> 225 us
  blocking collectives: 0 us -> 74.3 us
  starting transfers between devices: 24.7 us -> 69.9 us
  other arithmetic: 66.3 us -> 83.7 us
  local copies, waits for them, and re-layouts: 78.9 us -> 89.9 us
    psum x3 -> x0, waiting for transfers between devices: 126 us -> none  [the longest x1 57.4 us: body(): normed_grad_one = lax.psum(normed_low_one, 'col').astype(jnp.float32)]
    all_to_all x0 -> x5, waiting for transfers between devices: none -> 111 us  [the longest x4 94.1 us: col_gather(): lax.all_to_all(copies, 'col', split_axis=0, concat_axis=0, tiled=True)]
    all_to_all x0 -> x3, blocking collectives: none -> 74.3 us  [col_scatter(): lax.all_to_all(blocks, 'col', split_axis=0, concat_axis=0, tiled=True)]
    all_gather x2 -> x0, waiting for transfers between devices: 74.2 us -> none  [the longest x1 45.8 us: body(): full_pair = lax.all_gather(placed_pair, 'col', axis=2, tiled=True)]
    reduce_scatter x1, waiting for transfers between devices: 43.2 us -> 0.01 us  [body(): lax.psum_scatter(packed_weight_grads([normed_one, attn_grad_low], [(0, qu...]
    reduce_scatter x1, waiting for transfers between devices: 50.6 us -> 80.5 us  [body(): lax.psum_scatter(ffn_grads_packed, 'row', scatter_dimension=0, tiled=True)]
    all_to_all x1, starting transfers between devices: 7.28 us -> 31.6 us  [body(): lax.all_to_all(jnp.stack([output_share, input_share])[:, arrived_slots],...]
    all_to_all x0 -> x5, starting transfers between devices: none -> 22.1 us  [the longest x4 17.6 us: col_gather(): lax.all_to_all(copies, 'col', split_axis=0, concat_axis=0, tiled=True)]
  transfers between devices with their start and end apart: 12 -> 12, of which waited for: 10 -> 8; matrix products, arithmetic and copies ran while one was open for 28% -> 23% of each run, Pallas kernels for 5% -> 5%
where the time goes in v5:
time: 717 us; the launch traced here: 705 us
  waiting for transfers between devices  225 us (31%)
  matrix products  102 us (14%)
  local copies, waits for them, and re-layouts  89.9 us (13%)
  other arithmetic  83.7 us (12%)
  blocking collectives  74.3 us (10%)
  starting transfers between devices  69.9 us (10%)
  Pallas kernels  45.9 us (6%)
  between operations  15 us (2%)
    dot_general x70, matrix products, matmul(): return jnp.dot(left, right, preferred_element_type=jnp.float32)  102 us
    all_to_all x4, waiting for transfers between devices, col_gather(): lax.all_to_all(copies, 'col', split_axis=0, concat_axis=0, tiled=True)  94.1 us
    reduce_scatter x1, waiting for transfers between devices, body(): lax.psum_scatter(ffn_grads_packed, 'row', scatter_dimension=0, tiled=True)  80.5 us
    all_to_all x3, blocking collectives, col_scatter(): lax.all_to_all(blocks, 'col', split_axis=0, concat_axis=0, tiled=True)  74.3 us
    pallas_call x2, Pallas kernels, packed_weight_grads(): pl.pallas_call(kernel, out_shape=jax.ShapeDtypeStruct((features, len(sele...  45.9 us
    all_to_all x1, starting transfers between devices, body(): lax.all_to_all(jnp.stack([output_share, input_share])[:, arrived_slots],...  31.6 us
    all_to_all x1, waiting for transfers between devices, body(): lax.all_to_all(jnp.stack([tokens, cotangent])[:, send_order], 'row', spli...  19.6 us
    all_to_all x4, starting transfers between devices, col_gather(): lax.all_to_all(copies, 'col', split_axis=0, concat_axis=0, tiled=True)  17.6 us
  transfers between devices with their start and end apart: 12, of which 8 were waited for; matrix products, arithmetic and copies ran while one was open for 23% of the time, Pallas kernels for 5%

profile of v5, /device:TPU:0, one launch (start us, length us, event | category | flops | bytes accessed | tf_op | source)
XLA Modules:
  0.0 705.3 jit_solution(2501393625350336206)
XLA Ops:
  11.0 4.4 sort.45
  16.0 3.6 gather_fusion.1
  20.4 8.4 %all-to-all-start.1 = ((s32[32,16,1]{1,2,0:T(1,128)}), s32[32,16,1]{1,2,0:T(1,128)S(1)}, u32[]{:S(2)}, u32[]{:S(2)}) async-start(s32[32,16,1]{1,2,0:T(1,128)} %bitcast.3), calls=%async_computation.1 | async-start | bytes 32768 | tf_op jit(solution)/shard_map/all_to_all | solution.py:223
  30.5 2.4 pad_maximum_fusion.3
  32.9 4.1 gather_fusion
  37.0 7.4 %all-to-all-start = ((bf16[2,512,512]{2,0,1:T(2,128)(2,1)}), bf16[2,512,512]{2,0,1:T(2,128)(2,1)S(1)}, u32[]{:S(2)}, u32[]{:S(2)}) async-start(bf16[2,512,512]{2,0,1:T(2,128)(2,1)} %bitcast.2), calls=%async_computation | async-start | bytes 2097152 | tf_op jit(solution)/shard_map/all_to_all | solution.py:220
  45.7 3.8 sort.46
  49.5 19.6 %all-to-all-done = bf16[2,512,512]{2,0,1:T(2,128)(2,1)S(1)} async-done(((bf16[2,512,512]{2,0,1:T(2,128)(2,1)}), bf16[2,512,512]{2,0,1:T(2,128)(2,1)S(1)}, u32[]{:S(2)}, u32[]{:S(2)}) %all-to-all-start) | async-done | bytes 1048608 | tf_op jit(solution)/shard_map/all_to_all | solution.py:220
  69.1 3.6 gather_fusion.2
  74.1 2.4 broadcast_in_dim.100
  76.5 5.5 all-to-all-start.2
  84.1 45.7 %all-to-all-done.2 = bf16[4,2,512,512]{2,3,1,0:T(8,128)(2,1)} async-done(((bf16[4,2,512,512]{2,3,1,0:T(8,128)(2,1)}), bf16[4,2,512,512]{2,3,1,0:T(8,128)(2,1)}, u32[]{:S(2)}, u32[]{:S(2)}) %all-to-all-start.2) | async-done | bytes 4194336 | tf_op jit(solution)/shard_map/all_to_all | solution.py:125
  129.8 2.2 fusion.61
  132.0 3.8 fusion.63
  135.7 4.8 multiply_convert_fusion.2
  142.5 2.6 copy.105
  145.0 3.6 fusion.119
  156.2 28.8 %while.32 = (s32[]{:T(128)}, bf16[8,512,64]{1,2,0:T(8,128)(2,1)}, f32[8,512]{1,0:T(8,128)}, bf16[8,512,64]{2,1,0:T(8,128)(2,1)S(1)}, bf16[1,512,64]{2,1,0:T(8,12...) while((s32[]{:T(128)}, bf16[8,512,64]{1,2,0:T(8,128)(2,1)}, ...), condition=%wide.region_8.9_spmd.clone.clone, body=%wide.region_5.8_spmd.clone.sunk.clone | while | flops 69991936 | bytes 3629153 | solution.py:256
  185.0 3.1 convolution_convert_fusion
  188.3 26.5 %all_to_all.62 = bf16[4,512,512]{2,1,0:T(8,128)(2,1)S(1)} all-to-all(bf16[4,512,512]{2,1,0:T(8,128)(2,1)S(1)} %bitcast.314), channel_id=1, replica_groups=mesh['row'=32,'col'=4] {'col'}, dimensions={0} | all-to-all | bytes 4194304 | tf_op jit(solution)/shard_map/all_to_all | solution.py:118
  218.7 3.8 all-to-all-start.4
  222.5 3.0 slice.155
  225.5 20.0 %all-to-all-done.4 = bf16[4,512,512]{1,2,0:T(8,128)(2,1)S(1)} async-done(((bf16[4,512,512]{1,2,0:T(8,128)(2,1)}), bf16[4,512,512]{1,2,0:T(8,128)(2,1)S(1)}, u32[]{:S(2)}, u32[]{:S(2)}) %all-to-all-start.4) | async-done | bytes 2097184 | tf_op jit(solution)/shard_map/all_to_all | solution.py:125
  245.5 2.3 fusion.57
  248.5 3.7 multiply_convert_fusion.1
  252.1 6.4 fusion.41
  258.6 2.4 copy-done.31
  261.0 5.1 fusion.51
  266.1 7.2 %multiply_convert_fusion.5 = (bf16[512,1408]{1,0:T(8,128)(2,1)}, bf16[512,1408]{1,0:T(8,128)(2,1)S(1)}, bf16[512,1408]{1,0:T(8,128)(2,1)S(1)}) fusion(f32[512,1408]{1,0:T(8,128)} %fusion.51, f32[512,1408]{1,0:T(8,128)S(1)} %fusion.41, bf16[512,2048]{0,1:T(8,128)(2,1)S(1)} %copy-done.1, bf16[2048,4224]{1,0:T(8,128)(2,1)S(1)} %copy-done.31), kind=kOutput, calls=%fused_computation.110 | convolution fusion | flops 2964324352 | bytes 17956864 | tf_op jit(solution)/shard_map/dot_general | solution.py:68
  273.3 5.0 fusion.45
  278.3 5.3 add_convert_fusion.1
  283.8 25.4 %all_to_all.63 = bf16[4,512,512]{2,1,0:T(8,128)(2,1)} all-to-all(bf16[4,512,512]{2,1,0:T(8,128)(2,1)S(1)} %bitcast.315), channel_id=1, replica_groups=mesh['row'=32,'col'=4] {'col'}, dimensions={0} | all-to-all | bytes 4194304 | tf_op jit(solution)/shard_map/all_to_all | solution.py:118
  309.2 2.9 reduce_sum.144
  312.0 2.0 copy.120
  314.1 2.6 broadcast_in_dim.103
  316.7 4.7 all-to-all-start.7
  322.6 20.0 %all-to-all-done.7 = bf16[4,512,512]{1,2,0:T(8,128)(2,1)} async-done(((bf16[4,512,512]{1,2,0:T(8,128)(2,1)}), bf16[4,512,512]{1,2,0:T(8,128)(2,1)}, u32[]{:S(2)}, u32[]{:S(2)}) %all-to-all-start.7) | async-done | bytes 2097184 | tf_op jit(solution)/shard_map/all_to_all | solution.py:125
  342.6 4.2 fusion.65
  346.8 5.0 convert_bitcast_fusion.1
  353.8 3.8 fusion.78
  359.2 37.3 %while.33 = (s32[]{:T(128)}, f32[8,512,64]{1,2,0:T(8,128)}, f32[8,512,64]{1,2,0:T(8,128)}, f32[8,512,64]{1,2,0:T(8,128)S(1)}, bf16[8,512,64]{2,1,0:T(8,128)(2,1)...) while((s32[]{:T(128)}, f32[8,512,64]{1,2,0:T(8,128)}, ...), condition=%wide.region_16.17_spmd.clone.clone, body=%wide.region_14.16_spmd.clone.sunk.clone | while | flops 170982912 | bytes 9126013 | solution.py:302
  400.9 2.9 fusion.76
  407.6 22.5 %all_to_all.64 = bf16[4,512,512]{2,1,0:T(8,128)(2,1)S(1)} all-to-all(bf16[4,512,512]{2,1,0:T(8,128)(2,1)S(1)} %bitcast.316), channel_id=1, replica_groups=mesh['row'=32,'col'=4] {'col'}, dimensions={0} | all-to-all | bytes 4194304 | tf_op jit(solution)/shard_map/all_to_all | solution.py:118
  432.4 3.6 all-to-all-start.9
  439.0 2.9 concatenate.60.right_ref
  442.0 4.6 pad_maximum_fusion.1.left_ref
  446.6 8.5 %all-to-all-done.9 = bf16[4,512,512]{1,2,0:T(8,128)(2,1)S(1)} async-done(((bf16[4,512,512]{1,2,0:T(8,128)(2,1)}), bf16[4,512,512]{1,2,0:T(8,128)(2,1)S(1)}, u32[]{:S(2)}, u32[]{:S(2)}) %all-to-all-start.9) | async-done | bytes 2097184 | tf_op jit(solution)/shard_map/all_to_all | solution.py:125
  455.1 3.5 fusion.58
  460.0 11.8 %shard_map.230 = bf16[2048,1280]{1,0:T(8,128)(2,1)} custom-call(s32[10]{0:T(128)} %constant.130.clone.select_ref, bf16[2,2048,512]{2,1,0:T(8,128)(2,1)} %pad_maximum_fusion.1.left_ref, bf16[512,1152]{1,0:T(8,128)(2,1)} %concatenate.60.right_ref, bf16[2048,128]{1,0:T(8,128)(2,1)} %maximum_maximum_fusion.tail_ref), custom_call_target="tpu_custom_call" | custom-call | tf_op jit(solution)/shard_map/pallas_call | solution.py:186
  471.9 4.7 pad_maximum_fusion.2.left_ref
  476.7 2.2 pad_maximum_fusion.right_ref
  478.9 34.1 %shard_map.231 = bf16[2048,4224]{1,0:T(8,128)(2,1)} custom-call(s32[33]{0:T(128)} %constant.129.clone.select_ref, bf16[2,2048,512]{2,1,0:T(8,128)(2,1)} %pad_maximum_fusion.2.left_ref, bf16[512,4224]{1,0:T(8,128)(2,1)} %pad_maximum_fusion.right_ref), custom_call_target="tpu_custom_call" | custom-call | tf_op jit(solution)/shard_map/pallas_call | solution.py:186
  513.0 6.5 fusion.70
  521.0 4.5 all-to-all-start.5
  526.4 16.9 %all-to-all-done.5 = bf16[4,512,512]{2,1,0:T(8,128)(2,1)} async-done(((bf16[4,512,512]{2,1,0:T(8,128)(2,1)}), bf16[4,512,512]{2,1,0:T(8,128)(2,1)}, u32[]{:S(2)}, u32[]{:S(2)}) %all-to-all-start.5) | async-done | bytes 2097184 | tf_op jit(solution)/shard_map/all_to_all | solution.py:118
  543.3 2.2 reduce_sum.143
  550.8 4.1 gather_fusion.3
  554.9 31.6 %all-to-all-start.10 = ((bf16[2,512,512]{2,0,1:T(2,128)(2,1)}), bf16[2,512,512]{2,0,1:T(2,128)(2,1)S(1)}, u32[]{:S(2)}, u32[]{:S(2)}) async-start(bf16[2,512,512]{2,0,1:T(2,128)(2,1)} %bitcast.43), calls=%async_computation.10 | async-start | bytes 2097152 | tf_op jit(solution)/shard_map/all_to_all | solution.py:355
  586.5 3.8 sort.47
  590.3 13.5 %all-to-all-done.10 = bf16[2,512,512]{2,0,1:T(2,128)(2,1)S(1)} async-done(((bf16[2,512,512]{2,0,1:T(2,128)(2,1)}), bf16[2,512,512]{2,0,1:T(2,128)(2,1)S(1)}, u32[]{:S(2)}, u32[]{:S(2)}) %all-to-all-start.10) | async-done | bytes 1048608 | tf_op jit(solution)/shard_map/all_to_all | solution.py:355
  605.6 2.6 gather_fusion.5
  608.3 2.6 gather_fusion.4
  615.7 80.5 %reduce-scatter.5.cloned.1.call-done = bf16[64,4224]{1,0:T(8,128)(2,1)} async-done(((bf16[2048,4224]{1,0:T(8,128)(2,1)}), bf16[64,4224]{1,0:T(8,128)(2,1)}) %reduce-scatter.5.cloned.1.call-update) | async-done | bytes 540688 | tf_op jit(solution)/shard_map/reduce_scatter | solution.py:297
  696.2 2.1 fusion.116
  (265 shorter events, 125.5 us)
Async XLA Ops:
  7.2 21.6 %copy-start.10 = (bf16[512,512]{1,0:T(8,128)(2,1)S(1)}, bf16[512,512]{1,0:T(8,128)(2,1)}, u32[]{:S(2)}) copy-start(bf16[512,512]{1,0:T(8,128)(2,1)} %param.19) | copy-start | bytes 1572868
  7.2 22.4 %copy-start.11 = (bf16[512,512]{1,0:T(8,128)(2,1)S(1)}, bf16[512,512]{1,0:T(8,128)(2,1)}, u32[]{:S(2)}) copy-start(bf16[512,512]{1,0:T(8,128)(2,1)} %param.20) | copy-start | bytes 1572868
  7.2 133.4 %all-gather.3.cloned.1.call-start = ((), (), s32[]{:S(2)}) async-start(), calls=%async_computation.13 | async-start | bytes 4866048 | tf_op jit(solution)/shard_map/all_gather | solution.py:134
  9.0 243.1 %all-gather.5.cloned.1.call-start = ((), (), s32[]{:S(2)}) async-start(), calls=%async_computation.14 | async-start | bytes 17842176 | tf_op jit(solution)/shard_map/all_gather | solution.py:134
  15.5 0.6 copy-start.27
  20.4 16.7 %all-to-all-start.1 = ((s32[32,16,1]{1,2,0:T(1,128)}), s32[32,16,1]{1,2,0:T(1,128)S(1)}, u32[]{:S(2)}, u32[]{:S(2)}) async-start(s32[32,16,1]{1,2,0:T(1,128)} %bitcast.3), calls=%async_computation.1 | async-start | bytes 32768 | tf_op jit(solution)/shard_map/all_to_all | solution.py:223
  37.0 32.0 %all-to-all-start = ((bf16[2,512,512]{2,0,1:T(2,128)(2,1)}), bf16[2,512,512]{2,0,1:T(2,128)(2,1)S(1)}, u32[]{:S(2)}, u32[]{:S(2)}) async-start(bf16[2,512,512]{2,0,1:T(2,128)(2,1)} %bitcast.2), calls=%async_computation | async-start | bytes 2097152 | tf_op jit(solution)/shard_map/all_to_all | solution.py:220
  76.5 5.6 copy-start.26
  76.5 6.1 copy-start.19
  76.5 53.2 %all-to-all-start.2 = ((bf16[4,2,512,512]{2,3,1,0:T(8,128)(2,1)}), bf16[4,2,512,512]{2,3,1,0:T(8,128)(2,1)}, u32[]{:S(2)}, u32[]{:S(2)}) async-start(bf16[4,2,512,512]{2,3,1,0:T(8,128)(2,1)} %broadcast_in_dim.100), calls=%async_computation.2 | async-start | bytes 8388608 | tf_op jit(solution)/shard_map/all_to_all | solution.py:125
  82.7 57.9 %copy-start.14 = (f32[4,512]{1,0:T(4,128)}, f32[4,512]{1,0:T(4,128)S(1)}, u32[]{:S(2)}) copy-start(f32[4,512]{1,0:T(4,128)S(1)} %mul.305) | copy-start | bytes 24580
  82.7 72.1 %copy-start.29 = (f32[32]{0:T(128)}, f32[32]{0:T(128)S(1)}, u32[]{:S(2)}) copy-start(f32[32]{0:T(128)S(1)} %negate_power_fusion) | copy-start | bytes 388
  83.8 71.1 %copy-start.20 = (f32[512]{0:T(512)}, f32[512]{0:T(512)S(1)}, u32[]{:S(2)}) copy-start(f32[512]{0:T(512)S(1)} %fusion.112) | copy-start | bytes 6148
  132.0 8.6 %copy-start.16 = (f32[512]{0:T(512)}, f32[512]{0:T(512)S(1)}, u32[]{:S(2)}) copy-start(f32[512]{0:T(512)S(1)} %add_rsqrt_fusion.1) | copy-start | bytes 6148
  145.0 6.1 copy-start.2
  218.7 26.8 %all-to-all-start.4 = ((bf16[4,512,512]{1,2,0:T(8,128)(2,1)}), bf16[4,512,512]{1,2,0:T(8,128)(2,1)S(1)}, u32[]{:S(2)}, u32[]{:S(2)}) async-start(bf16[4,512,512]{1,2,0:T(8,128)(2,1)} %broadcast_in_dim.102), calls=%async_computation.4 | async-start | bytes 4194304 | tf_op jit(solution)/shard_map/all_to_all | solution.py:125
  245.5 2.9 copy-start.12
  247.9 0.6 copy-start.22
  252.1 6.5 copy-start.1
  252.1 8.9 %copy-start.31 = (bf16[2048,4224]{1,0:T(8,128)(2,1)S(1)}, bf16[2048,4224]{1,0:T(8,128)(2,1)}, u32[]{:S(2)}) copy-start(bf16[2048,4224]{1,0:T(8,128)(2,1)} %all-gather.5.cloned.1.call-done) | copy-start | bytes 51904516
  273.3 5.0 copy-start.7
  273.3 5.0 copy-start.5
  316.7 25.9 %all-to-all-start.7 = ((bf16[4,512,512]{1,2,0:T(8,128)(2,1)}), bf16[4,512,512]{1,2,0:T(8,128)(2,1)}, u32[]{:S(2)}, u32[]{:S(2)}) async-start(bf16[4,512,512]{1,2,0:T(8,128)(2,1)} %broadcast_in_dim.103), calls=%async_computation.7 | async-start | bytes 4194304 | tf_op jit(solution)/shard_map/all_to_all | solution.py:125
  342.6 4.2 copy-start
  342.6 4.2 copy-start.13
  342.6 4.2 copy-start.23
  351.9 2.0 copy-start.3
  353.8 5.3 copy-start.9
  396.5 3.0 copy-start.21
  396.5 3.0 copy-start.30
  430.9 7.8 %copy-start.24 = (bf16[4,512]{1,0:T(4,128)(2,1)S(1)}, bf16[4,512]{1,0:T(4,128)(2,1)}, u32[]{:S(2)}) copy-start(bf16[4,512]{1,0:T(4,128)(2,1)} %get-tuple-element.281) | copy-start | bytes 12292
  432.4 22.7 %all-to-all-start.9 = ((bf16[4,512,512]{1,2,0:T(8,128)(2,1)}), bf16[4,512,512]{1,2,0:T(8,128)(2,1)S(1)}, u32[]{:S(2)}, u32[]{:S(2)}) async-start(bf16[4,512,512]{1,2,0:T(8,128)(2,1)} %broadcast_in_dim.104), calls=%async_computation.9 | async-start | bytes 4194304 | tf_op jit(solution)/shard_map/all_to_all | solution.py:125
  436.0 174.9 %reduce-scatter.3.cloned.1.call-start = ((), (), s32[]{:S(2)}) async-start(), calls=%async_computation.15 | async-start | bytes 5406720 | tf_op jit(solution)/shard_map/reduce_scatter | solution.py:332
  442.0 13.1 %copy-start.15 = (f32[4,512]{1,0:T(4,128)S(1)}, f32[4,512]{1,0:T(4,128)}, u32[]{:S(2)}) copy-start(f32[4,512]{1,0:T(4,128)} %copy-done.14) | copy-start | bytes 24580
  442.0 13.1 %copy-start.17 = (f32[512]{0:T(512)S(1)}, f32[512]{0:T(512)}, u32[]{:S(2)}) copy-start(f32[512]{0:T(512)} %copy-done.16) | copy-start | bytes 6148
  471.9 224.3 %reduce-scatter.5.cloned.1.call-start = ((), (), s32[]{:S(2)}) async-start(), calls=%async_computation.16 | async-start | bytes 17842176 | tf_op jit(solution)/shard_map/reduce_scatter | solution.py:297
  471.9 4.8 copy-start.4
  471.9 4.8 copy-start.6
  471.9 4.8 copy-start.8
  521.0 22.3 %all-to-all-start.5 = ((bf16[4,512,512]{2,1,0:T(8,128)(2,1)}), bf16[4,512,512]{2,1,0:T(8,128)(2,1)}, u32[]{:S(2)}, u32[]{:S(2)}) async-start(bf16[4,512,512]{2,1,0:T(8,128)(2,1)} %bitcast.313), calls=%async_computation.5 | async-start | bytes 4194304 | tf_op jit(solution)/shard_map/all_to_all | solution.py:118
  545.8 2.0 copy-start.25
  545.8 2.0 copy-start.18
  549.7 36.8 %copy-start.28 = (s32[512]{0:T(512)S(1)}, s32[512]{0:T(512)}, u32[]{:S(2)}) copy-start(s32[512]{0:T(512)} %copy-done.27) | copy-start | bytes 6148
  554.9 48.9 %all-to-all-start.10 = ((bf16[2,512,512]{2,0,1:T(2,128)(2,1)}), bf16[2,512,512]{2,0,1:T(2,128)(2,1)S(1)}, u32[]{:S(2)}, u32[]{:S(2)}) async-start(bf16[2,512,512]{2,0,1:T(2,128)(2,1)} %bitcast.43), calls=%async_computation.10 | async-start | bytes 2097152 | tf_op jit(solution)/shard_map/all_to_all | solution.py:355
Sparse Core Ops, SparseCore 0:
  10.9 59.4 all-gather.2
  72.6 72.4 all-gather.4
  472.0 102.9 reduce-scatter.2
  579.3 116.7 reduce-scatter.4

commit v6 on v5

--- a/solution.py
+++ b/solution.py
@@ -269,7 +269,8 @@
         .astype(jnp.bfloat16)
     )
     attn_terms = matmul(mixed, output_w.T)
-    attn_full = col_sum(attn_terms.astype(jnp.bfloat16))
+    attn_terms, ffn_packed = lax.optimization_barrier((attn_terms, ffn_packed))
+    attn_full = lax.psum(attn_terms.astype(jnp.bfloat16), "col").astype(jnp.float32)
     resid = rows_wide + attn_full
     inv_two = rms_scale(resid)
     normed_two = (resid * inv_two * ffn_gain).astype(jnp.bfloat16)
@@ -279,19 +280,25 @@
     upper = matmul(normed_two, up_w)
     sigmoid_gate = jax.nn.sigmoid(gate)
     activ = (gate * sigmoid_gate * upper).astype(jnp.bfloat16)
-    ffn_share = col_scatter(matmul(activ, down_w.T).astype(jnp.bfloat16))
+    ffn_share_low = lax.psum_scatter(
+        matmul(activ, down_w.T).astype(jnp.bfloat16), "col", scatter_dimension=1, tiled=True
+    )
     act_grad = matmul(full_grads, down_w)
     gate_grad = (act_grad * upper * sigmoid_gate * (1.0 + gate * (1.0 - sigmoid_gate))).astype(
         jnp.bfloat16
     )
     up_grad = (act_grad * gate * sigmoid_gate).astype(jnp.bfloat16)
     normed_terms_two = matmul(gate_grad, gate_w.T) + matmul(up_grad, up_w.T)
-    output_share = (resid_part + ffn_share.astype(jnp.bfloat16).astype(jnp.float32)).astype(
-        jnp.bfloat16
-    )
-    normed_grad_two = col_sum(normed_terms_two.astype(jnp.bfloat16))
+    normed_low_two, ffn_share_low = lax.optimization_barrier(
+        (normed_terms_two.astype(jnp.bfloat16), ffn_share_low)
+    )
+    output_share = (resid_part + ffn_share_low.astype(jnp.float32)).astype(jnp.bfloat16)
+    normed_grad_two = lax.psum(normed_low_two, "col").astype(jnp.float32)
     ffn_grads_packed = packed_weight_grads(
         [normed_two, full_grads], [(0, gate_grad), (0, up_grad), (1, activ)]
+    )
+    ffn_grads_packed, normed_grad_two = lax.optimization_barrier(
+        (ffn_grads_packed, normed_grad_two)
     )
     resid_norm_grad, ffn_gain_grad = norm_back(resid, inv_two, ffn_gain, normed_grad_two)
     ffn_grads_local = lax.psum_scatter(ffn_grads_packed, "row", scatter_dimension=0, tiled=True)
@@ -325,7 +332,9 @@
     normed_terms_one = (
         matmul(query_grad, query_w.T) + matmul(key_grad, key_w.T) + matmul(value_grad, value_w.T)
     )
-    normed_grad_one = col_sum(normed_terms_one.astype(jnp.bfloat16))
+    normed_grad_one, ffn_grads_local = lax.optimization_barrier(
+        (col_sum(normed_terms_one.astype(jnp.bfloat16)), ffn_grads_local)
+    )
     rows_norm_grad, attn_gain_grad = norm_back(rows_wide, inv_one, attn_gain, normed_grad_one)
     rows_grad = resid_grad + rows_norm_grad
     input_share = lax.dynamic_slice_in_dim(rows_grad, col_start, quarter, 1).astype(jnp.bfloat16)

time: 717 us -> 612 us (0.85)
  blocking collectives: 74.3 us -> 29.1 us
  starting transfers between devices: 69.9 us -> 33.1 us
  local copies, waits for them, and re-layouts: 89.9 us -> 79.4 us
  waiting for transfers between devices: 225 us -> 217 us
    reduce_scatter x1, waiting for transfers between devices: 80.5 us -> 0.01 us  [body(): lax.psum_scatter(ffn_grads_packed, 'row', scatter_dimension=0, tiled=True)]
    psum x0 -> x2, waiting for transfers between devices: none -> 65.5 us  [the longest x1 46.2 us: body(): lax.psum(attn_terms.astype(jnp.bfloat16), 'col').astype(jnp.float32)]
    all_to_all x3 -> x1, blocking collectives: 74.3 us -> 29.1 us  [col_scatter(): lax.all_to_all(blocks, 'col', split_axis=0, concat_axis=0, tiled=True)]
    reduce_scatter x1, waiting for transfers between devices: 0.01 us -> 42.8 us  [body(): lax.psum_scatter(packed_weight_grads([normed_one, attn_grad_low], [(0, qu...]
    all_to_all x4 -> x2, waiting for transfers between devices: 94.1 us -> 60.1 us  [col_gather(): lax.all_to_all(copies, 'col', split_axis=0, concat_axis=0, tiled=True)]
    all_to_all x1, starting transfers between devices: 31.6 us -> 7.36 us  [body(): lax.all_to_all(jnp.stack([output_share, input_share])[:, arrived_slots],...]
    all_to_all x1 -> x0, waiting for transfers between devices: 16.9 us -> none  [col_scatter(): lax.all_to_all(blocks, 'col', split_axis=0, concat_axis=0, tiled=True)]
    reduce_scatter x0 -> x1, waiting for transfers between devices: none -> 16.1 us  [body(): lax.psum_scatter(matmul(activ, down_w.T).astype(jnp.bfloat16), 'col', sca...]
  transfers between devices with their start and end apart: 12 -> 12, of which waited for: 8 -> 8; matrix products, arithmetic and copies ran while one was open for 23% -> 34% of each run, Pallas kernels for 5% -> 6%
where the time goes in v6:
time: 612 us; the launch traced here: 602 us
  waiting for transfers between devices  217 us (35%)
  matrix products  98.4 us (16%)
  other arithmetic  84 us (14%)
  local copies, waits for them, and re-layouts  79.4 us (13%)
  Pallas kernels  45.7 us (7%)
  starting transfers between devices  33.1 us (5%)
  blocking collectives  29.1 us (5%)
  between operations  15.3 us (2%)
    dot_general x70, matrix products, matmul(): return jnp.dot(left, right, preferred_element_type=jnp.float32)  98.4 us
    all_to_all x2, waiting for transfers between devices, col_gather(): lax.all_to_all(copies, 'col', split_axis=0, concat_axis=0, tiled=True)  60.1 us
    psum x1, waiting for transfers between devices, body(): lax.psum(attn_terms.astype(jnp.bfloat16), 'col').astype(jnp.float32)  46.2 us
    pallas_call x2, Pallas kernels, packed_weight_grads(): pl.pallas_call(kernel, out_shape=jax.ShapeDtypeStruct((features, len(sele...  45.7 us
    reduce_scatter x1, waiting for transfers between devices, body(): lax.psum_scatter(packed_weight_grads([normed_one, attn_grad_low], [(0, qu...  42.8 us
    all_to_all x1, blocking collectives, col_scatter(): lax.all_to_all(blocks, 'col', split_axis=0, concat_axis=0, tiled=True)  29.1 us
    all_to_all x1, waiting for transfers between devices, body(): lax.all_to_all(jnp.stack([tokens, cotangent])[:, send_order], 'row', spli...  19.6 us
    psum x1, waiting for transfers between devices, body(): normed_grad_two = lax.psum(normed_low_two, 'col').astype(jnp.float32)  19.3 us
  transfers between devices with their start and end apart: 12, of which 8 were waited for; matrix products, arithmetic and copies ran while one was open for 34% of the time, Pallas kernels for 6%

profile of v6, /device:TPU:0, one launch (start us, length us, event | category | flops | bytes accessed | tf_op | source)
XLA Modules:
  0.0 601.9 jit_solution(7923539910509131941)
XLA Ops:
  9.0 1.9 pad_maximum_fusion.5
  11.0 4.4 sort.45
  16.1 3.6 gather_fusion.1
  20.4 8.4 %all-to-all-start.1 = ((s32[32,16,1]{1,2,0:T(1,128)}), s32[32,16,1]{1,2,0:T(1,128)S(1)}, u32[]{:S(2)}, u32[]{:S(2)}) async-start(s32[32,16,1]{1,2,0:T(1,128)} %bitcast.3), calls=%async_computation.1 | async-start | bytes 32768 | tf_op jit(solution)/shard_map/all_to_all | solution.py:223
  30.5 2.4 pad_maximum_fusion.3
  32.9 4.1 gather_fusion
  37.0 7.4 %all-to-all-start = ((bf16[2,512,512]{2,0,1:T(2,128)(2,1)}), bf16[2,512,512]{2,0,1:T(2,128)(2,1)S(1)}, u32[]{:S(2)}, u32[]{:S(2)}) async-start(bf16[2,512,512]{2,0,1:T(2,128)(2,1)} %bitcast.2), calls=%async_computation | async-start | bytes 2097152 | tf_op jit(solution)/shard_map/all_to_all | solution.py:220
  45.7 3.8 sort.46
  49.5 19.6 %all-to-all-done = bf16[2,512,512]{2,0,1:T(2,128)(2,1)S(1)} async-done(((bf16[2,512,512]{2,0,1:T(2,128)(2,1)}), bf16[2,512,512]{2,0,1:T(2,128)(2,1)S(1)}, u32[]{:S(2)}, u32[]{:S(2)}) %all-to-all-start) | async-done | bytes 1048608 | tf_op jit(solution)/shard_map/all_to_all | solution.py:220
  69.1 3.6 gather_fusion.2
  74.1 2.4 broadcast_in_dim.88
  76.5 5.0 all-to-all-start.2
  83.9 45.2 %all-to-all-done.2 = bf16[4,2,512,512]{2,3,1,0:T(8,128)(2,1)} async-done(((bf16[4,2,512,512]{2,3,1,0:T(8,128)(2,1)}), bf16[4,2,512,512]{2,3,1,0:T(8,128)(2,1)}, u32[]{:S(2)}, u32[]{:S(2)}) %all-to-all-start.2) | async-done | bytes 4194336 | tf_op jit(solution)/shard_map/all_to_all | solution.py:125
  129.2 2.2 fusion.53
  131.4 3.7 fusion.55
  135.1 3.4 multiply_convert_fusion.2
  138.5 1.7 slice_bitcast_fusion
  140.3 2.5 copy.111
  142.8 3.8 fusion.106
  151.0 1.8 convolution_bitcast_fusion.2
  154.1 22.9 %while.32 = (s32[]{:T(128)}, bf16[8,512,64]{1,2,0:T(8,128)(2,1)}, f32[8,512]{1,0:T(8,128)}, bf16[8,512,64]{2,1,0:T(8,128)(2,1)S(1)}, bf16[1,512,64]{2,1,0:T(8,12...) while((s32[]{:T(128)}, bf16[8,512,64]{1,2,0:T(8,128)(2,1)}, ...), condition=%wide.region_8.9_spmd.clone.clone, body=%wide.region_5.8_spmd.clone.sunk.clone | while | flops 69991936 | bytes 3629653 | solution.py:256
  177.0 3.1 fusion.63
  180.1 2.6 copy.117
  182.9 1.7 slice.152
  186.0 7.6 %fusion.51 = f32[512,1408]{1,0:T(8,128)} fusion(bf16[512,2048]{0,1:T(8,128)(2,1)S(1)} %bitcast.222, bf16[2048,4224]{1,0:T(8,128)(2,1)} %all-gather.5.cloned.1.call-done), kind=kOutput, calls=%fused_computation.69 | convolution fusion | flops 2952790016 | bytes 10747904 | tf_op jit(solution)/shard_map/dot_general | solution.py:68
  193.6 46.2 %all-reduce.3.cloned.1.call-done = bf16[512,2048]{0,1:T(8,128)(2,1)} async-done(((bf16[512,2048]{0,1:T(8,128)(2,1)}), bf16[512,2048]{0,1:T(8,128)(2,1)}) %all-reduce.3.cloned.1.call-update) | async-done | bytes 2097168 | tf_op jit(solution)/shard_map/psum | solution.py:273
  239.8 3.1 multiply_reduce_fusion.5
  243.0 3.6 bitcast_add_fusion
  246.5 6.4 %fusion.47 = f32[512,1408]{1,0:T(8,128)S(1)} fusion(bf16[512,2048]{0,1:T(8,128)(2,1)S(1)} %get-tuple-element.345, bf16[2048,4224]{1,0:T(8,128)(2,1)} %all-gather.5.cloned.1.call-done), kind=kOutput, calls=%fused_computation.65 | convolution fusion | flops 2952790016 | bytes 10747904 | tf_op jit(solution)/shard_map/dot_general | solution.py:68
  253.0 9.2 %multiply_convert_fusion.5 = (bf16[512,1408]{1,0:T(8,128)(2,1)}, bf16[512,1408]{1,0:T(8,128)(2,1)}, bf16[512,1408]{1,0:T(8,128)(2,1)S(1)}) fusion(f32[512,1408]{1,0:T(8,128)S(1)} %copy-done.34, f32[512,1408]{1,0:T(8,128)S(1)} %fusion.47, bf16[512,2048]{0,1:T(8,128)(2,1)S(1)} %get-tuple-element.345, bf16[2048,4224]{1,0:T(8,128)(2,1)} %all-gather.5.cloned.1.call-done), kind=kOutput, calls=%fused_computation.94 | convolution fusion | flops 2964324352 | bytes 17956864 | tf_op jit(solution)/shard_map/dot_general | solution.py:68
  263.4 7.3 %fusion.58 = bf16[512,2048]{0,1:T(8,128)(2,1)} fusion(bf16[512,1408]{1,0:T(8,128)(2,1)S(1)} %get-tuple-element.348, bf16[2048,4224]{1,0:T(8,128)(2,1)} %all-gather.5.cloned.1.call-done), kind=kOutput, calls=%fused_computation.91 | convolution fusion | flops 2953838592 | bytes 9306112 | tf_op jit(solution)/shard_map/dot_general | solution.py:68
  270.8 6.0 %fusion.41 = f32[512,2048]{0,1:T(8,128)S(1)} fusion(bf16[512,1408]{1,0:T(8,128)(2,1)} %get-tuple-element.346, bf16[2048,4224]{1,0:T(8,128)(2,1)} %all-gather.5.cloned.1.call-done), kind=kOutput, calls=%fused_computation.59 | convolution fusion | flops 2952790016 | bytes 11403264 | tf_op jit(solution)/shard_map/dot_general | solution.py:68
  276.8 7.5 %add_convert_fusion.1 = bf16[512,2048]{0,1:T(8,128)(2,1)} fusion(f32[512,2048]{0,1:T(8,128)S(1)} %fusion.41, bf16[512,1408]{1,0:T(8,128)(2,1)S(1)} %copy-done.9, bf16[2048,4224]{1,0:T(8,128)(2,1)} %all-gather.5.cloned.1.call-done), kind=kOutput, calls=%fused_computation.87 | convolution fusion | flops 2954887168 | bytes 13500416 | tf_op jit(solution)/shard_map/dot_general | solution.py:68
  284.3 16.1 %reduce-scatter.4.cloned.1.call-done = bf16[512,512]{0,1:T(8,128)(2,1)} async-done(((bf16[512,2048]{0,1:T(8,128)(2,1)}), bf16[512,512]{0,1:T(8,128)(2,1)}) %reduce-scatter.4.cloned.1.call-update) | async-done | bytes 524304 | tf_op jit(solution)/shard_map/reduce_scatter | solution.py:283
  300.6 4.8 pad_maximum_fusion.1.left_ref
  305.4 2.2 pad_maximum_fusion.right_ref
  307.7 33.9 %shard_map.230 = bf16[2048,4224]{1,0:T(8,128)(2,1)} custom-call(s32[33]{0:T(128)} %constant.126.clone.select_ref, bf16[2,2048,512]{2,1,0:T(8,128)(2,1)} %pad_maximum_fusion.1.left_ref, bf16[512,4224]{1,0:T(8,128)(2,1)} %pad_maximum_fusion.right_ref), custom_call_target="tpu_custom_call" | custom-call | tf_op jit(solution)/shard_map/pallas_call | solution.py:186
  341.6 19.3 %all-reduce.5.cloned.1.call-done = bf16[512,2048]{0,1:T(8,128)(2,1)} async-done(((bf16[512,2048]{0,1:T(8,128)(2,1)}), bf16[512,2048]{0,1:T(8,128)(2,1)}) %all-reduce.5.cloned.1.call-update) | async-done | bytes 2097168 | tf_op jit(solution)/shard_map/psum | solution.py:296
  360.9 4.2 convert_element_type.159
  365.2 4.3 multiply_reduce_fusion.1
  369.9 3.7 convert_bitcast_fusion
  373.6 2.0 copy-done.6
  375.6 4.0 fusion.67
  381.2 31.2 %while.33 = (s32[]{:T(128)}, f32[8,512,64]{1,2,0:T(8,128)}, f32[8,512,64]{1,2,0:T(8,128)S(1)}, f32[8,512,64]{1,2,0:T(8,128)}, bf16[8,512,64]{2,1,0:T(8,128)(2,1)...) while((s32[]{:T(128)}, f32[8,512,64]{1,2,0:T(8,128)}, ...), condition=%wide.region_16.17_spmd.clone.clone, body=%wide.region_14.16_spmd.clone.sunk.clone | while | flops 170982912 | bytes 9126513 | solution.py:309
  414.2 1.9 fusion.94
  416.4 1.7 fusion.78
  418.2 2.9 fusion.65
  421.1 1.8 add_convert_fusion
  423.1 29.1 %all_to_all.37 = bf16[4,512,512]{2,1,0:T(8,128)(2,1)S(1)} all-to-all(bf16[4,512,512]{2,1,0:T(8,128)(2,1)S(1)} %bitcast.226), channel_id=1, replica_groups=mesh['row'=32,'col'=4] {'col'}, dimensions={0} | all-to-all | bytes 4194304 | tf_op jit(solution)/shard_map/all_to_all | solution.py:118
  454.7 3.6 all-to-all-start.4
  461.3 3.0 concatenate.61.right_ref
  464.3 4.6 pad_maximum_fusion.2.left_ref
  468.8 14.9 %all-to-all-done.4 = bf16[4,512,512]{1,2,0:T(8,128)(2,1)S(1)} async-done(((bf16[4,512,512]{1,2,0:T(8,128)(2,1)}), bf16[4,512,512]{1,2,0:T(8,128)(2,1)S(1)}, u32[]{:S(2)}, u32[]{:S(2)}) %all-to-all-start.4) | async-done | bytes 2097184 | tf_op jit(solution)/shard_map/all_to_all | solution.py:125
  483.7 2.6 convert_element_type.174
  486.3 5.8 multiply_reduce_fusion.2
  493.6 11.8 %shard_map.231 = bf16[2048,1280]{1,0:T(8,128)(2,1)} custom-call(s32[10]{0:T(128)} %constant.127.clone.select_ref, bf16[2,2048,512]{2,1,0:T(8,128)(2,1)} %pad_maximum_fusion.2.left_ref, bf16[512,1152]{1,0:T(8,128)(2,1)} %concatenate.61.right_ref, bf16[2048,128]{1,0:T(8,128)(2,1)} %maximum_maximum_fusion.tail_ref), custom_call_target="tpu_custom_call" | custom-call | tf_op jit(solution)/shard_map/pallas_call | solution.py:186
  507.8 2.3 fusion.75
  511.2 4.1 gather_fusion.3
  515.3 7.4 %all-to-all-start.5 = ((bf16[2,512,512]{2,0,1:T(2,128)(2,1)}), bf16[2,512,512]{2,0,1:T(2,128)(2,1)S(1)}, u32[]{:S(2)}, u32[]{:S(2)}) async-start(bf16[2,512,512]{2,0,1:T(2,128)(2,1)} %bitcast.37), calls=%async_computation.7 | async-start | bytes 2097152 | tf_op jit(solution)/shard_map/all_to_all | solution.py:364
  522.7 3.8 sort.47
  527.5 12.5 %all-to-all-done.5 = bf16[2,512,512]{2,0,1:T(2,128)(2,1)S(1)} async-done(((bf16[2,512,512]{2,0,1:T(2,128)(2,1)}), bf16[2,512,512]{2,0,1:T(2,128)(2,1)S(1)}, u32[]{:S(2)}, u32[]{:S(2)}) %all-to-all-start.5) | async-done | bytes 1048608 | tf_op jit(solution)/shard_map/all_to_all | solution.py:364
  541.8 2.6 gather_fusion.5
  544.5 2.6 gather_fusion.4
  547.1 42.8 %reduce-scatter.8.cloned.1.call-done = bf16[64,1280]{1,0:T(8,128)(2,1)} async-done(((bf16[2048,1280]{1,0:T(8,128)(2,1)}), bf16[64,1280]{1,0:T(8,128)(2,1)}) %reduce-scatter.8.cloned.1.call-update) | async-done | bytes 163856 | tf_op jit(solution)/shard_map/reduce_scatter | solution.py:341
  (259 shorter events, 94.7 us)
Async XLA Ops:
  7.2 21.6 %copy-start.15 = (bf16[512,512]{1,0:T(8,128)(2,1)S(1)}, bf16[512,512]{1,0:T(8,128)(2,1)}, u32[]{:S(2)}) copy-start(bf16[512,512]{1,0:T(8,128)(2,1)} %param.19) | copy-start | bytes 1572868
  7.2 22.4 %copy-start.16 = (bf16[512,512]{1,0:T(8,128)(2,1)S(1)}, bf16[512,512]{1,0:T(8,128)(2,1)}, u32[]{:S(2)}) copy-start(bf16[512,512]{1,0:T(8,128)(2,1)} %param.20) | copy-start | bytes 1572868
  7.2 131.3 %all-gather.3.cloned.1.call-start = ((), (), s32[]{:S(2)}) async-start(), calls=%async_computation.9 | async-start | bytes 4866048 | tf_op jit(solution)/shard_map/all_gather | solution.py:134
  9.0 171.1 %all-gather.5.cloned.1.call-start = ((), (), s32[]{:S(2)}) async-start(), calls=%async_computation.10 | async-start | bytes 17842176 | tf_op jit(solution)/shard_map/all_gather | solution.py:134
  15.5 0.6 copy-start.31
  20.4 16.7 %all-to-all-start.1 = ((s32[32,16,1]{1,2,0:T(1,128)}), s32[32,16,1]{1,2,0:T(1,128)S(1)}, u32[]{:S(2)}, u32[]{:S(2)}) async-start(s32[32,16,1]{1,2,0:T(1,128)} %bitcast.3), calls=%async_computation.1 | async-start | bytes 32768 | tf_op jit(solution)/shard_map/all_to_all | solution.py:223
  37.0 12.5 %copy-start.18 = (s32[32,16,1]{1,2,0:T(1,128)}, s32[32,16,1]{1,2,0:T(1,128)S(1)}, u32[]{:S(2)}) copy-start(s32[32,16,1]{1,2,0:T(1,128)S(1)} %all-to-all-done.1) | copy-start | bytes 6148
  37.0 32.0 %all-to-all-start = ((bf16[2,512,512]{2,0,1:T(2,128)(2,1)}), bf16[2,512,512]{2,0,1:T(2,128)(2,1)S(1)}, u32[]{:S(2)}, u32[]{:S(2)}) async-start(bf16[2,512,512]{2,0,1:T(2,128)(2,1)} %bitcast.2), calls=%async_computation | async-start | bytes 2097152 | tf_op jit(solution)/shard_map/all_to_all | solution.py:220
  76.5 5.5 copy-start.20
  76.5 5.5 copy-start.29
  76.5 52.7 %all-to-all-start.2 = ((bf16[4,2,512,512]{2,3,1,0:T(8,128)(2,1)}), bf16[4,2,512,512]{2,3,1,0:T(8,128)(2,1)}, u32[]{:S(2)}, u32[]{:S(2)}) async-start(bf16[4,2,512,512]{2,3,1,0:T(8,128)(2,1)} %broadcast_in_dim.88), calls=%async_computation.2 | async-start | bytes 8388608 | tf_op jit(solution)/shard_map/all_to_all | solution.py:125
  81.5 158.4 %all-reduce.3.cloned.1.call-start = ((), (), s32[]{:S(2)}) async-start(), calls=%async_computation.11 | async-start | bytes 4194304 | tf_op jit(solution)/shard_map/psum | solution.py:273
  82.6 70.2 %copy-start.33 = (f32[32]{0:T(128)}, f32[32]{0:T(128)S(1)}, u32[]{:S(2)}) copy-start(f32[32]{0:T(128)S(1)} %negate_power_fusion) | copy-start | bytes 388
  83.6 69.1 %copy-start.24 = (f32[512]{0:T(512)}, f32[512]{0:T(512)S(1)}, u32[]{:S(2)}) copy-start(f32[512]{0:T(512)S(1)} %fusion.100) | copy-start | bytes 6148
  131.4 3.7 copy-start.22
  142.8 6.3 %copy-start.5 = (bf16[512,2048]{0,1:T(8,128)(2,1)S(1)}, bf16[512,2048]{0,1:T(8,128)(2,1)}, u32[]{:S(2)}) copy-start(bf16[512,2048]{0,1:T(8,128)(2,1)} %multiply_convert_fusion.2) | copy-start | bytes 6291460
  182.7 117.7 %reduce-scatter.4.cloned.1.call-start = ((), (), s32[]{:S(2)}) async-start(), calls=%async_computation.12 | async-start | bytes 2621440 | tf_op jit(solution)/shard_map/reduce_scatter | solution.py:283
  184.6 1.3 copy-start.2
  193.6 49.3 %copy-start.21 = (f32[2048]{0:T(1024)S(1)}, f32[2048]{0:T(1024)}, u32[]{:S(2)}) copy-start(f32[2048]{0:T(1024)} %param.28) | copy-start | bytes 24580
  239.8 3.1 copy-start.1
  242.9 3.6 copy-start.26
  246.5 6.4 %copy-start.4 = (bf16[512,2048]{0,1:T(8,128)(2,1)}, bf16[512,2048]{0,1:T(8,128)(2,1)S(1)}, u32[]{:S(2)}) copy-start(bf16[512,2048]{0,1:T(8,128)(2,1)S(1)} %get-tuple-element.345) | copy-start | bytes 6291460
  246.5 6.4 %copy-start.34 = (f32[512,1408]{1,0:T(8,128)S(1)}, f32[512,1408]{1,0:T(8,128)}, u32[]{:S(2)}) copy-start(f32[512,1408]{1,0:T(8,128)} %fusion.51) | copy-start | bytes 8650756
  262.2 1.2 copy-start.11
  270.7 90.2 %all-reduce.5.cloned.1.call-start = ((), (), s32[]{:S(2)}) async-start(), calls=%async_computation.13 | async-start | bytes 4194304 | tf_op jit(solution)/shard_map/psum | solution.py:296
  270.7 6.0 %copy-start.9 = (bf16[512,1408]{1,0:T(8,128)(2,1)S(1)}, bf16[512,1408]{1,0:T(8,128)(2,1)}, u32[]{:S(2)}) copy-start(bf16[512,1408]{1,0:T(8,128)(2,1)} %get-tuple-element.347) | copy-start | bytes 4325380
  300.3 186.0 %reduce-scatter.6.cloned.1.call-start = ((), (), s32[]{:S(2)}) async-start(), calls=%async_computation.14 | async-start | bytes 17842176 | tf_op jit(solution)/shard_map/reduce_scatter | solution.py:304
  300.6 4.8 copy-start.8
  300.6 4.8 copy-start.10
  300.6 4.8 copy-start.12
  365.2 4.4 copy-start
  365.2 4.7 copy-start.3
  365.2 4.7 copy-start.27
  373.6 2.0 copy-start.6
  375.6 5.5 copy-start.13
  375.6 5.5 copy-start.30
  381.2 33.0 %copy-start.25 = (f32[512]{0:T(512)S(1)}, f32[512]{0:T(512)}, u32[]{:S(2)}) copy-start(f32[512]{0:T(512)} %copy-done.24) | copy-start | bytes 6148
  412.4 3.8 copy-start.14
  453.2 7.8 %copy-start.28 = (bf16[2048]{0:T(1024)(128)(2,1)S(1)}, bf16[2048]{0:T(1024)(128)(2,1)}, u32[]{:S(2)}) copy-start(bf16[2048]{0:T(1024)(128)(2,1)} %get-tuple-element.297) | copy-start | bytes 12292
  454.7 29.0 %all-to-all-start.4 = ((bf16[4,512,512]{1,2,0:T(8,128)(2,1)}), bf16[4,512,512]{1,2,0:T(8,128)(2,1)S(1)}, u32[]{:S(2)}, u32[]{:S(2)}) async-start(bf16[4,512,512]{1,2,0:T(8,128)(2,1)} %broadcast_in_dim.90), calls=%async_computation.5 | async-start | bytes 4194304 | tf_op jit(solution)/shard_map/all_to_all | solution.py:125
  458.3 131.5 %reduce-scatter.8.cloned.1.call-start = ((), (), s32[]{:S(2)}) async-start(), calls=%async_computation.15 | async-start | bytes 5406720 | tf_op jit(solution)/shard_map/reduce_scatter | solution.py:341
  468.8 17.5 %copy-start.23 = (f32[512]{0:T(512)S(1)}, f32[512]{0:T(512)}, u32[]{:S(2)}) copy-start(f32[512]{0:T(512)} %copy-done.22) | copy-start | bytes 6148
  505.4 0.7 copy-start.19
  505.4 1.1 copy-start.17
  510.1 12.6 %copy-start.32 = (s32[512]{0:T(512)S(1)}, s32[512]{0:T(512)}, u32[]{:S(2)}) copy-start(s32[512]{0:T(512)} %copy-done.31) | copy-start | bytes 6148
  510.1 16.4 %copy-start.7 = (bf16[64,4224]{1,0:T(8,128)(2,1)S(1)}, bf16[64,4224]{1,0:T(8,128)(2,1)}, u32[]{:S(2)}) copy-start(bf16[64,4224]{1,0:T(8,128)(2,1)} %reduce-scatter.6.cloned.1.call-done) | copy-start | bytes 1622020
  515.3 24.7 %all-to-all-start.5 = ((bf16[2,512,512]{2,0,1:T(2,128)(2,1)}), bf16[2,512,512]{2,0,1:T(2,128)(2,1)S(1)}, u32[]{:S(2)}, u32[]{:S(2)}) async-start(bf16[2,512,512]{2,0,1:T(2,128)(2,1)} %bitcast.37), calls=%async_computation.7 | async-start | bytes 2097152 | tf_op jit(solution)/shard_map/all_to_all | solution.py:364
Sparse Core Ops, SparseCore 0:
  10.9 59.4 all-gather.2
  72.6 72.4 all-gather.4
  182.8 56.9 all-reduce.2
  270.8 29.4 reduce-scatter.3
  302.5 58.3 all-reduce.4
  365.3 117.2 reduce-scatter.5
  505.5 84.2 reduce-scatter.7

commit v7 on v6

--- a/solution.py
+++ b/solution.py
@@ -97,6 +97,64 @@
     query_grad = matmul(score_grad, key_head) * scale_factor
     key_grad = matmul(score_grad.T, query_head) * scale_factor
     return (query_grad, key_grad, value_grad)
+
+
+def grouped(heads, kv_count):
+    return heads.reshape(kv_count, heads.shape[0] // kv_count, *heads.shape[1:])
+
+
+def group_scores(query_groups, key_heads, allowed, scale_factor):
+    scores = (
+        jnp.einsum("kgqd,kpd->kgqp", query_groups, key_heads, preferred_element_type=jnp.float32)
+        * scale_factor
+    )
+    return jnp.where(allowed, scores, -1e30)
+
+
+def attention_forward(query_heads, key_heads, value_heads, allowed, scale_factor):
+    query_groups = grouped(query_heads, key_heads.shape[0])
+    scores = group_scores(query_groups, key_heads, allowed, scale_factor)
+    peak = jnp.max(scores, axis=-1, keepdims=True)
+    expo = jnp.exp(scores - peak)
+    total = jnp.sum(expo, axis=-1, keepdims=True)
+    probs = expo / total
+    mixed = jnp.einsum(
+        "kgqp,kpd->kgqd", probs.astype(jnp.bfloat16), value_heads, preferred_element_type=jnp.float32
+    )
+    return mixed.reshape(query_heads.shape), (peak + jnp.log(total))[..., 0]
+
+
+def attention_backward(
+    query_heads, key_heads, value_heads, grad_heads, log_totals, allowed, scale_factor
+):
+    kv_count = key_heads.shape[0]
+    query_groups = grouped(query_heads, kv_count)
+    grad_groups = grouped(grad_heads, kv_count)
+    scores = group_scores(query_groups, key_heads, allowed, scale_factor)
+    probs = jnp.exp(scores - log_totals[..., None])
+    prob_grad = jnp.einsum(
+        "kgqd,kpd->kgqp", grad_groups, value_heads, preferred_element_type=jnp.float32
+    )
+    value_grad = jnp.einsum(
+        "kgqp,kgqd->kpd", probs.astype(jnp.bfloat16), grad_groups, preferred_element_type=jnp.float32
+    )
+    inner = jnp.sum(probs * prob_grad, axis=-1, keepdims=True)
+    score_grad = (probs * (prob_grad - inner)).astype(jnp.bfloat16)
+    query_grad = (
+        jnp.einsum("kgqp,kpd->kgqd", score_grad, key_heads, preferred_element_type=jnp.float32)
+        * scale_factor
+    )
+    key_grad = (
+        jnp.einsum("kgqp,kgqd->kpd", score_grad, query_groups, preferred_element_type=jnp.float32)
+        * scale_factor
+    )
+    return query_grad.reshape(query_heads.shape), key_grad, value_grad
+
+
+def row_scatter_sum(vectors):
+    count = lax.axis_size("row")
+    blocks = jnp.moveaxis(vectors.reshape(vectors.shape[0], count, -1), 1, 0)
+    return jnp.sum(lax.all_to_all(blocks, "row", split_axis=0, concat_axis=0, tiled=True), axis=0)
 
 
 GRAD_BLOCK = 128
@@ -251,17 +309,9 @@
         .transpose(1, 0, 2)
     )
     value_heads = value_raw.astype(jnp.bfloat16).reshape(row_count, kv_count, HD).transpose(1, 0, 2)
-    kv_slots = jnp.arange(query_heads_count, dtype=jnp.int32) // group_size
     scale_factor = HD ** (-0.5)
-    mixed_heads, log_totals = lax.map(
-        partial(
-            head_forward,
-            key_heads=key_rot,
-            value_heads=value_heads,
-            allowed=allowed,
-            scale_factor=scale_factor,
-        ),
-        (query_rot, kv_slots),
+    mixed_heads, log_totals = attention_forward(
+        query_rot, key_rot, value_heads, allowed, scale_factor
     )
     mixed = (
         mixed_heads.transpose(1, 0, 2)
@@ -306,61 +356,44 @@
     attn_grad_low = resid_grad.astype(jnp.bfloat16)
     mixed_grad = matmul(attn_grad_low, output_w).astype(jnp.bfloat16)
     mixed_grad_heads = mixed_grad.reshape(row_count, query_heads_count, HD).transpose(1, 0, 2)
-    query_grads, key_grads, value_grads = lax.map(
-        partial(
-            head_backward,
-            key_heads=key_rot,
-            value_heads=value_heads,
-            allowed=allowed,
-            scale_factor=scale_factor,
-        ),
-        (query_rot, kv_slots, mixed_grad_heads, log_totals),
+    query_grads, key_grads, value_grads = attention_backward(
+        query_rot, key_rot, value_heads, mixed_grad_heads, log_totals, allowed, scale_factor
     )
     query_grad = (
         rotate_back(query_grads.transpose(1, 0, 2), cosine, sine)
         .reshape(row_count, query_heads_count * HD)
         .astype(jnp.bfloat16)
     )
-    key_sum = key_grads.reshape(kv_count, group_size, row_count, HD).sum(axis=1).transpose(1, 0, 2)
+    key_sum = key_grads.transpose(1, 0, 2)
     key_grad = (
         rotate_back(key_sum, cosine, sine).reshape(row_count, kv_count * HD).astype(jnp.bfloat16)
     )
-    value_sum = (
-        value_grads.reshape(kv_count, group_size, row_count, HD).sum(axis=1).transpose(1, 0, 2)
-    )
+    value_sum = value_grads.transpose(1, 0, 2)
     value_grad = value_sum.reshape(row_count, kv_count * HD).astype(jnp.bfloat16)
     normed_terms_one = (
         matmul(query_grad, query_w.T) + matmul(key_grad, key_w.T) + matmul(value_grad, value_w.T)
     )
-    normed_grad_one, ffn_grads_local = lax.optimization_barrier(
-        (col_sum(normed_terms_one.astype(jnp.bfloat16)), ffn_grads_local)
-    )
+    attn_grads_packed, ffn_grads_local = lax.optimization_barrier(
+        (
+            packed_weight_grads(
+                [normed_one, attn_grad_low],
+                [(0, query_grad), (0, key_grad), (0, value_grad), (1, mixed)],
+            ),
+            ffn_grads_local,
+        )
+    )
+    attn_grads_local = lax.psum_scatter(attn_grads_packed, "row", scatter_dimension=0, tiled=True)
+    normed_grad_one = col_sum(normed_terms_one.astype(jnp.bfloat16))
     rows_norm_grad, attn_gain_grad = norm_back(rows_wide, inv_one, attn_gain, normed_grad_one)
     rows_grad = resid_grad + rows_norm_grad
     input_share = lax.dynamic_slice_in_dim(rows_grad, col_start, quarter, 1).astype(jnp.bfloat16)
-    attn_grads_local = lax.psum_scatter(
-        packed_weight_grads(
-            [normed_one, attn_grad_low],
-            [(0, query_grad), (0, key_grad), (0, value_grad), (1, mixed)],
-            gain_tail_of([attn_gain_grad, ffn_gain_grad]),
-        ),
-        "row",
-        scatter_dimension=0,
-        tiled=True,
-    )
-    (
-        query_result,
-        key_result,
-        value_result,
-        output_result,
-        attn_gain_result,
-        ffn_gain_result,
-    ) = split_columns(attn_grads_local.astype(jnp.float32), attn_widths + [1, 1])
+    query_result, key_result, value_result, output_result = split_columns(
+        attn_grads_local.astype(jnp.float32), attn_widths
+    )
+    attn_gain_result, ffn_gain_result = row_scatter_sum(jnp.stack([attn_gain_grad, ffn_gain_grad]))
     gate_result, up_result, down_result = split_columns(
         ffn_grads_local.astype(jnp.float32), ffn_widths
     )
-    attn_gain_result = attn_gain_result.reshape(-1)
-    ffn_gain_result = ffn_gain_result.reshape(-1)
     back_pair = lax.all_to_all(
         jnp.stack([output_share, input_share])[:, arrived_slots],
         "row",

time: 612 us -> 598 us (0.977)
  waiting for transfers between devices: 217 us -> 239 us
  matrix products: 98.4 us -> 81.4 us
  local copies, waits for them, and re-layouts: 79.4 us -> 64.3 us
  other arithmetic: 84 us -> 74.1 us
    reduce_scatter x1, waiting for transfers between devices: 0.01 us -> 57.8 us  [body(): lax.psum_scatter(ffn_grads_packed, 'row', scatter_dimension=0, tiled=True)]
    reduce_scatter x1, waiting for transfers between devices: 42.8 us -> 0.01 us  [body(): lax.psum_scatter(attn_grads_packed, 'row', scatter_dimension=0, tiled=True)]
    dot_general x70 -> x14, matrix products: 98.4 us -> 65.6 us  [matmul(): return jnp.dot(left, right, preferred_element_type=jnp.float32)]
    dot_general x0 -> x6, matrix products: none -> 15.9 us  [the longest x1 5.53 us: attention_backward(): jnp.einsum('kgqp,kgqd->kpd', probs.astype(jnp.bfloat16), grad_groups, pre...]
    dynamic_update_slice x8 -> x0, local copies, waits for them, and re-layouts: 10.8 us -> none  [body(): lax.map(partial(head_forward, key_heads=key_rot, value_heads=value_heads,...]
    all_to_all x2, waiting for transfers between devices: 60.1 us -> 67.7 us  [col_gather(): lax.all_to_all(copies, 'col', split_axis=0, concat_axis=0, tiled=True)]
  transfers between devices with their start and end apart: 12 -> 13, of which waited for: 8 -> 8; matrix products, arithmetic and copies ran while one was open for 34% -> 29% of each run, Pallas kernels for 6% -> 8%
where the time goes in v7:
time: 598 us; the launch traced here: 588 us
  waiting for transfers between devices  239 us (40%)
  matrix products  81.4 us (14%)
  other arithmetic  74.1 us (12%)
  local copies, waits for them, and re-layouts  64.3 us (11%)
  Pallas kernels  45.6 us (8%)
  starting transfers between devices  38.3 us (6%)
  blocking collectives  29.2 us (5%)
  between operations  15.6 us (3%)
    all_to_all x2, waiting for transfers between devices, col_gather(): lax.all_to_all(copies, 'col', split_axis=0, concat_axis=0, tiled=True)  67.7 us
    dot_general x14, matrix products, matmul(): return jnp.dot(left, right, preferred_element_type=jnp.float32)  65.6 us
    reduce_scatter x1, waiting for transfers between devices, body(): lax.psum_scatter(ffn_grads_packed, 'row', scatter_dimension=0, tiled=True)  57.8 us
    psum x1, waiting for transfers between devices, body(): lax.psum(attn_terms.astype(jnp.bfloat16), 'col').astype(jnp.float32)  45.9 us
    pallas_call x2, Pallas kernels, packed_weight_grads(): pl.pallas_call(kernel, out_shape=jax.ShapeDtypeStruct((features, len(sele...  45.6 us
    all_to_all x1, blocking collectives, col_scatter(): lax.all_to_all(blocks, 'col', split_axis=0, concat_axis=0, tiled=True)  29.2 us
    psum x1, waiting for transfers between devices, body(): normed_grad_two = lax.psum(normed_low_two, 'col').astype(jnp.float32)  19.8 us
    all_to_all x1, waiting for transfers between devices, body(): lax.all_to_all(jnp.stack([tokens, cotangent])[:, send_order], 'row', spli...  19.6 us
  transfers between devices with their start and end apart: 13, of which 8 were waited for; matrix products, arithmetic and copies ran while one was open for 29% of the time, Pallas kernels for 8%

profile of v7, /device:TPU:0, one launch (start us, length us, event | category | flops | bytes accessed | tf_op | source)
XLA Modules:
  0.0 587.5 jit_solution(1322537056196526184)
XLA Ops:
  9.0 2.0 pad_maximum_fusion.5
  11.0 4.4 sort.45
  16.1 3.6 gather_fusion.1
  20.4 8.4 %all-to-all-start.1 = ((s32[32,16,1]{1,2,0:T(1,128)}), s32[32,16,1]{1,2,0:T(1,128)S(1)}, u32[]{:S(2)}, u32[]{:S(2)}) async-start(s32[32,16,1]{1,2,0:T(1,128)} %bitcast.3), calls=%async_computation.1 | async-start | bytes 32768 | tf_op jit(solution)/shard_map/all_to_all | solution.py:281
  30.5 2.4 pad_maximum_fusion.3
  32.9 4.1 gather_fusion
  37.1 7.4 %all-to-all-start = ((bf16[2,512,512]{2,0,1:T(2,128)(2,1)}), bf16[2,512,512]{2,0,1:T(2,128)(2,1)S(1)}, u32[]{:S(2)}, u32[]{:S(2)}) async-start(bf16[2,512,512]{2,0,1:T(2,128)(2,1)} %bitcast.2), calls=%async_computation | async-start | bytes 2097152 | tf_op jit(solution)/shard_map/all_to_all | solution.py:278
  45.7 3.8 sort.46
  49.5 19.6 %all-to-all-done = bf16[2,512,512]{2,0,1:T(2,128)(2,1)S(1)} async-done(((bf16[2,512,512]{2,0,1:T(2,128)(2,1)}), bf16[2,512,512]{2,0,1:T(2,128)(2,1)S(1)}, u32[]{:S(2)}, u32[]{:S(2)}) %all-to-all-start) | async-done | bytes 1048608 | tf_op jit(solution)/shard_map/all_to_all | solution.py:278
  69.1 3.6 gather_fusion.2
  74.1 2.3 broadcast_in_dim.22
  76.4 5.0 all-to-all-start.2
  83.1 46.1 %all-to-all-done.2 = bf16[4,2,512,512]{2,3,1,0:T(8,128)(2,1)} async-done(((bf16[4,2,512,512]{2,3,1,0:T(8,128)(2,1)}), bf16[4,2,512,512]{2,3,1,0:T(8,128)(2,1)}, u32[]{:S(2)}, u32[]{:S(2)}) %all-to-all-start.2) | async-done | bytes 4194336 | tf_op jit(solution)/shard_map/all_to_all | solution.py:183
  129.1 2.3 fusion.19
  131.4 3.7 fusion.21
  135.1 4.7 multiply_convert_fusion.2
  141.5 2.5 copy.115
  144.0 2.6 convolution_bitcast_fusion.1
  147.9 2.4 fusion.48
  154.5 2.1 copy-done
  159.0 2.9 fusion.31
  161.9 2.5 copy.121
  168.0 7.6 %fusion.12 = f32[512,1408]{1,0:T(8,128)} fusion(bf16[512,2048]{0,1:T(8,128)(2,1)S(1)} %bitcast.161, bf16[2048,4224]{1,0:T(8,128)(2,1)} %all-gather.5.cloned.1.call-done), kind=kOutput, calls=%fused_computation.24 | convolution fusion | flops 2952790016 | bytes 10747904 | tf_op jit(solution)/shard_map/dot_general | solution.py:68
  175.6 45.9 %all-reduce.3.cloned.1.call-done = bf16[512,2048]{0,1:T(8,128)(2,1)} async-done(((bf16[512,2048]{0,1:T(8,128)(2,1)}), bf16[512,2048]{0,1:T(8,128)(2,1)}) %all-reduce.3.cloned.1.call-update) | async-done | bytes 2097168 | tf_op jit(solution)/shard_map/psum | solution.py:323
  221.6 3.1 multiply_reduce_fusion.3
  224.7 3.7 bitcast_add_fusion
  228.4 6.4 %fusion.8 = f32[512,1408]{1,0:T(8,128)S(1)} fusion(bf16[512,2048]{0,1:T(8,128)(2,1)S(1)} %get-tuple-element.40, bf16[2048,4224]{1,0:T(8,128)(2,1)} %all-gather.5.cloned.1.call-done), kind=kOutput, calls=%fused_computation.20 | convolution fusion | flops 2952790016 | bytes 10747904 | tf_op jit(solution)/shard_map/dot_general | solution.py:68
  234.9 8.7 %multiply_convert_fusion.5 = (bf16[512,1408]{1,0:T(8,128)(2,1)S(1)}, bf16[512,1408]{1,0:T(8,128)(2,1)}, bf16[512,1408]{1,0:T(8,128)(2,1)S(1)}) fusion(f32[512,1408]{1,0:T(8,128)S(1)} %copy-done.56, f32[512,1408]{1,0:T(8,128)S(1)} %fusion.8, bf16[512,2048]{0,1:T(8,128)(2,1)S(1)} %get-tuple-element.40, bf16[2048,4224]{1,0:T(8,128)(2,1)} %all-gather.5.cloned.1.call-done), kind=kOutput, calls=%fused_computation.56 | convolution fusion | flops 2964324352 | bytes 17956864 | tf_op jit(solution)/shard_map/dot_general | solution.py:68
  244.7 7.3 %fusion.26 = bf16[512,2048]{0,1:T(8,128)(2,1)} fusion(bf16[512,1408]{1,0:T(8,128)(2,1)S(1)} %get-tuple-element.43, bf16[2048,4224]{1,0:T(8,128)(2,1)} %all-gather.5.cloned.1.call-done), kind=kOutput, calls=%fused_computation.53 | convolution fusion | flops 2953838592 | bytes 9306112 | tf_op jit(solution)/shard_map/dot_general | solution.py:68
  252.3 5.6 fusion.2
  257.9 7.4 %add_convert_fusion.1 = bf16[512,2048]{0,1:T(8,128)(2,1)} fusion(f32[512,2048]{0,1:T(8,128)S(1)} %fusion.2, bf16[512,1408]{1,0:T(8,128)(2,1)S(1)} %copy-done.13, bf16[2048,4224]{1,0:T(8,128)(2,1)} %all-gather.5.cloned.1.call-done), kind=kOutput, calls=%fused_computation.48 | convolution fusion | flops 2954887168 | bytes 13500416 | tf_op jit(solution)/shard_map/dot_general | solution.py:68
  265.3 16.4 %reduce-scatter.4.cloned.1.call-done = bf16[512,512]{0,1:T(8,128)(2,1)} async-done(((bf16[512,2048]{0,1:T(8,128)(2,1)}), bf16[512,512]{0,1:T(8,128)(2,1)}) %reduce-scatter.4.cloned.1.call-update) | async-done | bytes 524304 | tf_op jit(solution)/shard_map/reduce_scatter | solution.py:333
  281.8 4.7 pad_maximum_fusion.1.left_ref
  286.5 2.1 pad_maximum_fusion.right_ref
  288.6 33.9 %shard_map.230 = bf16[2048,4224]{1,0:T(8,128)(2,1)} custom-call(s32[33]{0:T(128)} %constant.64.clone.select_ref, bf16[2,2048,512]{2,1,0:T(8,128)(2,1)} %pad_maximum_fusion.1.left_ref, bf16[512,4224]{1,0:T(8,128)(2,1)} %pad_maximum_fusion.right_ref), custom_call_target="tpu_custom_call" | custom-call | tf_op jit(solution)/shard_map/pallas_call | solution.py:244
  322.5 19.8 %all-reduce.5.cloned.1.call-done = bf16[512,2048]{0,1:T(8,128)(2,1)} async-done(((bf16[512,2048]{0,1:T(8,128)(2,1)}), bf16[512,2048]{0,1:T(8,128)(2,1)}) %all-reduce.5.cloned.1.call-update) | async-done | bytes 2097168 | tf_op jit(solution)/shard_map/psum | solution.py:346
  342.3 4.1 convert_element_type.167
  348.5 3.7 multiply_reduce_fusion.1
  353.3 4.0 convert_bitcast_fusion
  357.2 4.7 fusion.36
  362.0 2.5 multiply_reduce_fusion
  364.5 2.6 multiply_convert_fusion
  367.1 1.9 copy-done.6
  371.3 3.8 fusion.44
  376.5 5.5 fusion.45
  382.0 3.2 concatenate.54.right_ref
  385.3 4.1 pad_maximum_fusion.2.left_ref
  389.4 11.7 %shard_map.231 = bf16[2048,1152]{1,0:T(8,128)(2,1)} custom-call(s32[9]{0:T(128)} %constant.65.clone.select_ref, bf16[2,2048,512]{2,1,0:T(8,128)(2,1)} %pad_maximum_fusion.2.left_ref, bf16[512,1152]{1,0:T(8,128)(2,1)} %concatenate.54.right_ref), custom_call_target="tpu_custom_call" | custom-call | tf_op jit(solution)/shard_map/pallas_call | solution.py:244
  401.1 5.0 fusion.33
  406.1 57.8 %reduce-scatter.6.cloned.1.call-done = bf16[64,4224]{1,0:T(8,128)(2,1)} async-done(((bf16[2048,4224]{1,0:T(8,128)(2,1)}), bf16[64,4224]{1,0:T(8,128)(2,1)}) %reduce-scatter.6.cloned.1.call-update) | async-done | bytes 540688 | tf_op jit(solution)/shard_map/reduce_scatter | solution.py:354
  463.9 1.9 fusion.56
  466.3 1.8 add_convert_fusion
  468.3 29.2 %all_to_all.42 = bf16[4,512,512]{2,1,0:T(8,128)(2,1)S(1)} all-to-all(bf16[4,512,512]{2,1,0:T(8,128)(2,1)S(1)} %bitcast.164), channel_id=1, replica_groups=mesh['row'=32,'col'=4] {'col'}, dimensions={0} | all-to-all | bytes 4194304 | tf_op jit(solution)/shard_map/all_to_all | solution.py:176
  499.9 3.6 all-to-all-start.4
  505.9 21.6 %all-to-all-done.4 = bf16[4,512,512]{1,2,0:T(8,128)(2,1)S(1)} async-done(((bf16[4,512,512]{1,2,0:T(8,128)(2,1)}), bf16[4,512,512]{1,2,0:T(8,128)(2,1)S(1)}, u32[]{:S(2)}, u32[]{:S(2)}) %all-to-all-start.4) | async-done | bytes 2097184 | tf_op jit(solution)/shard_map/all_to_all | solution.py:183
  527.5 2.9 fusion.16
  531.3 5.4 all-to-all-start.6
  537.3 1.9 fusion.55
  540.3 4.1 gather_fusion.3
  544.5 7.4 %all-to-all-start.5 = ((bf16[2,512,512]{2,0,1:T(2,128)(2,1)}), bf16[2,512,512]{2,0,1:T(2,128)(2,1)S(1)}, u32[]{:S(2)}, u32[]{:S(2)}) async-start(bf16[2,512,512]{2,0,1:T(2,128)(2,1)} %bitcast.43), calls=%async_computation.6 | async-start | bytes 2097152 | tf_op jit(solution)/shard_map/all_to_all | solution.py:397
  551.9 3.8 sort.47
  557.5 11.7 %all-to-all-done.5 = bf16[2,512,512]{2,0,1:T(2,128)(2,1)S(1)} async-done(((bf16[2,512,512]{2,0,1:T(2,128)(2,1)}), bf16[2,512,512]{2,0,1:T(2,128)(2,1)S(1)}, u32[]{:S(2)}, u32[]{:S(2)}) %all-to-all-start.5) | async-done | bytes 1048608 | tf_op jit(solution)/shard_map/all_to_all | solution.py:397
  571.0 2.6 gather_fusion.5
  573.6 2.6 gather_fusion.4
  (211 shorter events, 45.7 us)
Async XLA Ops:
  7.2 21.6 %copy-start.29 = (bf16[512,512]{1,0:T(8,128)(2,1)S(1)}, bf16[512,512]{1,0:T(8,128)(2,1)}, u32[]{:S(2)}) copy-start(bf16[512,512]{1,0:T(8,128)(2,1)} %param.15) | copy-start | bytes 1572868
  7.2 22.5 %copy-start.30 = (bf16[512,512]{1,0:T(8,128)(2,1)S(1)}, bf16[512,512]{1,0:T(8,128)(2,1)}, u32[]{:S(2)}) copy-start(bf16[512,512]{1,0:T(8,128)(2,1)} %param.16) | copy-start | bytes 1572868
  7.2 132.6 %all-gather.3.cloned.1.call-start = ((), (), s32[]{:S(2)}) async-start(), calls=%async_computation.10 | async-start | bytes 4866048 | tf_op jit(solution)/shard_map/all_gather | solution.py:192
  9.0 152.9 %all-gather.5.cloned.1.call-start = ((), (), s32[]{:S(2)}) async-start(), calls=%async_computation.11 | async-start | bytes 17842176 | tf_op jit(solution)/shard_map/all_gather | solution.py:192
  20.4 16.7 %all-to-all-start.1 = ((s32[32,16,1]{1,2,0:T(1,128)}), s32[32,16,1]{1,2,0:T(1,128)S(1)}, u32[]{:S(2)}, u32[]{:S(2)}) async-start(s32[32,16,1]{1,2,0:T(1,128)} %bitcast.3), calls=%async_computation.1 | async-start | bytes 32768 | tf_op jit(solution)/shard_map/all_to_all | solution.py:281
  37.1 12.5 %copy-start.34 = (s32[32,16,1]{1,2,0:T(1,128)}, s32[32,16,1]{1,2,0:T(1,128)S(1)}, u32[]{:S(2)}) copy-start(s32[32,16,1]{1,2,0:T(1,128)S(1)} %all-to-all-done.1) | copy-start | bytes 6148
  37.1 32.0 %all-to-all-start = ((bf16[2,512,512]{2,0,1:T(2,128)(2,1)}), bf16[2,512,512]{2,0,1:T(2,128)(2,1)S(1)}, u32[]{:S(2)}, u32[]{:S(2)}) async-start(bf16[2,512,512]{2,0,1:T(2,128)(2,1)} %bitcast.2), calls=%async_computation | async-start | bytes 2097152 | tf_op jit(solution)/shard_map/all_to_all | solution.py:278
  76.4 5.3 copy-start.49
  76.4 5.8 copy-start.46
  76.4 52.7 %all-to-all-start.2 = ((bf16[4,2,512,512]{2,3,1,0:T(8,128)(2,1)}), bf16[4,2,512,512]{2,3,1,0:T(8,128)(2,1)}, u32[]{:S(2)}, u32[]{:S(2)}) async-start(bf16[4,2,512,512]{2,3,1,0:T(8,128)(2,1)} %broadcast_in_dim.22), calls=%async_computation.2 | async-start | bytes 8388608 | tf_op jit(solution)/shard_map/all_to_all | solution.py:183
  81.4 140.1 %all-reduce.3.cloned.1.call-start = ((), (), s32[]{:S(2)}) async-start(), calls=%async_computation.12 | async-start | bytes 4194304 | tf_op jit(solution)/shard_map/psum | solution.py:323
  82.3 57.5 %copy-start.36 = (f32[4,512]{1,0:T(4,128)}, f32[4,512]{1,0:T(4,128)S(1)}, u32[]{:S(2)}) copy-start(f32[4,512]{1,0:T(4,128)S(1)} %mul.296) | copy-start | bytes 24580
  82.3 64.3 %copy-start.54 = (f32[32]{0:T(128)}, f32[32]{0:T(128)S(1)}, u32[]{:S(2)}) copy-start(f32[32]{0:T(128)S(1)} %negate_power_fusion) | copy-start | bytes 388
  82.5 64.1 %copy-start.47 = (f32[512]{0:T(512)}, f32[512]{0:T(512)S(1)}, u32[]{:S(2)}) copy-start(f32[512]{0:T(512)S(1)} %fusion.80) | copy-start | bytes 6148
  82.8 68.8 %copy-start.25 = (f32[512,32]{0,1:T(8,128)}, f32[512,32]{0,1:T(8,128)S(1)}, u32[]{:S(2)}) copy-start(f32[512,32]{0,1:T(8,128)S(1)} %get-tuple-element.63) | copy-start | bytes 196612
  82.8 68.8 %copy-start.27 = (f32[512,32]{0,1:T(8,128)}, f32[512,32]{0,1:T(8,128)S(1)}, u32[]{:S(2)}) copy-start(f32[512,32]{0,1:T(8,128)S(1)} %get-tuple-element.64) | copy-start | bytes 196612
  131.4 8.4 %copy-start.44 = (f32[512]{0:T(512)}, f32[512]{0:T(512)S(1)}, u32[]{:S(2)}) copy-start(f32[512]{0:T(512)S(1)} %add_rsqrt_fusion.1) | copy-start | bytes 6148
  144.0 6.3 %copy-start.11 = (bf16[512,2048]{1,0:T(8,128)(2,1)S(1)}, bf16[512,2048]{1,0:T(8,128)(2,1)}, u32[]{:S(2)}) copy-start(bf16[512,2048]{1,0:T(8,128)(2,1)} %copy.115) | copy-start | bytes 6291460
  144.0 6.3 %copy-start.12 = (bf16[1,512,4,512]{1,3,0,2:T(8,128)(2,1)S(1)}, bf16[1,512,4,512]{1,3,0,2:T(8,128)(2,1)}, u32[]{:S(2)}) copy-start(bf16[1,512,4,512]{1,3,0,2:T(8,128)(2,1)} %fusion.21) | copy-start | bytes 6291460
  147.9 3.9 copy-start.17
  147.9 3.9 copy-start.19
  150.3 4.2 copy-start.40
  151.8 1.5 copy-start.21
  153.3 3.3 copy-start
  156.6 1.6 copy-start.42
  164.5 117.2 %reduce-scatter.4.cloned.1.call-start = ((), (), s32[]{:S(2)}) async-start(), calls=%async_computation.13 | async-start | bytes 2621440 | tf_op jit(solution)/shard_map/reduce_scatter | solution.py:333
  175.6 49.0 %copy-start.38 = (f32[2048]{0:T(1024)S(1)}, f32[2048]{0:T(1024)}, u32[]{:S(2)}) copy-start(f32[2048]{0:T(1024)} %param.24) | copy-start | bytes 24580
  221.6 3.1 copy-start.2
  224.7 3.7 copy-start.50
  228.4 6.4 %copy-start.8 = (bf16[512,2048]{0,1:T(8,128)(2,1)}, bf16[512,2048]{0,1:T(8,128)(2,1)S(1)}, u32[]{:S(2)}) copy-start(bf16[512,2048]{0,1:T(8,128)(2,1)S(1)} %get-tuple-element.40) | copy-start | bytes 6291460
  228.4 6.4 %copy-start.56 = (f32[512,1408]{1,0:T(8,128)S(1)}, f32[512,1408]{1,0:T(8,128)}, u32[]{:S(2)}) copy-start(f32[512,1408]{1,0:T(8,128)} %fusion.12) | copy-start | bytes 8650756
  252.1 90.2 %all-reduce.5.cloned.1.call-start = ((), (), s32[]{:S(2)}) async-start(), calls=%async_computation.14 | async-start | bytes 4194304 | tf_op jit(solution)/shard_map/psum | solution.py:346
  252.3 5.6 copy-start.13
  281.7 182.2 %reduce-scatter.6.cloned.1.call-start = ((), (), s32[]{:S(2)}) async-start(), calls=%async_computation.15 | async-start | bytes 17842176 | tf_op jit(solution)/shard_map/reduce_scatter | solution.py:354
  281.7 4.7 copy-start.14
  281.8 4.7 copy-start.16
  346.4 2.0 copy-start.43
  346.4 2.1 copy-start.39
  346.4 2.1 copy-start.51
  346.5 230.7 %reduce-scatter.8.cloned.1.call-start = ((), (), s32[]{:S(2)}) async-start(), calls=%async_computation.16 | async-start | bytes 4866048 | tf_op jit(solution)/shard_map/reduce_scatter | solution.py:385
  348.5 4.1 copy-start.1
  348.5 4.7 copy-start.5
  352.3 9.7 %slice-start = ((s8[8388608]{0:T(1024)(128)(4,1)}), s8[4194304]{0:T(1024)(128)(4,1)S(1)}, s32[]{:S(2)}) async-start(s8[8388608]{0:T(1024)(128)(4,1)} %bitcast.159), calls=%async_computation.17 | async-start | bytes 8388608
  353.3 8.7 %slice-start.1 = ((s8[8388608]{0:T(1024)(128)(4,1)}), s8[4194304]{0:T(1024)(128)(4,1)S(1)}, s32[]{:S(2)}) async-start(s8[8388608]{0:T(1024)(128)(4,1)} %bitcast.159), calls=%async_computation.18 | async-start | bytes 8388608
  357.2 4.7 copy-start.9
  357.2 4.7 copy-start.41
  364.5 4.5 copy-start.18
  364.5 4.5 copy-start.20
  367.1 1.9 copy-start.6
  369.0 2.3 copy-start.22
  369.0 2.3 copy-start.24
  370.2 4.9 copy-start.48
  370.2 4.9 copy-start.55
  376.5 8.8 %copy-start.7 = (bf16[1,2048,512]{2,1,0:T(8,128)(2,1)S(1)}, bf16[1,2048,512]{2,1,0:T(8,128)(2,1)}, u32[]{:S(2)}) copy-start(bf16[1,2048,512]{2,1,0:T(8,128)(2,1)} %get-tuple-element.37) | copy-start | bytes 6291460
  463.9 2.4 copy-start.3
  498.2 6.1 %copy-start.35 = (s32[32,16,1]{1,2,0:T(1,128)S(1)}, s32[32,16,1]{1,2,0:T(1,128)}, u32[]{:S(2)}) copy-start(s32[32,16,1]{1,2,0:T(1,128)} %copy-done.34) | copy-start | bytes 6148
  498.2 6.2 %copy-start.31 = (bf16[512,512]{0,1:T(8,128)(2,1)S(1)}, bf16[512,512]{0,1:T(8,128)(2,1)}, u32[]{:S(2)}) copy-start(bf16[512,512]{0,1:T(8,128)(2,1)} %reduce-scatter.4.cloned.1.call-done) | copy-start | bytes 1572868
  498.4 29.1 %copy-start.37 = (f32[4,512]{1,0:T(4,128)S(1)}, f32[4,512]{1,0:T(4,128)}, u32[]{:S(2)}) copy-start(f32[4,512]{1,0:T(4,128)} %copy-done.36) | copy-start | bytes 24580
  498.4 29.1 %copy-start.45 = (f32[512]{0:T(512)S(1)}, f32[512]{0:T(512)}, u32[]{:S(2)}) copy-start(f32[512]{0:T(512)} %copy-done.44) | copy-start | bytes 6148
  499.9 27.6 %all-to-all-start.4 = ((bf16[4,512,512]{1,2,0:T(8,128)(2,1)}), bf16[4,512,512]{1,2,0:T(8,128)(2,1)S(1)}, u32[]{:S(2)}, u32[]{:S(2)}) async-start(bf16[4,512,512]{1,2,0:T(8,128)(2,1)} %broadcast_in_dim.25), calls=%async_computation.5 | async-start | bytes 4194304 | tf_op jit(solution)/shard_map/all_to_all | solution.py:183
  531.3 13.2 %all-to-all-start.6 = ((f32[32,1,128]{2,1,0:T(1,128)}), f32[32,1,128]{2,1,0:T(1,128)S(1)}, u32[]{:S(2)}, u32[]{:S(2)}) async-start(f32[32,1,128]{2,1,0:T(1,128)} %reshape.509), calls=%async_computation.7 | async-start | bytes 32768 | tf_op jit(solution)/shard_map/all_to_all | solution.py:157
  539.2 12.6 %copy-start.53 = (s32[512]{0:T(512)S(1)}, s32[512]{0:T(512)}, u32[]{:S(2)}) copy-start(s32[512]{0:T(512)} %copy-done.52) | copy-start | bytes 6148
  544.5 24.7 %all-to-all-start.5 = ((bf16[2,512,512]{2,0,1:T(2,128)(2,1)}), bf16[2,512,512]{2,0,1:T(2,128)(2,1)S(1)}, u32[]{:S(2)}, u32[]{:S(2)}) async-start(bf16[2,512,512]{2,0,1:T(2,128)(2,1)} %bitcast.43), calls=%async_computation.6 | async-start | bytes 2097152 | tf_op jit(solution)/shard_map/all_to_all | solution.py:397
  571.0 5.3 copy-start.10
  (8 other events, 8.4 us)
Sparse Core Ops, SparseCore 0:
  10.9 59.4 all-gather.2
  72.6 72.3 all-gather.4
  164.6 56.9 all-reduce.2
  252.2 29.4 reduce-scatter.3
  283.9 58.3 all-reduce.4
  346.6 117.2 reduce-scatter.5
  468.1 82.8 reduce-scatter.7

commit v8 on v7

--- a/solution.py
+++ b/solution.py
@@ -192,34 +192,13 @@
     return lax.all_gather(jnp.concatenate(parts, axis=1), "row", axis=0, tiled=True)
 
 
-def grad_block_kernel(select_ref, left_ref, right_ref, tail_ref, out_ref):
-    step = pl.program_id(0)
-    last = pl.num_programs(0) - 1
-
-    @pl.when(step < last)
-    def _():
-        out_ref[...] = jnp.dot(
-            left_ref[0], right_ref[...], preferred_element_type=jnp.float32
-        ).astype(out_ref.dtype)
-
-    @pl.when(step == last)
-    def _():
-        out_ref[...] = tail_ref[...]
-
-
 def grad_plain_kernel(select_ref, left_ref, right_ref, out_ref):
     out_ref[...] = jnp.dot(
         left_ref[0], right_ref[...], preferred_element_type=jnp.float32
     ).astype(out_ref.dtype)
 
 
-def gain_tail_of(gain_grads):
-    columns = [grad[:, None] for grad in gain_grads]
-    padding = jnp.zeros((gain_grads[0].shape[0], GRAD_BLOCK - len(columns)), jnp.float32)
-    return jnp.concatenate(columns + [padding], axis=1).astype(jnp.bfloat16)
-
-
-def packed_weight_grads(lefts, segments, tail=None):
+def packed_weight_grads(lefts, segments):
     left_stack = jnp.stack([left.T for left in lefts])
     right = jnp.concatenate([seg for _, seg in segments], axis=1)
     column_owner = []
@@ -234,15 +213,8 @@
         pl.BlockSpec((1, features, tokens), lambda j, sel: (sel[j], 0, 0)),
         pl.BlockSpec((tokens, GRAD_BLOCK), lambda j, sel: (0, jnp.minimum(j, right_blocks - 1))),
     ]
-    operands = [left_stack, right]
-    kernel = grad_plain_kernel
-    if tail is not None:
-        select.append(select[-1])
-        in_specs.append(pl.BlockSpec((features, GRAD_BLOCK), lambda j, sel: (0, 0)))
-        operands.append(tail)
-        kernel = grad_block_kernel
     return pl.pallas_call(
-        kernel,
+        grad_plain_kernel,
         out_shape=jax.ShapeDtypeStruct((features, len(select) * GRAD_BLOCK), jnp.bfloat16),
         grid_spec=pltpu.PrefetchScalarGridSpec(
             num_scalar_prefetch=1,
@@ -250,7 +222,7 @@
             in_specs=in_specs,
             out_specs=pl.BlockSpec((features, GRAD_BLOCK), lambda j, sel: (0, j)),
         ),
-    )(jnp.asarray(select, dtype=jnp.int32), *operands)
+    )(jnp.asarray(select, dtype=jnp.int32), left_stack, right)
 
 
 def body(
@@ -271,13 +243,10 @@
     row_count = tokens.shape[0]
     quarter = tokens.shape[1]
     col_start = lax.axis_index("col") * quarter
-    group_size = HEADS // KV
     send_order = jnp.argsort(destination)
     slot_ids = destination[send_order] % row_count
-    arrived_pair, arrived_slots = (
-        lax.all_to_all(
-            jnp.stack([tokens, cotangent])[:, send_order], "row", split_axis=1, concat_axis=1, tiled=True
-        ),
+    arrived_rows, arrived_slots = (
+        lax.all_to_all(tokens[send_order], "row", split_axis=0, concat_axis=0, tiled=True),
         lax.all_to_all(slot_ids, "row", split_axis=0, concat_axis=0, tiled=True),
     )
     placing = jnp.argsort(arrived_slots)
@@ -285,8 +254,7 @@
     ffn_widths = [w_gate.shape[1], w_up.shape[1], w_down.shape[1]]
     attn_packed = gather_rows([w_query, w_key, w_value, w_output])
     ffn_packed = gather_rows([w_gate, w_up, w_down])
-    full_pair = col_gather(arrived_pair[:, placing])
-    full_rows, full_grads = full_pair[0], full_pair[1]
+    full_rows = col_gather(arrived_rows[placing])
     query_w, key_w, value_w, output_w = split_columns(attn_packed, attn_widths)
     cosine, sine = rope_tables(positions_of(segment_ids))
     allowed = allowed_pairs(segment_ids)
@@ -319,7 +287,11 @@
         .astype(jnp.bfloat16)
     )
     attn_terms = matmul(mixed, output_w.T)
-    attn_terms, ffn_packed = lax.optimization_barrier((attn_terms, ffn_packed))
+    sorted_grads, attn_terms, ffn_packed = lax.optimization_barrier(
+        (cotangent[send_order], attn_terms, ffn_packed)
+    )
+    arrived_grads = lax.all_to_all(sorted_grads, "row", split_axis=0, concat_axis=0, tiled=True)
+    full_grads = col_gather(arrived_grads[placing])
     attn_full = lax.psum(attn_terms.astype(jnp.bfloat16), "col").astype(jnp.float32)
     resid = rows_wide + attn_full
     inv_two = rms_scale(resid)
@@ -373,17 +345,17 @@
     normed_terms_one = (
         matmul(query_grad, query_w.T) + matmul(key_grad, key_w.T) + matmul(value_grad, value_w.T)
     )
-    attn_grads_packed, ffn_grads_local = lax.optimization_barrier(
+    attn_grads_packed, ffn_grads_local, normed_grad_one = lax.optimization_barrier(
         (
             packed_weight_grads(
                 [normed_one, attn_grad_low],
                 [(0, query_grad), (0, key_grad), (0, value_grad), (1, mixed)],
             ),
             ffn_grads_local,
+            col_sum(normed_terms_one.astype(jnp.bfloat16)),
         )
     )
     attn_grads_local = lax.psum_scatter(attn_grads_packed, "row", scatter_dimension=0, tiled=True)
-    normed_grad_one = col_sum(normed_terms_one.astype(jnp.bfloat16))
     rows_norm_grad, attn_gain_grad = norm_back(rows_wide, inv_one, attn_gain, normed_grad_one)
     rows_grad = resid_grad + rows_norm_grad
     input_share = lax.dynamic_slice_in_dim(rows_grad, col_start, quarter, 1).astype(jnp.bfloat16)

time: 598 us -> 577 us (0.965)
  waiting for transfers between devices: 239 us -> 220 us
  blocking collectives: 29.2 us -> 46.7 us
  matrix products: 81.4 us -> 67.4 us
    reduce_scatter x1, waiting for transfers between devices: 57.8 us -> 20.6 us  [body(): lax.psum_scatter(ffn_grads_packed, 'row', scatter_dimension=0, tiled=True)]
    reduce_scatter x1, waiting for transfers between devices: 0.01 us -> 31.4 us  [body(): lax.psum_scatter(attn_grads_packed, 'row', scatter_dimension=0, tiled=True)]
    psum x1, waiting for transfers between devices: 45.9 us -> 21.4 us  [body(): lax.psum(attn_terms.astype(jnp.bfloat16), 'col').astype(jnp.float32)]
    all_gather x2, waiting for transfers between devices: 0.02 us -> 20.2 us  [gather_rows(): lax.all_gather(jnp.concatenate(parts, axis=1), 'row', axis=0, tiled=True)]
    all_to_all x0 -> x1, blocking collectives: none -> 17.1 us  [body(): lax.all_to_all(sorted_grads, 'row', split_axis=0, concat_axis=0, tiled=True)]
    all_to_all x1, waiting for transfers between devices: 19.6 us -> 7.56 us  [body(): lax.all_to_all(tokens[send_order], 'row', split_axis=0, concat_axis=0, ti...]
    dot_general x14, matrix products: 65.6 us -> 58.4 us  [matmul(): return jnp.dot(left, right, preferred_element_type=jnp.float32)]
    convert_element_type x2 -> x1, other arithmetic: 8.4 us -> 1.84 us  [body(): normed_one = (rows_wide * inv_one * attn_gain).astype(jnp.bfloat16)]
  transfers between devices with their start and end apart: 13 -> 14, of which waited for: 8 -> 12; matrix products, arithmetic and copies ran while one was open for 29% -> 28% of each run, Pallas kernels for 8% -> 8%
where the time goes in v8:
time: 577 us; the launch traced here: 570 us
  waiting for transfers between devices  220 us (38%)
  other arithmetic  73.3 us (13%)
  matrix products  67.4 us (12%)
  local copies, waits for them, and re-layouts  62.7 us (11%)
  blocking collectives  46.7 us (8%)
  Pallas kernels  45.5 us (8%)
  starting transfers between devices  39.4 us (7%)
  between operations  15.3 us (3%)
    all_to_all x3, waiting for transfers between devices, col_gather(): lax.all_to_all(copies, 'col', split_axis=0, concat_axis=0, tiled=True)  63.6 us
    dot_general x14, matrix products, matmul(): return jnp.dot(left, right, preferred_element_type=jnp.float32)  58.4 us
    pallas_call x2, Pallas kernels, packed_weight_grads(): pl.pallas_call(grad_plain_kernel, out_shape=jax.ShapeDtypeStruct((feature...  45.5 us
    reduce_scatter x1, waiting for transfers between devices, body(): lax.psum_scatter(attn_grads_packed, 'row', scatter_dimension=0, tiled=True)  31.4 us
    all_to_all x1, blocking collectives, col_scatter(): lax.all_to_all(blocks, 'col', split_axis=0, concat_axis=0, tiled=True)  29.5 us
    psum x1, waiting for transfers between devices, body(): lax.psum(attn_terms.astype(jnp.bfloat16), 'col').astype(jnp.float32)  21.4 us
    reduce_scatter x1, waiting for transfers between devices, body(): lax.psum_scatter(ffn_grads_packed, 'row', scatter_dimension=0, tiled=True)  20.6 us
    all_gather x2, waiting for transfers between devices, gather_rows(): lax.all_gather(jnp.concatenate(parts, axis=1), 'row', axis=0, tiled=True)  20.2 us
  transfers between devices with their start and end apart: 14, of which 12 were waited for; matrix products, arithmetic and copies ran while one was open for 28% of the time, Pallas kernels for 8%

profile of v8, /device:TPU:0, one launch (start us, length us, event | category | flops | bytes accessed | tf_op | source)
XLA Modules:
  0.0 570.4 jit_solution(10371285244621652181)
XLA Ops:
  9.0 1.9 pad_maximum_fusion.4
  11.0 4.4 sort.45
  16.0 3.6 gather_fusion.1
  20.3 8.4 %all-to-all-start.1 = ((s32[32,16,1]{1,2,0:T(1,128)}), s32[32,16,1]{1,2,0:T(1,128)S(1)}, u32[]{:S(2)}, u32[]{:S(2)}) async-start(s32[32,16,1]{1,2,0:T(1,128)} %bitcast.2), calls=%async_computation.1 | async-start | bytes 32768 | tf_op jit(solution)/shard_map/all_to_all | solution.py:250
  28.8 2.6 gather_fusion
  31.4 4.6 all-to-all-done.1
  36.0 3.9 all-to-all-start
  41.2 3.8 sort.46
  45.0 7.6 %all-to-all-done = bf16[32,16,512]{2,1,0:T(8,128)(2,1)S(1)} async-done(((bf16[32,16,512]{2,1,0:T(8,128)(2,1)}), bf16[32,16,512]{2,1,0:T(8,128)(2,1)S(1)}, u32[]{:S(2)}, u32[]{:S(2)}) %all-to-all-start) | async-done | bytes 524320 | tf_op jit(solution)/shard_map/all_to_all | solution.py:249
  52.6 2.0 gather_fusion.2
  56.3 4.8 all-to-all-start.2
  61.7 2.0 gather_fusion.3
  64.5 23.2 %all-to-all-done.2 = bf16[4,512,512]{1,2,0:T(8,128)(2,1)S(1)} async-done(((bf16[4,512,512]{1,2,0:T(8,128)(2,1)}), bf16[4,512,512]{1,2,0:T(8,128)(2,1)S(1)}, u32[]{:S(2)}, u32[]{:S(2)}) %all-to-all-start.2) | async-done | bytes 2097184 | tf_op jit(solution)/shard_map/all_to_all | solution.py:183
  88.2 1.9 fusion.18
  90.1 1.8 multiply_convert_fusion.2
  92.0 3.1 slice_bitcast_fusion
  95.1 4.0 copy.114
  99.1 2.6 convolution_bitcast_fusion.1
  102.9 2.4 fusion.45
  109.6 2.1 copy-done.2
  114.0 4.3 fusion.28
  118.3 20.2 %all-gather.5.cloned.1.call-done = bf16[2048,4224]{1,0:T(8,128)(2,1)} async-done(((bf16[64,4224]{1,0:T(8,128)(2,1)}), bf16[2048,4224]{1,0:T(8,128)(2,1)}) %all-gather.5.cloned.1.call-update) | async-done | bytes 17301520 | tf_op jit(solution)/shard_map/all_gather | solution.py:192
  138.5 17.1 %all_to_all.66 = bf16[32,16,512]{2,1,0:T(8,128)(2,1)S(1)} all-to-all(bf16[32,16,512]{2,1,0:T(8,128)(2,1)S(1)} %bitcast.174), channel_id=1, replica_groups=mesh['row'=32,'col'=4] {'row'}, dimensions={0} | all-to-all | bytes 1048576 | tf_op jit(solution)/shard_map/all_to_all | solution.py:293
  155.6 2.0 gather_fusion.4
  159.3 4.4 all-to-all-start.4
  163.8 3.9 copy.119
  167.8 36.7 %all-to-all-done.4 = bf16[4,512,512]{1,2,0:T(8,128)(2,1)} async-done(((bf16[4,512,512]{1,2,0:T(8,128)(2,1)}), bf16[4,512,512]{1,2,0:T(8,128)(2,1)}, u32[]{:S(2)}, u32[]{:S(2)}) %all-to-all-start.4) | async-done | bytes 2097184 | tf_op jit(solution)/shard_map/all_to_all | solution.py:183
  204.6 8.3 %fusion.12 = f32[512,1408]{1,0:T(8,128)} fusion(bf16[512,2048]{0,1:T(8,128)(2,1)} %bitcast.24, bf16[2048,4224]{1,0:T(8,128)(2,1)} %all-gather.5.cloned.1.call-done), kind=kOutput, calls=%fused_computation.26 | convolution fusion | flops 2952790016 | bytes 10747904 | tf_op jit(solution)/shard_map/dot_general | solution.py:68
  212.9 21.4 %all-reduce.3.cloned.1.call-done = bf16[512,2048]{0,1:T(8,128)(2,1)} async-done(((bf16[512,2048]{0,1:T(8,128)(2,1)}), bf16[512,2048]{0,1:T(8,128)(2,1)}) %all-reduce.3.cloned.1.call-update) | async-done | bytes 2097168 | tf_op jit(solution)/shard_map/psum | solution.py:295
  234.3 2.5 multiply_reduce_fusion.5
  237.6 6.4 %fusion.8 = f32[512,1408]{1,0:T(8,128)S(1)} fusion(bf16[512,2048]{0,1:T(8,128)(2,1)S(1)} %multiply_convert_fusion.1, bf16[2048,4224]{1,0:T(8,128)(2,1)} %all-gather.5.cloned.1.call-done), kind=kOutput, calls=%fused_computation.22 | convolution fusion | flops 2952790016 | bytes 10747904 | tf_op jit(solution)/shard_map/dot_general | solution.py:68
  244.0 8.7 %multiply_convert_fusion.5 = (bf16[512,1408]{1,0:T(8,128)(2,1)S(1)}, bf16[512,1408]{1,0:T(8,128)(2,1)}, bf16[512,1408]{1,0:T(8,128)(2,1)S(1)}) fusion(f32[512,1408]{1,0:T(8,128)S(1)} %copy-done.51, f32[512,1408]{1,0:T(8,128)S(1)} %fusion.8, bf16[512,2048]{0,1:T(8,128)(2,1)S(1)} %multiply_convert_fusion.1, bf16[2048,4224]{1,0:T(8,128)(2,1)} %all-gather.5.cloned.1.call-done), kind=kOutput, calls=%fused_computation.54 | convolution fusion | flops 2964324352 | bytes 17956864 | tf_op jit(solution)/shard_map/dot_general | solution.py:68
  253.8 7.3 %fusion.23 = bf16[512,2048]{0,1:T(8,128)(2,1)} fusion(bf16[512,1408]{1,0:T(8,128)(2,1)S(1)} %get-tuple-element.46, bf16[2048,4224]{1,0:T(8,128)(2,1)} %all-gather.5.cloned.1.call-done), kind=kOutput, calls=%fused_computation.51 | convolution fusion | flops 2953838592 | bytes 9306112 | tf_op jit(solution)/shard_map/dot_general | solution.py:68
  261.5 5.6 fusion.2
  267.1 7.4 %add_convert_fusion.1 = bf16[512,2048]{0,1:T(8,128)(2,1)} fusion(f32[512,2048]{0,1:T(8,128)S(1)} %fusion.2, bf16[512,1408]{1,0:T(8,128)(2,1)S(1)} %copy-done.12, bf16[2048,4224]{1,0:T(8,128)(2,1)} %all-gather.5.cloned.1.call-done), kind=kOutput, calls=%fused_computation.46 | convolution fusion | flops 2954887168 | bytes 13500416 | tf_op jit(solution)/shard_map/dot_general | solution.py:68
  274.5 16.3 %reduce-scatter.4.cloned.1.call-done = bf16[512,512]{0,1:T(8,128)(2,1)} async-done(((bf16[512,2048]{0,1:T(8,128)(2,1)}), bf16[512,512]{0,1:T(8,128)(2,1)}) %reduce-scatter.4.cloned.1.call-update) | async-done | bytes 524304 | tf_op jit(solution)/shard_map/reduce_scatter | solution.py:305
  290.9 4.7 pad_maximum_fusion.1.left_ref
  295.6 2.1 pad_maximum_fusion.right_ref
  297.8 33.9 %shard_map.230 = bf16[2048,4224]{1,0:T(8,128)(2,1)} custom-call(s32[33]{0:T(128)} %constant.64.clone.select_ref, bf16[2,2048,512]{2,1,0:T(8,128)(2,1)} %pad_maximum_fusion.1.left_ref, bf16[512,4224]{1,0:T(8,128)(2,1)} %pad_maximum_fusion.right_ref), custom_call_target="tpu_custom_call" | custom-call | tf_op jit(solution)/shard_map/pallas_call | solution.py:216
  331.6 19.8 %all-reduce.5.cloned.1.call-done = bf16[512,2048]{0,1:T(8,128)(2,1)} async-done(((bf16[512,2048]{0,1:T(8,128)(2,1)}), bf16[512,2048]{0,1:T(8,128)(2,1)}) %all-reduce.5.cloned.1.call-update) | async-done | bytes 2097168 | tf_op jit(solution)/shard_map/psum | solution.py:318
  351.4 4.2 convert_element_type.157
  356.4 5.0 multiply_reduce_fusion.1
  362.6 4.8 convert_bitcast_fusion
  369.3 2.5 multiply_reduce_fusion
  371.9 2.6 multiply_convert_fusion
  383.1 29.5 %all_to_all.67 = bf16[4,512,512]{2,1,0:T(8,128)(2,1)} all-to-all(bf16[4,512,512]{2,1,0:T(8,128)(2,1)S(1)} %bitcast.165), channel_id=1, replica_groups=mesh['row'=32,'col'=4] {'col'}, dimensions={0} | all-to-all | bytes 4194304 | tf_op jit(solution)/shard_map/all_to_all | solution.py:176
  412.6 2.9 reduce_sum.98
  418.2 4.5 all-to-all-start.6
  425.0 3.0 concatenate.54.right_ref
  428.0 4.9 pad_maximum_fusion.2.left_ref
  432.8 11.6 %shard_map.231 = bf16[2048,1152]{1,0:T(8,128)(2,1)} custom-call(s32[9]{0:T(128)} %constant.65.clone.select_ref, bf16[2,2048,512]{2,1,0:T(8,128)(2,1)} %pad_maximum_fusion.2.left_ref, bf16[512,1152]{1,0:T(8,128)(2,1)} %concatenate.54.right_ref), custom_call_target="tpu_custom_call" | custom-call | tf_op jit(solution)/shard_map/pallas_call | solution.py:216
  444.5 3.7 all-to-all-done.6
  448.1 4.3 convert_element_type.175
  452.5 20.6 %reduce-scatter.6.cloned.1.call-done = bf16[64,4224]{1,0:T(8,128)(2,1)} async-done(((bf16[2048,4224]{1,0:T(8,128)(2,1)}), bf16[64,4224]{1,0:T(8,128)(2,1)}) %reduce-scatter.6.cloned.1.call-update) | async-done | bytes 540688 | tf_op jit(solution)/shard_map/reduce_scatter | solution.py:326
  473.1 3.8 sort.47
  477.0 5.6 multiply_reduce_fusion.2
  483.5 5.4 all-to-all-start.8
  488.9 2.9 fusion.50
  492.9 4.1 gather_fusion.5
  497.0 7.5 %all-to-all-start.7 = ((bf16[2,512,512]{2,0,1:T(2,128)(2,1)}), bf16[2,512,512]{2,0,1:T(2,128)(2,1)S(1)}, u32[]{:S(2)}, u32[]{:S(2)}) async-start(bf16[2,512,512]{2,0,1:T(2,128)(2,1)} %bitcast.51), calls=%async_computation.9 | async-start | bytes 2097152 | tf_op jit(solution)/shard_map/all_to_all | solution.py:369
  507.4 14.4 %all-to-all-done.7 = bf16[2,512,512]{2,0,1:T(2,128)(2,1)S(1)} async-done(((bf16[2,512,512]{2,0,1:T(2,128)(2,1)}), bf16[2,512,512]{2,0,1:T(2,128)(2,1)S(1)}, u32[]{:S(2)}, u32[]{:S(2)}) %all-to-all-start.7) | async-done | bytes 1048608 | tf_op jit(solution)/shard_map/all_to_all | solution.py:369
  523.6 2.6 gather_fusion.7
  526.3 2.6 gather_fusion.6
  528.9 31.4 %reduce-scatter.8.cloned.1.call-done = bf16[64,1152]{1,0:T(8,128)(2,1)} async-done(((bf16[2048,1152]{1,0:T(8,128)(2,1)}), bf16[64,1152]{1,0:T(8,128)(2,1)}) %reduce-scatter.8.cloned.1.call-update) | async-done | bytes 147472 | tf_op jit(solution)/shard_map/reduce_scatter | solution.py:358
  (208 shorter events, 46.8 us)
Async XLA Ops:
  7.2 21.6 %copy-start = (bf16[512,512]{1,0:T(8,128)(2,1)S(1)}, bf16[512,512]{1,0:T(8,128)(2,1)}, u32[]{:S(2)}) copy-start(bf16[512,512]{1,0:T(8,128)(2,1)} %param.15) | copy-start | bytes 1572868
  7.2 84.8 %all-gather.3.cloned.1.call-start = ((), (), s32[]{:S(2)}) async-start(), calls=%async_computation.12 | async-start | bytes 4866048 | tf_op jit(solution)/shard_map/all_gather | solution.py:192
  9.0 129.6 %all-gather.5.cloned.1.call-start = ((), (), s32[]{:S(2)}) async-start(), calls=%async_computation.13 | async-start | bytes 17842176 | tf_op jit(solution)/shard_map/all_gather | solution.py:192
  20.3 15.7 %all-to-all-start.1 = ((s32[32,16,1]{1,2,0:T(1,128)}), s32[32,16,1]{1,2,0:T(1,128)S(1)}, u32[]{:S(2)}, u32[]{:S(2)}) async-start(s32[32,16,1]{1,2,0:T(1,128)} %bitcast.2), calls=%async_computation.1 | async-start | bytes 32768 | tf_op jit(solution)/shard_map/all_to_all | solution.py:250
  36.0 16.5 %copy-start.30 = (s32[32,16,1]{1,2,0:T(1,128)}, s32[32,16,1]{1,2,0:T(1,128)S(1)}, u32[]{:S(2)}) copy-start(s32[32,16,1]{1,2,0:T(1,128)S(1)} %all-to-all-done.1) | copy-start | bytes 6148
  36.0 16.5 %all-to-all-start = ((bf16[32,16,512]{2,1,0:T(8,128)(2,1)}), bf16[32,16,512]{2,1,0:T(8,128)(2,1)S(1)}, u32[]{:S(2)}, u32[]{:S(2)}) async-start(bf16[32,16,512]{2,1,0:T(8,128)(2,1)} %bitcast), calls=%async_computation | async-start | bytes 1048576 | tf_op jit(solution)/shard_map/all_to_all | solution.py:249
  54.5 6.6 %copy-start.46 = (s32[512]{0:T(512)S(1)}, s32[512]{0:T(512)}, u32[]{:S(2)}) copy-start(s32[512]{0:T(512)} %param.18) | copy-start | bytes 6148
  54.6 7.2 %copy-start.32 = (f32[2048]{0:T(1024)S(1)}, f32[2048]{0:T(1024)}, u32[]{:S(2)}) copy-start(f32[2048]{0:T(1024)} %param.19) | copy-start | bytes 24580
  54.6 7.2 %copy-start.6 = (bf16[512,512]{1,0:T(8,128)(2,1)S(1)}, bf16[512,512]{1,0:T(8,128)(2,1)}, u32[]{:S(2)}) copy-start(bf16[512,512]{1,0:T(8,128)(2,1)} %param.16) | copy-start | bytes 1572868
  56.3 31.4 %all-to-all-start.2 = ((bf16[4,512,512]{1,2,0:T(8,128)(2,1)}), bf16[4,512,512]{1,2,0:T(8,128)(2,1)S(1)}, u32[]{:S(2)}, u32[]{:S(2)}) async-start(bf16[4,512,512]{1,2,0:T(8,128)(2,1)} %broadcast_in_dim.24), calls=%async_computation.2 | async-start | bytes 4194304 | tf_op jit(solution)/shard_map/all_to_all | solution.py:183
  63.7 37.9 %copy-start.49 = (f32[32]{0:T(128)}, f32[32]{0:T(128)S(1)}, u32[]{:S(2)}) copy-start(f32[32]{0:T(128)S(1)} %negate_power_fusion) | copy-start | bytes 388
  63.9 37.7 %copy-start.42 = (f32[512]{0:T(512)}, f32[512]{0:T(512)S(1)}, u32[]{:S(2)}) copy-start(f32[512]{0:T(512)S(1)} %fusion.76) | copy-start | bytes 6148
  64.3 42.4 %copy-start.24 = (f32[512,32]{0,1:T(8,128)}, f32[512,32]{0,1:T(8,128)S(1)}, u32[]{:S(2)}) copy-start(f32[512,32]{0,1:T(8,128)S(1)} %get-tuple-element.66) | copy-start | bytes 196612
  64.3 42.4 %copy-start.26 = (f32[512,32]{0,1:T(8,128)}, f32[512,32]{0,1:T(8,128)S(1)}, u32[]{:S(2)}) copy-start(f32[512,32]{0,1:T(8,128)S(1)} %get-tuple-element.67) | copy-start | bytes 196612
  88.2 3.7 copy-start.40
  99.1 6.3 %copy-start.10 = (bf16[512,2048]{1,0:T(8,128)(2,1)S(1)}, bf16[512,2048]{1,0:T(8,128)(2,1)}, u32[]{:S(2)}) copy-start(bf16[512,2048]{1,0:T(8,128)(2,1)} %copy.114) | copy-start | bytes 6291460
  99.1 6.3 %copy-start.11 = (bf16[4,512,512]{1,2,0:T(8,128)(2,1)S(1)}, bf16[4,512,512]{1,2,0:T(8,128)(2,1)}, u32[]{:S(2)}) copy-start(bf16[4,512,512]{1,2,0:T(8,128)(2,1)} %fusion.18) | copy-start | bytes 6291460
  102.9 3.9 copy-start.16
  102.9 3.9 copy-start.18
  105.3 4.2 copy-start.36
  106.8 1.5 copy-start.20
  106.8 1.5 copy-start.22
  108.3 3.3 copy-start.2
  111.6 1.6 copy-start.38
  159.3 45.2 %all-to-all-start.4 = ((bf16[4,512,512]{1,2,0:T(8,128)(2,1)}), bf16[4,512,512]{1,2,0:T(8,128)(2,1)}, u32[]{:S(2)}, u32[]{:S(2)}) async-start(bf16[4,512,512]{1,2,0:T(8,128)(2,1)} %broadcast_in_dim.27), calls=%async_computation.4 | async-start | bytes 4194304 | tf_op jit(solution)/shard_map/all_to_all | solution.py:183
  163.8 70.5 %all-reduce.3.cloned.1.call-start = ((), (), s32[]{:S(2)}) async-start(), calls=%async_computation.14 | async-start | bytes 4194304 | tf_op jit(solution)/shard_map/psum | solution.py:295
  167.8 123.0 %reduce-scatter.4.cloned.1.call-start = ((), (), s32[]{:S(2)}) async-start(), calls=%async_computation.15 | async-start | bytes 2621440 | tf_op jit(solution)/shard_map/reduce_scatter | solution.py:305
  212.9 23.9 %copy-start.34 = (f32[2048]{0:T(1024)S(1)}, f32[2048]{0:T(1024)}, u32[]{:S(2)}) copy-start(f32[2048]{0:T(1024)} %param.24) | copy-start | bytes 24580
  234.3 2.5 copy-start.4
  237.6 6.5 %copy-start.7 = (bf16[512,2048]{0,1:T(8,128)(2,1)}, bf16[512,2048]{0,1:T(8,128)(2,1)S(1)}, u32[]{:S(2)}) copy-start(bf16[512,2048]{0,1:T(8,128)(2,1)S(1)} %multiply_convert_fusion.1) | copy-start | bytes 6291460
  237.6 6.5 %copy-start.51 = (f32[512,1408]{1,0:T(8,128)S(1)}, f32[512,1408]{1,0:T(8,128)}, u32[]{:S(2)}) copy-start(f32[512,1408]{1,0:T(8,128)} %fusion.12) | copy-start | bytes 8650756
  252.8 1.1 copy-start.14
  261.2 90.2 %all-reduce.5.cloned.1.call-start = ((), (), s32[]{:S(2)}) async-start(), calls=%async_computation.16 | async-start | bytes 4194304 | tf_op jit(solution)/shard_map/psum | solution.py:318
  261.5 5.6 copy-start.12
  290.8 182.2 %reduce-scatter.6.cloned.1.call-start = ((), (), s32[]{:S(2)}) async-start(), calls=%async_computation.17 | async-start | bytes 17842176 | tf_op jit(solution)/shard_map/reduce_scatter | solution.py:326
  290.9 4.8 copy-start.13
  290.9 4.8 copy-start.15
  356.4 5.0 copy-start.3
  356.4 6.2 %copy-start.5 = (bf16[512,2048]{0,1:T(8,128)(2,1)S(1)}, bf16[512,2048]{0,1:T(8,128)(2,1)}, u32[]{:S(2)}) copy-start(bf16[512,2048]{0,1:T(8,128)(2,1)} %all-reduce.3.cloned.1.call-done) | copy-start | bytes 6291460
  356.4 11.1 %slice-start.2 = ((s8[4718592]{0:T(1024)(128)(4,1)}), s8[4194304]{0:T(1024)(128)(4,1)S(1)}, s32[]{:S(2)}) async-start(s8[4718592]{0:T(1024)(128)(4,1)} %bitcast.170), calls=%async_computation.21 | async-start | bytes 8388608
  361.4 7.4 %slice-start = ((s8[8388608]{0:T(1024)(128)(4,1)}), s8[4194304]{0:T(1024)(128)(4,1)S(1)}, s32[]{:S(2)}) async-start(s8[8388608]{0:T(1024)(128)(4,1)} %bitcast.157), calls=%async_computation.19 | async-start | bytes 8388608
  362.6 4.9 slice-start.3
  362.6 6.7 %slice-start.1 = ((s8[8388608]{0:T(1024)(128)(4,1)}), s8[4194304]{0:T(1024)(128)(4,1)S(1)}, s32[]{:S(2)}) async-start(s8[8388608]{0:T(1024)(128)(4,1)} %bitcast.157), calls=%async_computation.20 | async-start | bytes 8388608
  367.5 4.4 copy-start.8
  367.5 1.9 copy-start.37
  371.9 2.6 copy-start.21
  371.9 2.6 copy-start.23
  374.5 1.3 copy-start.43
  374.5 1.3 copy-start.50
  374.5 3.1 copy-start.17
  374.5 3.0 copy-start.19
  375.8 2.8 copy-start.25
  375.8 2.8 copy-start.27
  418.2 29.9 %all-to-all-start.6 = ((bf16[4,512,512]{1,2,0:T(8,128)(2,1)}), bf16[4,512,512]{1,2,0:T(8,128)(2,1)}, u32[]{:S(2)}, u32[]{:S(2)}) async-start(bf16[4,512,512]{1,2,0:T(8,128)(2,1)} %broadcast_in_dim.28), calls=%async_computation.8 | async-start | bytes 4194304 | tf_op jit(solution)/shard_map/all_to_all | solution.py:183
  422.7 137.6 %reduce-scatter.8.cloned.1.call-start = ((), (), s32[]{:S(2)}) async-start(), calls=%async_computation.18 | async-start | bytes 4866048 | tf_op jit(solution)/shard_map/reduce_scatter | solution.py:358
  444.5 28.6 %copy-start.48 = (s32[512]{0:T(512)S(1)}, s32[512]{0:T(512)}, u32[]{:S(2)}) copy-start(s32[512]{0:T(512)} %copy-done.47) | copy-start | bytes 6148
  444.5 32.4 %copy-start.31 = (s32[32,16,1]{1,2,0:T(1,128)S(1)}, s32[32,16,1]{1,2,0:T(1,128)}, u32[]{:S(2)}) copy-start(s32[32,16,1]{1,2,0:T(1,128)} %copy-done.30) | copy-start | bytes 6148
  444.5 32.5 %copy-start.33 = (f32[2048]{0:T(1024)S(1)}, f32[2048]{0:T(1024)}, u32[]{:S(2)}) copy-start(f32[2048]{0:T(1024)} %param.19) | copy-start | bytes 24580
  444.5 32.5 %copy-start.41 = (f32[512]{0:T(512)S(1)}, f32[512]{0:T(512)}, u32[]{:S(2)}) copy-start(f32[512]{0:T(512)} %copy-done.40) | copy-start | bytes 6148
  477.0 11.9 %copy-start.29 = (bf16[512,512]{0,1:T(8,128)(2,1)S(1)}, bf16[512,512]{0,1:T(8,128)(2,1)}, u32[]{:S(2)}) copy-start(bf16[512,512]{0,1:T(8,128)(2,1)} %reduce-scatter.4.cloned.1.call-done) | copy-start | bytes 1572868
  483.5 13.5 %all-to-all-start.8 = ((f32[32,1,128]{2,1,0:T(1,128)}), f32[32,1,128]{2,1,0:T(1,128)S(1)}, u32[]{:S(2)}, u32[]{:S(2)}) async-start(f32[32,1,128]{2,1,0:T(1,128)} %reshape.508), calls=%async_computation.10 | async-start | bytes 32768 | tf_op jit(solution)/shard_map/all_to_all | solution.py:157
  491.8 12.8 %copy-start.9 = (bf16[64,4224]{1,0:T(8,128)(2,1)S(1)}, bf16[64,4224]{1,0:T(8,128)(2,1)}, u32[]{:S(2)}) copy-start(bf16[64,4224]{1,0:T(8,128)(2,1)} %reduce-scatter.6.cloned.1.call-done) | copy-start | bytes 1622020
  497.0 24.8 %all-to-all-start.7 = ((bf16[2,512,512]{2,0,1:T(2,128)(2,1)}), bf16[2,512,512]{2,0,1:T(2,128)(2,1)S(1)}, u32[]{:S(2)}, u32[]{:S(2)}) async-start(bf16[2,512,512]{2,0,1:T(2,128)(2,1)} %bitcast.51), calls=%async_computation.9 | async-start | bytes 2097152 | tf_op jit(solution)/shard_map/all_to_all | solution.py:369
  523.6 39.7 %copy-start.1 = (bf16[512,512]{1,0:T(8,128)(2,1)S(1)}, bf16[512,512]{1,0:T(8,128)(2,1)}, u32[]{:S(2)}) copy-start(bf16[512,512]{1,0:T(8,128)(2,1)} %param.15) | copy-start | bytes 1572868
  (6 other events, 4.3 us)
Sparse Core Ops, SparseCore 0:
  10.9 52.1 all-gather.2
  65.3 73.1 all-gather.4
  167.9 66.3 all-reduce.2
  261.3 29.4 reduce-scatter.3
  293.0 58.3 all-reduce.4
  355.8 117.2 reduce-scatter.5
  477.2 82.9 reduce-scatter.7

commit v9 on v8

--- a/solution.py
+++ b/solution.py
@@ -245,8 +245,10 @@
     col_start = lax.axis_index("col") * quarter
     send_order = jnp.argsort(destination)
     slot_ids = destination[send_order] % row_count
-    arrived_rows, arrived_slots = (
-        lax.all_to_all(tokens[send_order], "row", split_axis=0, concat_axis=0, tiled=True),
+    arrived_pair, arrived_slots = (
+        lax.all_to_all(
+            jnp.stack([tokens, cotangent])[:, send_order], "row", split_axis=1, concat_axis=1, tiled=True
+        ),
         lax.all_to_all(slot_ids, "row", split_axis=0, concat_axis=0, tiled=True),
     )
     placing = jnp.argsort(arrived_slots)
@@ -254,7 +256,8 @@
     ffn_widths = [w_gate.shape[1], w_up.shape[1], w_down.shape[1]]
     attn_packed = gather_rows([w_query, w_key, w_value, w_output])
     ffn_packed = gather_rows([w_gate, w_up, w_down])
-    full_rows = col_gather(arrived_rows[placing])
+    placed_pair = arrived_pair[:, placing]
+    full_rows = col_gather(placed_pair[0])
     query_w, key_w, value_w, output_w = split_columns(attn_packed, attn_widths)
     cosine, sine = rope_tables(positions_of(segment_ids))
     allowed = allowed_pairs(segment_ids)
@@ -287,11 +290,10 @@
         .astype(jnp.bfloat16)
     )
     attn_terms = matmul(mixed, output_w.T)
-    sorted_grads, attn_terms, ffn_packed = lax.optimization_barrier(
-        (cotangent[send_order], attn_terms, ffn_packed)
-    )
-    arrived_grads = lax.all_to_all(sorted_grads, "row", split_axis=0, concat_axis=0, tiled=True)
-    full_grads = col_gather(arrived_grads[placing])
+    placed_grads, attn_terms, ffn_packed = lax.optimization_barrier(
+        (placed_pair[1], attn_terms, ffn_packed)
+    )
+    full_grads = col_gather(placed_grads)
     attn_full = lax.psum(attn_terms.astype(jnp.bfloat16), "col").astype(jnp.float32)
     resid = rows_wide + attn_full
     inv_two = rms_scale(resid)
@@ -302,9 +304,7 @@
     upper = matmul(normed_two, up_w)
     sigmoid_gate = jax.nn.sigmoid(gate)
     activ = (gate * sigmoid_gate * upper).astype(jnp.bfloat16)
-    ffn_share_low = lax.psum_scatter(
-        matmul(activ, down_w.T).astype(jnp.bfloat16), "col", scatter_dimension=1, tiled=True
-    )
+    ffn_share_low = col_scatter(matmul(activ, down_w.T).astype(jnp.bfloat16)).astype(jnp.bfloat16)
     act_grad = matmul(full_grads, down_w)
     gate_grad = (act_grad * upper * sigmoid_gate * (1.0 + gate * (1.0 - sigmoid_gate))).astype(
         jnp.bfloat16

time: 577 us -> 571 us (0.990)
  blocking collectives: 46.7 us -> 29.6 us
  waiting for transfers between devices: 220 us -> 208 us
  starting transfers between devices: 39.4 us -> 47.4 us
  local copies, waits for them, and re-layouts: 62.7 us -> 69 us
  other arithmetic: 73.3 us -> 79.1 us
    all_to_all x1 -> x2, waiting for transfers between devices: 7.56 us -> 33 us  [the longest x1 19.6 us: body(): lax.all_to_all(jnp.stack([tokens, cotangent])[:, send_order], 'row', spli...]
    all_to_all x1 -> x0, blocking collectives: 17.1 us -> none  [body(): lax.all_to_all(sorted_grads, 'row', split_axis=0, concat_axis=0, tiled=True)]
    reduce_scatter x1 -> x0, waiting for transfers between devices: 16.3 us -> none  [body(): lax.psum_scatter(matmul(activ, down_w.T).astype(jnp.bfloat16), 'col', sca...]
    all_gather x2, waiting for transfers between devices: 20.2 us -> 6.86 us  [gather_rows(): lax.all_gather(jnp.concatenate(parts, axis=1), 'row', axis=0, tiled=True)]
    all_to_all x1 -> x2, starting transfers between devices: 3.89 us -> 11.8 us  [the longest x1 7.38 us: body(): lax.all_to_all(jnp.stack([tokens, cotangent])[:, send_order], 'row', spli...]
  transfers between devices with their start and end apart: 14 -> 14, of which waited for: 12 -> 11; matrix products, arithmetic and copies ran while one was open for 28% -> 30% of each run, Pallas kernels for 8% -> 8%
where the time goes in v9:
time: 571 us; the launch traced here: 561 us
  waiting for transfers between devices  208 us (36%)
  other arithmetic  79.1 us (14%)
  local copies, waits for them, and re-layouts  69 us (12%)
  matrix products  67.2 us (12%)
  starting transfers between devices  47.4 us (8%)
  Pallas kernels  45.5 us (8%)
  blocking collectives  29.6 us (5%)
  between operations  15.6 us (3%)
    all_to_all x3, waiting for transfers between devices, col_gather(): lax.all_to_all(copies, 'col', split_axis=0, concat_axis=0, tiled=True)  59.8 us
    dot_general x14, matrix products, matmul(): return jnp.dot(left, right, preferred_element_type=jnp.float32)  58.2 us
    pallas_call x2, Pallas kernels, packed_weight_grads(): pl.pallas_call(grad_plain_kernel, out_shape=jax.ShapeDtypeStruct((feature...  45.5 us
    reduce_scatter x1, waiting for transfers between devices, body(): lax.psum_scatter(attn_grads_packed, 'row', scatter_dimension=0, tiled=True)  30.5 us
    all_to_all x1, blocking collectives, col_scatter(): lax.all_to_all(blocks, 'col', split_axis=0, concat_axis=0, tiled=True)  29.6 us
    psum x1, waiting for transfers between devices, body(): lax.psum(attn_terms.astype(jnp.bfloat16), 'col').astype(jnp.float32)  25.2 us
    reduce_scatter x1, waiting for transfers between devices, body(): lax.psum_scatter(ffn_grads_packed, 'row', scatter_dimension=0, tiled=True)  20.7 us
    all_to_all x1, waiting for transfers between devices, body(): lax.all_to_all(jnp.stack([tokens, cotangent])[:, send_order], 'row', spli...  19.6 us
  transfers between devices with their start and end apart: 14, of which 11 were waited for; matrix products, arithmetic and copies ran while one was open for 30% of the time, Pallas kernels for 8%

profile of v9, /device:TPU:0, one launch (start us, length us, event | category | flops | bytes accessed | tf_op | source)
XLA Modules:
  0.0 561.4 jit_solution(2183163682330953065)
XLA Ops:
  7.2 1.7 concatenate.43
  9.0 2.0 pad_maximum_fusion.5
  11.0 4.4 sort.45
  16.1 3.6 gather_fusion.1
  20.4 8.4 %all-to-all-start.1 = ((s32[32,16,1]{1,2,0:T(1,128)}), s32[32,16,1]{1,2,0:T(1,128)S(1)}, u32[]{:S(2)}, u32[]{:S(2)}) async-start(s32[32,16,1]{1,2,0:T(1,128)} %bitcast.3), calls=%async_computation.1 | async-start | bytes 32768 | tf_op jit(solution)/shard_map/all_to_all | solution.py:252
  30.5 2.4 pad_maximum_fusion.3
  32.9 4.1 gather_fusion
  37.0 7.4 %all-to-all-start = ((bf16[2,512,512]{2,0,1:T(2,128)(2,1)}), bf16[2,512,512]{2,0,1:T(2,128)(2,1)S(1)}, u32[]{:S(2)}, u32[]{:S(2)}) async-start(bf16[2,512,512]{2,0,1:T(2,128)(2,1)} %bitcast.2), calls=%async_computation | async-start | bytes 2097152 | tf_op jit(solution)/shard_map/all_to_all | solution.py:249
  45.7 3.8 sort.46
  49.5 19.6 %all-to-all-done = bf16[2,512,512]{2,0,1:T(2,128)(2,1)S(1)} async-done(((bf16[2,512,512]{2,0,1:T(2,128)(2,1)}), bf16[2,512,512]{2,0,1:T(2,128)(2,1)S(1)}, u32[]{:S(2)}, u32[]{:S(2)}) %all-to-all-start) | async-done | bytes 1048608 | tf_op jit(solution)/shard_map/all_to_all | solution.py:249
  69.1 3.6 gather_fusion.2
  77.0 4.5 all-to-all-start.2
  84.7 21.6 %all-to-all-done.2 = bf16[4,512,512]{1,2,0:T(8,128)(2,1)S(1)} async-done(((bf16[4,512,512]{1,2,0:T(8,128)(2,1)}), bf16[4,512,512]{1,2,0:T(8,128)(2,1)S(1)}, u32[]{:S(2)}, u32[]{:S(2)}) %all-to-all-start.2) | async-done | bytes 2097184 | tf_op jit(solution)/shard_map/all_to_all | solution.py:183
  106.8 2.6 fusion.18
  109.4 1.8 multiply_convert_fusion.2
  111.3 3.3 slice_bitcast_fusion
  114.6 4.2 copy.119
  118.8 2.6 convolution_bitcast_fusion.1
  122.6 2.7 fusion.45
  129.5 2.1 copy-done
  134.0 4.3 fusion.28
  138.3 6.9 %all-gather.5.cloned.1.call-done = bf16[2048,4224]{1,0:T(8,128)(2,1)} async-done(((bf16[64,4224]{1,0:T(8,128)(2,1)}), bf16[2048,4224]{1,0:T(8,128)(2,1)}) %all-gather.5.cloned.1.call-update) | async-done | bytes 17301520 | tf_op jit(solution)/shard_map/all_gather | solution.py:192
  146.8 4.4 all-to-all-start.3
  151.7 3.9 copy.124
  155.7 34.4 %all-to-all-done.3 = bf16[4,512,512]{1,2,0:T(8,128)(2,1)} async-done(((bf16[4,512,512]{1,2,0:T(8,128)(2,1)}), bf16[4,512,512]{1,2,0:T(8,128)(2,1)}, u32[]{:S(2)}, u32[]{:S(2)}) %all-to-all-start.3) | async-done | bytes 2097184 | tf_op jit(solution)/shard_map/all_to_all | solution.py:183
  190.1 8.3 %fusion.12 = f32[512,1408]{1,0:T(8,128)} fusion(bf16[512,2048]{0,1:T(8,128)(2,1)} %bitcast.25, bf16[2048,4224]{1,0:T(8,128)(2,1)} %all-gather.5.cloned.1.call-done), kind=kOutput, calls=%fused_computation.24 | convolution fusion | flops 2952790016 | bytes 10747904 | tf_op jit(solution)/shard_map/dot_general | solution.py:68
  198.4 25.2 %all-reduce.3.cloned.1.call-done = bf16[512,2048]{0,1:T(8,128)(2,1)} async-done(((bf16[512,2048]{0,1:T(8,128)(2,1)}), bf16[512,2048]{0,1:T(8,128)(2,1)}) %all-reduce.3.cloned.1.call-update) | async-done | bytes 2097168 | tf_op jit(solution)/shard_map/psum | solution.py:297
  223.6 2.5 multiply_reduce_fusion.5
  226.9 6.4 %fusion.8 = f32[512,1408]{1,0:T(8,128)S(1)} fusion(bf16[512,2048]{0,1:T(8,128)(2,1)S(1)} %multiply_convert_fusion.1, bf16[2048,4224]{1,0:T(8,128)(2,1)} %all-gather.5.cloned.1.call-done), kind=kOutput, calls=%fused_computation.20 | convolution fusion | flops 2952790016 | bytes 10747904 | tf_op jit(solution)/shard_map/dot_general | solution.py:68
  233.4 8.7 %multiply_convert_fusion.5 = (bf16[512,1408]{1,0:T(8,128)(2,1)S(1)}, bf16[512,1408]{1,0:T(8,128)(2,1)}, bf16[512,1408]{1,0:T(8,128)(2,1)S(1)}) fusion(f32[512,1408]{1,0:T(8,128)S(1)} %copy-done.52, f32[512,1408]{1,0:T(8,128)S(1)} %fusion.8, bf16[512,2048]{0,1:T(8,128)(2,1)S(1)} %multiply_convert_fusion.1, bf16[2048,4224]{1,0:T(8,128)(2,1)} %all-gather.5.cloned.1.call-done), kind=kOutput, calls=%fused_computation.52 | convolution fusion | flops 2964324352 | bytes 17956864 | tf_op jit(solution)/shard_map/dot_general | solution.py:68
  242.1 6.9 %fusion.23 = bf16[512,2048]{1,0:T(8,128)(2,1)S(1)} fusion(bf16[512,1408]{1,0:T(8,128)(2,1)S(1)} %get-tuple-element.46, bf16[2048,4224]{1,0:T(8,128)(2,1)} %all-gather.5.cloned.1.call-done), kind=kOutput, calls=%fused_computation.49 | convolution fusion | flops 2953838592 | bytes 9306112 | tf_op jit(solution)/shard_map/dot_general | solution.py:68
  250.5 4.4 all-to-all-start.4
  255.2 5.6 fusion.2
  260.8 7.4 %add_convert_fusion.1 = bf16[512,2048]{0,1:T(8,128)(2,1)} fusion(f32[512,2048]{0,1:T(8,128)S(1)} %fusion.2, bf16[512,1408]{1,0:T(8,128)(2,1)S(1)} %copy-done.11, bf16[2048,4224]{1,0:T(8,128)(2,1)} %all-gather.5.cloned.1.call-done), kind=kOutput, calls=%fused_computation.44 | convolution fusion | flops 2954887168 | bytes 13500416 | tf_op jit(solution)/shard_map/dot_general | solution.py:68
  268.2 13.4 %all-to-all-done.4 = bf16[4,512,512]{2,1,0:T(8,128)(2,1)} async-done(((bf16[4,512,512]{2,1,0:T(8,128)(2,1)}), bf16[4,512,512]{2,1,0:T(8,128)(2,1)}, u32[]{:S(2)}, u32[]{:S(2)}) %all-to-all-start.4) | async-done | bytes 2097184 | tf_op jit(solution)/shard_map/all_to_all | solution.py:176
  281.6 2.9 reduce_sum.108
  284.6 4.7 pad_maximum_fusion.1.left_ref
  289.3 2.1 pad_maximum_fusion.right_ref
  291.5 34.0 %shard_map.230 = bf16[2048,4224]{1,0:T(8,128)(2,1)} custom-call(s32[33]{0:T(128)} %constant.65.clone.select_ref, bf16[2,2048,512]{2,1,0:T(8,128)(2,1)} %pad_maximum_fusion.1.left_ref, bf16[512,4224]{1,0:T(8,128)(2,1)} %pad_maximum_fusion.right_ref), custom_call_target="tpu_custom_call" | custom-call | tf_op jit(solution)/shard_map/pallas_call | solution.py:216
  325.4 17.3 %all-reduce.5.cloned.1.call-done = bf16[512,2048]{0,1:T(8,128)(2,1)} async-done(((bf16[512,2048]{0,1:T(8,128)(2,1)}), bf16[512,2048]{0,1:T(8,128)(2,1)}) %all-reduce.5.cloned.1.call-update) | async-done | bytes 2097168 | tf_op jit(solution)/shard_map/psum | solution.py:318
  342.7 4.2 convert_element_type.159
  347.7 5.0 multiply_reduce_fusion.1
  353.9 4.8 convert_bitcast_fusion
  360.6 2.5 multiply_reduce_fusion
  363.2 2.6 multiply_convert_fusion
  374.2 29.6 %all_to_all.52 = bf16[4,512,512]{2,1,0:T(8,128)(2,1)} all-to-all(bf16[4,512,512]{2,1,0:T(8,128)(2,1)S(1)} %bitcast.176), channel_id=1, replica_groups=mesh['row'=32,'col'=4] {'col'}, dimensions={0} | all-to-all | bytes 4194304 | tf_op jit(solution)/shard_map/all_to_all | solution.py:176
  403.8 2.9 reduce_sum.111
  409.4 4.4 all-to-all-start.6
  416.1 3.0 concatenate.54.right_ref
  419.1 4.9 pad_maximum_fusion.2.left_ref
  424.0 11.6 %shard_map.231 = bf16[2048,1152]{1,0:T(8,128)(2,1)} custom-call(s32[9]{0:T(128)} %constant.66.clone.select_ref, bf16[2,2048,512]{2,1,0:T(8,128)(2,1)} %pad_maximum_fusion.2.left_ref, bf16[512,1152]{1,0:T(8,128)(2,1)} %concatenate.54.right_ref), custom_call_target="tpu_custom_call" | custom-call | tf_op jit(solution)/shard_map/pallas_call | solution.py:216
  435.6 3.8 all-to-all-done.6
  439.3 4.3 convert_element_type.177
  443.6 20.7 %reduce-scatter.3.cloned.1.call-done = bf16[64,4224]{1,0:T(8,128)(2,1)} async-done(((bf16[2048,4224]{1,0:T(8,128)(2,1)}), bf16[64,4224]{1,0:T(8,128)(2,1)}) %reduce-scatter.3.cloned.1.call-update) | async-done | bytes 540688 | tf_op jit(solution)/shard_map/reduce_scatter | solution.py:326
  464.4 3.8 sort.47
  468.6 5.6 multiply_reduce_fusion.2
  475.0 5.5 all-to-all-start.8
  480.6 2.9 fusion.50
  484.6 4.1 gather_fusion.3
  488.7 7.5 %all-to-all-start.7 = ((bf16[2,512,512]{2,0,1:T(2,128)(2,1)}), bf16[2,512,512]{2,0,1:T(2,128)(2,1)S(1)}, u32[]{:S(2)}, u32[]{:S(2)}) async-start(bf16[2,512,512]{2,0,1:T(2,128)(2,1)} %bitcast.53), calls=%async_computation.8 | async-start | bytes 2097152 | tf_op jit(solution)/shard_map/all_to_all | solution.py:369
  499.1 14.4 %all-to-all-done.7 = bf16[2,512,512]{2,0,1:T(2,128)(2,1)S(1)} async-done(((bf16[2,512,512]{2,0,1:T(2,128)(2,1)}), bf16[2,512,512]{2,0,1:T(2,128)(2,1)S(1)}, u32[]{:S(2)}, u32[]{:S(2)}) %all-to-all-start.7) | async-done | bytes 1048608 | tf_op jit(solution)/shard_map/all_to_all | solution.py:369
  515.3 2.6 gather_fusion.5
  517.9 2.6 gather_fusion.4
  520.5 30.5 %reduce-scatter.5.cloned.1.call-done = bf16[64,1152]{1,0:T(8,128)(2,1)} async-done(((bf16[2048,1152]{1,0:T(8,128)(2,1)}), bf16[64,1152]{1,0:T(8,128)(2,1)}) %reduce-scatter.5.cloned.1.call-update) | async-done | bytes 147472 | tf_op jit(solution)/shard_map/reduce_scatter | solution.py:358
  (214 shorter events, 51.9 us)
Async XLA Ops:
  7.2 21.6 %copy-start.27 = (bf16[512,512]{1,0:T(8,128)(2,1)S(1)}, bf16[512,512]{1,0:T(8,128)(2,1)}, u32[]{:S(2)}) copy-start(bf16[512,512]{1,0:T(8,128)(2,1)} %param.15) | copy-start | bytes 1572868
  7.2 22.5 %copy-start.28 = (bf16[512,512]{1,0:T(8,128)(2,1)S(1)}, bf16[512,512]{1,0:T(8,128)(2,1)}, u32[]{:S(2)}) copy-start(bf16[512,512]{1,0:T(8,128)(2,1)} %param.16) | copy-start | bytes 1572868
  7.2 104.1 %all-gather.3.cloned.1.call-start = ((), (), s32[]{:S(2)}) async-start(), calls=%async_computation.11 | async-start | bytes 4866048 | tf_op jit(solution)/shard_map/all_gather | solution.py:192
  9.0 136.1 %all-gather.5.cloned.1.call-start = ((), (), s32[]{:S(2)}) async-start(), calls=%async_computation.12 | async-start | bytes 17842176 | tf_op jit(solution)/shard_map/all_gather | solution.py:192
  20.4 16.7 %all-to-all-start.1 = ((s32[32,16,1]{1,2,0:T(1,128)}), s32[32,16,1]{1,2,0:T(1,128)S(1)}, u32[]{:S(2)}, u32[]{:S(2)}) async-start(s32[32,16,1]{1,2,0:T(1,128)} %bitcast.3), calls=%async_computation.1 | async-start | bytes 32768 | tf_op jit(solution)/shard_map/all_to_all | solution.py:252
  37.0 35.6 %copy-start.30 = (s32[32,16,1]{1,2,0:T(1,128)}, s32[32,16,1]{1,2,0:T(1,128)S(1)}, u32[]{:S(2)}) copy-start(s32[32,16,1]{1,2,0:T(1,128)S(1)} %all-to-all-done.1) | copy-start | bytes 6148
  37.0 32.0 %all-to-all-start = ((bf16[2,512,512]{2,0,1:T(2,128)(2,1)}), bf16[2,512,512]{2,0,1:T(2,128)(2,1)S(1)}, u32[]{:S(2)}, u32[]{:S(2)}) async-start(bf16[2,512,512]{2,0,1:T(2,128)(2,1)} %bitcast.2), calls=%async_computation | async-start | bytes 2097152 | tf_op jit(solution)/shard_map/all_to_all | solution.py:249
  74.2 7.3 %copy-start.46 = (s32[512]{0:T(512)S(1)}, s32[512]{0:T(512)}, u32[]{:S(2)}) copy-start(s32[512]{0:T(512)} %param.18) | copy-start | bytes 6148
  74.2 7.9 %copy-start.32 = (f32[2048]{0:T(1024)S(1)}, f32[2048]{0:T(1024)}, u32[]{:S(2)}) copy-start(f32[2048]{0:T(1024)} %param.19) | copy-start | bytes 24580
  77.0 29.3 %all-to-all-start.2 = ((bf16[4,512,512]{1,2,0:T(8,128)(2,1)}), bf16[4,512,512]{1,2,0:T(8,128)(2,1)S(1)}, u32[]{:S(2)}, u32[]{:S(2)}) async-start(bf16[4,512,512]{1,2,0:T(8,128)(2,1)} %broadcast_in_dim.27), calls=%async_computation.2 | async-start | bytes 4194304 | tf_op jit(solution)/shard_map/all_to_all | solution.py:183
  83.2 38.1 %copy-start.42 = (f32[512]{0:T(512)}, f32[512]{0:T(512)S(1)}, u32[]{:S(2)}) copy-start(f32[512]{0:T(512)S(1)} %fusion.76) | copy-start | bytes 6148
  83.5 43.0 %copy-start.23 = (f32[512,32]{0,1:T(8,128)}, f32[512,32]{0,1:T(8,128)S(1)}, u32[]{:S(2)}) copy-start(f32[512,32]{0,1:T(8,128)S(1)} %get-tuple-element.68) | copy-start | bytes 196612
  83.6 43.0 %copy-start.25 = (f32[512,32]{0,1:T(8,128)}, f32[512,32]{0,1:T(8,128)S(1)}, u32[]{:S(2)}) copy-start(f32[512,32]{0,1:T(8,128)S(1)} %get-tuple-element.69) | copy-start | bytes 196612
  106.8 2.6 copy-start.40
  114.6 6.8 %copy-start.50 = (f32[32]{0:T(128)S(1)}, f32[32]{0:T(128)}, u32[]{:S(2)}) copy-start(f32[32]{0:T(128)} %copy-done.49) | copy-start | bytes 388
  118.8 6.5 %copy-start.8 = (bf16[512,2048]{1,0:T(8,128)(2,1)S(1)}, bf16[512,2048]{1,0:T(8,128)(2,1)}, u32[]{:S(2)}) copy-start(bf16[512,2048]{1,0:T(8,128)(2,1)} %copy.119) | copy-start | bytes 6291460
  118.8 6.5 %copy-start.9 = (bf16[4,512,512]{1,2,0:T(8,128)(2,1)S(1)}, bf16[4,512,512]{1,2,0:T(8,128)(2,1)}, u32[]{:S(2)}) copy-start(bf16[4,512,512]{1,2,0:T(8,128)(2,1)} %fusion.18) | copy-start | bytes 6291460
  122.6 4.2 copy-start.15
  122.6 4.2 copy-start.17
  125.3 4.2 copy-start.36
  126.8 1.5 copy-start.19
  126.8 1.5 copy-start.21
  128.3 3.3 copy-start
  131.6 1.6 copy-start.38
  134.0 11.1 %copy-start.7 = (bf16[1,512,512]{2,1,0:T(8,128)(2,1)S(1)}, bf16[1,512,512]{2,1,0:T(8,128)(2,1)}, u32[]{:S(2)}) copy-start(bf16[1,512,512]{2,1,0:T(8,128)(2,1)} %copy.176) | copy-start | bytes 1572868
  146.8 43.3 %all-to-all-start.3 = ((bf16[4,512,512]{1,2,0:T(8,128)(2,1)}), bf16[4,512,512]{1,2,0:T(8,128)(2,1)}, u32[]{:S(2)}, u32[]{:S(2)}) async-start(bf16[4,512,512]{1,2,0:T(8,128)(2,1)} %broadcast_in_dim.30), calls=%async_computation.3 | async-start | bytes 4194304 | tf_op jit(solution)/shard_map/all_to_all | solution.py:183
  151.3 72.3 %all-reduce.3.cloned.1.call-start = ((), (), s32[]{:S(2)}) async-start(), calls=%async_computation.13 | async-start | bytes 4194304 | tf_op jit(solution)/shard_map/psum | solution.py:297
  198.4 27.7 %copy-start.34 = (f32[2048]{0:T(1024)S(1)}, f32[2048]{0:T(1024)}, u32[]{:S(2)}) copy-start(f32[2048]{0:T(1024)} %param.24) | copy-start | bytes 24580
  223.6 2.5 copy-start.2
  226.9 6.4 %copy-start.4 = (bf16[512,2048]{0,1:T(8,128)(2,1)}, bf16[512,2048]{0,1:T(8,128)(2,1)S(1)}, u32[]{:S(2)}) copy-start(bf16[512,2048]{0,1:T(8,128)(2,1)S(1)} %multiply_convert_fusion.1) | copy-start | bytes 6291460
  226.9 6.4 %copy-start.52 = (f32[512,1408]{1,0:T(8,128)S(1)}, f32[512,1408]{1,0:T(8,128)}, u32[]{:S(2)}) copy-start(f32[512,1408]{1,0:T(8,128)} %fusion.12) | copy-start | bytes 8650756
  242.1 6.9 %copy-start.13 = (bf16[512,1408]{1,0:T(8,128)(2,1)}, bf16[512,1408]{1,0:T(8,128)(2,1)S(1)}, u32[]{:S(2)}) copy-start(bf16[512,1408]{1,0:T(8,128)(2,1)S(1)} %get-tuple-element.46) | copy-start | bytes 4325380
  250.5 31.1 %all-to-all-start.4 = ((bf16[4,512,512]{2,1,0:T(8,128)(2,1)}), bf16[4,512,512]{2,1,0:T(8,128)(2,1)}, u32[]{:S(2)}, u32[]{:S(2)}) async-start(bf16[4,512,512]{2,1,0:T(8,128)(2,1)} %bitcast.175), calls=%async_computation.4 | async-start | bytes 4194304 | tf_op jit(solution)/shard_map/all_to_all | solution.py:176
  255.0 87.8 %all-reduce.5.cloned.1.call-start = ((), (), s32[]{:S(2)}) async-start(), calls=%async_computation.14 | async-start | bytes 4194304 | tf_op jit(solution)/shard_map/psum | solution.py:318
  255.2 5.6 %copy-start.11 = (bf16[512,1408]{1,0:T(8,128)(2,1)S(1)}, bf16[512,1408]{1,0:T(8,128)(2,1)}, u32[]{:S(2)}) copy-start(bf16[512,1408]{1,0:T(8,128)(2,1)} %get-tuple-element.45) | copy-start | bytes 4325380
  284.5 179.9 %reduce-scatter.3.cloned.1.call-start = ((), (), s32[]{:S(2)}) async-start(), calls=%async_computation.15 | async-start | bytes 17842176 | tf_op jit(solution)/shard_map/reduce_scatter | solution.py:326
  284.6 4.8 copy-start.12
  284.6 4.8 copy-start.14
  347.7 5.0 copy-start.1
  347.7 6.2 %copy-start.3 = (bf16[512,2048]{0,1:T(8,128)(2,1)S(1)}, bf16[512,2048]{0,1:T(8,128)(2,1)}, u32[]{:S(2)}) copy-start(bf16[512,2048]{0,1:T(8,128)(2,1)} %all-reduce.3.cloned.1.call-done) | copy-start | bytes 6291460
  347.7 11.1 %slice-start.2 = ((s8[4718592]{0:T(1024)(128)(4,1)}), s8[4194304]{0:T(1024)(128)(4,1)S(1)}, s32[]{:S(2)}) async-start(s8[4718592]{0:T(1024)(128)(4,1)} %bitcast.181), calls=%async_computation.19 | async-start | bytes 8388608
  352.7 7.4 %slice-start = ((s8[8388608]{0:T(1024)(128)(4,1)}), s8[4194304]{0:T(1024)(128)(4,1)S(1)}, s32[]{:S(2)}) async-start(s8[8388608]{0:T(1024)(128)(4,1)} %bitcast.168), calls=%async_computation.17 | async-start | bytes 8388608
  353.9 4.9 slice-start.3
  353.9 6.7 %slice-start.1 = ((s8[8388608]{0:T(1024)(128)(4,1)}), s8[4194304]{0:T(1024)(128)(4,1)S(1)}, s32[]{:S(2)}) async-start(s8[8388608]{0:T(1024)(128)(4,1)} %bitcast.168), calls=%async_computation.18 | async-start | bytes 8388608
  358.8 4.4 copy-start.5
  358.8 1.9 copy-start.37
  363.2 2.6 copy-start.20
  363.2 2.6 copy-start.22
  365.8 1.3 copy-start.43
  365.8 1.3 copy-start.51
  365.8 2.9 copy-start.16
  365.8 2.9 copy-start.18
  367.1 2.6 copy-start.24
  367.1 2.6 copy-start.26
  409.4 30.0 %all-to-all-start.6 = ((bf16[4,512,512]{1,2,0:T(8,128)(2,1)}), bf16[4,512,512]{1,2,0:T(8,128)(2,1)}, u32[]{:S(2)}, u32[]{:S(2)}) async-start(bf16[4,512,512]{1,2,0:T(8,128)(2,1)} %broadcast_in_dim.31), calls=%async_computation.7 | async-start | bytes 4194304 | tf_op jit(solution)/shard_map/all_to_all | solution.py:183
  413.8 137.2 %reduce-scatter.5.cloned.1.call-start = ((), (), s32[]{:S(2)}) async-start(), calls=%async_computation.16 | async-start | bytes 4866048 | tf_op jit(solution)/shard_map/reduce_scatter | solution.py:358
  435.5 28.9 %copy-start.48 = (s32[512]{0:T(512)S(1)}, s32[512]{0:T(512)}, u32[]{:S(2)}) copy-start(s32[512]{0:T(512)} %copy-done.47) | copy-start | bytes 6148
  435.5 32.7 %copy-start.31 = (s32[32,16,1]{1,2,0:T(1,128)S(1)}, s32[32,16,1]{1,2,0:T(1,128)}, u32[]{:S(2)}) copy-start(s32[32,16,1]{1,2,0:T(1,128)} %copy-done.30) | copy-start | bytes 6148
  435.5 32.7 %copy-start.10 = (bf16[512,512]{1,0:T(8,128)(2,1)S(1)}, bf16[512,512]{1,0:T(8,128)(2,1)}, u32[]{:S(2)}) copy-start(bf16[512,512]{1,0:T(8,128)(2,1)} %reduce_sum.108) | copy-start | bytes 1572868
  443.6 25.0 %copy-start.33 = (f32[2048]{0:T(1024)S(1)}, f32[2048]{0:T(1024)}, u32[]{:S(2)}) copy-start(f32[2048]{0:T(1024)} %param.19) | copy-start | bytes 24580
  443.6 25.0 %copy-start.41 = (f32[512]{0:T(512)S(1)}, f32[512]{0:T(512)}, u32[]{:S(2)}) copy-start(f32[512]{0:T(512)} %copy-done.40) | copy-start | bytes 6148
  475.0 13.7 %all-to-all-start.8 = ((f32[32,1,128]{2,1,0:T(1,128)}), f32[32,1,128]{2,1,0:T(1,128)S(1)}, u32[]{:S(2)}, u32[]{:S(2)}) async-start(f32[32,1,128]{2,1,0:T(1,128)} %reshape.489), calls=%async_computation.9 | async-start | bytes 32768 | tf_op jit(solution)/shard_map/all_to_all | solution.py:157
  483.5 12.8 %copy-start.6 = (bf16[64,4224]{1,0:T(8,128)(2,1)S(1)}, bf16[64,4224]{1,0:T(8,128)(2,1)}, u32[]{:S(2)}) copy-start(bf16[64,4224]{1,0:T(8,128)(2,1)} %reduce-scatter.3.cloned.1.call-done) | copy-start | bytes 1622020
  488.7 24.8 %all-to-all-start.7 = ((bf16[2,512,512]{2,0,1:T(2,128)(2,1)}), bf16[2,512,512]{2,0,1:T(2,128)(2,1)S(1)}, u32[]{:S(2)}, u32[]{:S(2)}) async-start(bf16[2,512,512]{2,0,1:T(2,128)(2,1)} %bitcast.53), calls=%async_computation.8 | async-start | bytes 2097152 | tf_op jit(solution)/shard_map/all_to_all | solution.py:369
  (7 other events, 4.8 us)
Sparse Core Ops, SparseCore 0:
  10.9 59.4 all-gather.2
  72.6 72.4 all-gather.4
  155.8 67.7 all-reduce.2
  284.6 58.0 all-reduce.4
  347.1 117.2 reduce-scatter.2
  468.0 82.9 reduce-scatter.4
